TPU v7x, 256 devices: a whole 4x4x8 slice. The times are simulated.
256 devices in a mesh: dom: 64 (over z, x, core), grp: 4 (over y).
Axes of the slice: x: 4, y: 4, z: 8, core: 2. Of those that a mesh axis runs over, the one named last changes fastest.
Arguments:
- features: bfloat16 [131072, 128], P('dom'), may hold values from -6 to 6
- weight_self: bfloat16 [128, 1024], P(None, 'grp'), may hold values from -0.5 to 0.5
- weight_neigh: bfloat16 [128, 1024], P(None, 'grp'), may hold values from -3 to 3
- cotangent: bfloat16 [131072, 1024], P('dom', 'grp'), may hold values from -6 to 6
- inner_rows: int32 [64, 64], P('dom'), may hold values from 0 to 15
- inner_cols: int32 [64, 64], P('dom'), may hold values from 0 to 15
- inner_values: bfloat16 [64, 64, 128, 128], P('dom'), may hold values from 0 to 1, as said below
- send_blocks: int32 [64, 64, 3], P('dom'), may hold values from 0 to 15
- outer_rows: int32 [64, 192], P('dom'), may hold values from 0 to 15
- outer_values: bfloat16 [64, 192, 128, 128], P('dom'), may hold values from 0 to 1, as said below
- live_count: int32 [64, 64], P('dom'), may hold values from 0 to 3
Outputs:
- layer_out: bfloat16 [131072, 1024], P('dom', 'grp')
- feature_grad: float32 [131072, 128], P('dom')
- self_grad: float32 [128, 1024], P(None, 'grp')
- neigh_grad: float32 [128, 1024], P(None, 'grp')
Inputs may be any that keep to these rules, and one draw needn't show every extreme that they name: `inner_values`: edge weights are zero or positive; most are zero. `outer_values`: edge weights are zero or positive; most are zero.
All inputs are finite; a program needn't handle non-finite values.
Results may differ from a plain program's by a relative error of at most 0.0055.
Values may be sent and summed in bfloat16 or wider, within the bound.
A program may use at most 128 MiB of HBM per device.

v0:
```python
import jax
import jax.numpy as jnp
from jax import lax
from jax.sharding import PartitionSpec as P


def block_segment(one_hot, products, block_size):
    count = products.shape[0]
    summed = jnp.dot(one_hot, products.reshape(count, -1), precision=lax.Precision.HIGHEST)
    return summed.reshape(one_hot.shape[0], block_size, -1)


def shards(
    features,
    weight_self,
    weight_neigh,
    cotangent,
    inner_rows,
    inner_cols,
    inner_values,
    send_blocks,
    outer_rows,
    outer_values,
    live_count,
):
    block_size = inner_values.shape[-1]
    node_rows, feat_width = features.shape
    loc_blocks = node_rows // block_size
    peer_count = lax.axis_size("dom")
    slot_depth = send_blocks.shape[-1]
    inner_a = inner_values[0]
    outer_a = outer_values[0]
    row_inner = inner_rows[0]
    col_inner = inner_cols[0]
    row_outer = outer_rows[0]
    targets = send_blocks[0]
    slot_limit = jnp.repeat(live_count[0], slot_depth)
    slot_index = jnp.tile(jnp.arange(slot_depth, dtype=jnp.int32), peer_count)
    live_mask = (slot_index < slot_limit).astype(jnp.float32)
    block_ids = jnp.arange(loc_blocks, dtype=jnp.int32)[:, None]
    inner_onehot = (row_inner[None, :] == block_ids).astype(jnp.float32)
    outer_onehot = (row_outer[None, :] == block_ids).astype(jnp.float32) * live_mask[None, :]
    degree = 1.0 + jnp.dot(
        inner_onehot, jnp.sum(inner_a, axis=-1, dtype=jnp.float32), precision=lax.Precision.HIGHEST
    )
    degree = degree + jnp.dot(
        outer_onehot, jnp.sum(outer_a, axis=-1, dtype=jnp.float32), precision=lax.Precision.HIGHEST
    )
    feat_blocks = features.reshape(loc_blocks, block_size, feat_width)
    outgoing = feat_blocks[targets]
    incoming = lax.all_to_all(outgoing, "dom", split_axis=0, concat_axis=0, tiled=True)
    incoming = incoming.reshape(peer_count * slot_depth, block_size, feat_width)
    inner_prod = jnp.einsum(
        "nij,njf->nif", inner_a, feat_blocks[col_inner], preferred_element_type=jnp.float32
    )
    outer_prod = jnp.einsum("nij,njf->nif", outer_a, incoming, preferred_element_type=jnp.float32)
    neighbour = block_segment(inner_onehot, inner_prod, block_size) + block_segment(
        outer_onehot, outer_prod, block_size
    )
    agg_part = ((feat_blocks.astype(jnp.float32) + neighbour) / degree[..., None]).astype(
        jnp.bfloat16
    )
    agg_part = agg_part.reshape(node_rows, feat_width)
    preact = jnp.dot(features, weight_self, preferred_element_type=jnp.float32) + jnp.dot(
        agg_part, weight_neigh, preferred_element_type=jnp.float32
    )
    layer_out = jax.nn.silu(preact).astype(jnp.bfloat16)
    sigmoid_v = jax.nn.sigmoid(preact)
    grad_pre = (
        cotangent.astype(jnp.float32) * sigmoid_v * (1.0 + preact * (1.0 - sigmoid_v))
    ).astype(jnp.bfloat16)
    first_dims = (((0,), (0,)), ((), ()))
    grad_self = lax.dot_general(features, grad_pre, first_dims, preferred_element_type=jnp.float32)
    grad_neigh = lax.dot_general(agg_part, grad_pre, first_dims, preferred_element_type=jnp.float32)
    grad_self, grad_neigh = lax.psum((grad_self, grad_neigh), "dom")
    second_dims = (((1,), (1,)), ((), ()))
    self_part = lax.dot_general(
        grad_pre, weight_self, second_dims, preferred_element_type=jnp.float32
    )
    neigh_part = lax.dot_general(
        grad_pre, weight_neigh, second_dims, preferred_element_type=jnp.float32
    )
    self_back, neigh_back = lax.psum((self_part, neigh_part), "grp")
    scaled = (neigh_back.reshape(loc_blocks, block_size, feat_width) / degree[..., None]).astype(
        jnp.bfloat16
    )
    inner_back = jnp.einsum(
        "nij,nif->njf", inner_a, scaled[row_inner], preferred_element_type=jnp.float32
    )
    outer_back = (
        jnp.einsum("nij,nif->njf", outer_a, scaled[row_outer], preferred_element_type=jnp.float32)
        * live_mask[:, None, None]
    )
    returned = lax.all_to_all(
        outer_back.reshape(peer_count, slot_depth, block_size, feat_width).astype(jnp.bfloat16),
        "dom",
        split_axis=0,
        concat_axis=0,
        tiled=True,
    ).astype(jnp.float32)
    col_onehot = (col_inner[None, :] == block_ids).astype(jnp.float32)
    target_onehot = (targets.reshape(-1)[None, :] == block_ids).astype(jnp.float32)
    pulled_back = block_segment(col_onehot, inner_back, block_size)
    pulled_back = pulled_back + block_segment(
        target_onehot, returned.reshape(peer_count * slot_depth, block_size, feat_width), block_size
    )
    grad_part = self_back + (scaled.astype(jnp.float32) + pulled_back).reshape(
        node_rows, feat_width
    )
    return (layer_out, grad_part, grad_self, grad_neigh)


def solution(mesh):
    placed = (
        P("dom", None),
        P(None, "grp"),
        P(None, "grp"),
        P("dom", "grp"),
        P("dom", None),
        P("dom", None),
        P("dom", None, None, None),
        P("dom", None, None),
        P("dom", None),
        P("dom", None, None, None),
        P("dom", None),
    )
    return jax.shard_map(
        shards,
        mesh=mesh,
        in_specs=placed,
        out_specs=(P("dom", "grp"), P("dom", None), P(None, "grp"), P(None, "grp")),
        check_vma=False,
    )
```

profile of v0, /device:TPU:1, one launch (start us, length us, event | category | flops | bytes accessed | tf_op | source)
XLA Modules:
  0.0 577.5 jit_solution(11746302763327650803)
XLA Ops:
  9.0 9.1 %gather_fusion.1 = bf16[192,128,128]{2,1,0:T(8,128)(2,1)} fusion(bf16[16,128,128]{2,1,0:T(8,128)(2,1)} %bitcast.149, s32[1024]{0:T(1024)S(1)} %pad_clamp_fusion.2), kind=kCustom, calls=%fused_computation.1 | custom fusion | bytes 12583680 | tf_op jit(solution)/shard_map/gather | solution.py:50
  18.1 13.3 %all-to-all-start = ((bf16[64,3,128,128]{3,2,1,0:T(8,128)(2,1)}), bf16[64,3,128,128]{3,2,1,0:T(8,128)(2,1)}, u32[]{:S(2)}, u32[]{:S(2)}) async-start(bf16[64,3,128,128]{3,2,1,0:T(8,128)(2,1)} %bitcast.153), calls=%async_computation | async-start | bytes 12582912 | tf_op jit(solution)/shard_map/all_to_all | solution.py:51
  32.6 4.5 convert_reduce_fusion
  37.5 2.2 gather_fusion
  39.6 5.3 convolution_bitcast_fusion.1
  44.9 5.7 copy.23
  52.3 117.6 %all-to-all-done = bf16[64,3,128,128]{3,2,1,0:T(8,128)(2,1)} async-done(((bf16[64,3,128,128]{3,2,1,0:T(8,128)(2,1)}), bf16[64,3,128,128]{3,2,1,0:T(8,128)(2,1)}, u32[]{:S(2)}, u32[]{:S(2)}) %all-to-all-start) | async-done | bytes 6291488 | tf_op jit(solution)/shard_map/all_to_all | solution.py:51
  169.9 13.7 %fusion.10 = f32[192,128,128]{1,2,0:T(8,128)} fusion(bf16[192,128,128]{2,1,0:T(8,128)(2,1)} %bitcast.34, bf16[1,192,128,128]{3,2,1,0:T(8,128)(2,1)} %param.20), kind=kOutput, calls=%fused_computation.18 | convolution fusion | flops 805306368 | bytes 25165824 | tf_op jit(solution)/shard_map/nij,njf->nif/dot_general | solution.py:56
  183.5 12.6 %copy.27 = f32[192,128,128]{2,1,0:T(8,128)} copy(f32[192,128,128]{1,2,0:T(8,128)} %fusion.10) | data formatting | bytes 25165824 | tf_op jit(solution)/shard_map/nij,njf->nif/dot_general | solution.py:56
  196.2 18.4 %fusion = f32[16,128,128]{2,0,1:T(8,128)S(1)} fusion(f32[192]{0:T(256)S(1)} %reshape.188, s32[192]{0:T(256)S(1)} %bitcast.161, f32[24,8,128,128]{3,2,1,0:T(8,128)} %bitcast.152), kind=kOutput, calls=%fused_computation.5 | convolution fusion | flops 603985920 | bytes 13633024 | tf_op jit(solution)/shard_map/dot_general | solution.py:9
  214.7 4.3 fusion.38
  219.1 2.2 multiply_convert_fusion.1
  225.4 63.3 %all-reduce.7.cloned.1.call-done = (f32[2048,128]{1,0:T(8,128)}, f32[16,128,128]{2,0,1:T(8,128)}) async-done(((f32[2048,128]{1,0:T(8,128)}, f32[16,128,128]{2,0,1:T(8,128)}), (f32[2048,128]{1,0:T(8,128)}, f32[16,128,128]{2,0,1:T(8,128)})) %all-reduce.7.cloned.1.call-update) | async-done | bytes 2097168 | tf_op jit(solution)/shard_map/psum | solution.py:83
  291.2 8.5 %gather_fusion.3 = bf16[192,128,128]{2,1,0:T(8,128)(2,1)} fusion(bf16[16,128,128]{2,1,0:T(8,128)(2,1)S(1)} %copy.32, s32[1024]{0:T(1024)S(1)} %pad_clamp_fusion), kind=kCustom, calls=%fused_computation.3 | custom fusion | bytes 12583680 | tf_op jit(solution)/shard_map/gather | solution.py:91
  299.7 10.3 %multiply_convert_fusion = bf16[192,128,128]{2,1,0:T(8,128)(2,1)} fusion(f32[192]{0:T(256)S(1)} %reshape.188, bf16[192,128,128]{2,1,0:T(8,128)(2,1)} %gather_fusion.3, bf16[1,192,128,128]{3,2,1,0:T(8,128)(2,1)} %param.20), kind=kOutput, calls=%fused_computation.8 | convolution fusion | flops 811597824 | bytes 18875136 | tf_op jit(solution)/shard_map/nij,nif->njf/dot_general | solution.py:91
  310.0 8.6 %copy.39 = bf16[64,3,128,128]{3,2,1,0:T(8,128)(2,1)} copy(bf16[64,3,128,128]{2,3,1,0:T(8,128)(2,1)} %bitcast.154) | data formatting | bytes 12582912 | tf_op jit(solution)/shard_map/convert_element_type | solution.py:95
  318.6 10.9 %all-to-all-start.1 = ((bf16[64,3,128,128]{3,2,1,0:T(8,128)(2,1)}), bf16[64,3,128,128]{3,2,1,0:T(8,128)(2,1)}, u32[]{:S(2)}, u32[]{:S(2)}) async-start(bf16[64,3,128,128]{3,2,1,0:T(8,128)(2,1)} %copy.39), calls=%async_computation.1 | async-start | bytes 12582912 | tf_op jit(solution)/shard_map/all_to_all | solution.py:94
  329.6 2.4 fusion.66
  332.0 2.4 convolution_bitcast_fusion.2
  334.7 208.8 %all-reduce.5.cloned.1.call-done = (f32[128,256]{0,1:T(8,128)}, f32[128,256]{1,0:T(8,128)}) async-done(((f32[128,256]{0,1:T(8,128)}, f32[128,256]{1,0:T(8,128)}), (f32[128,256]{0,1:T(8,128)}, f32[128,256]{1,0:T(8,128)})) %all-reduce.5.cloned.1.call-update) | async-done | bytes 262160 | tf_op jit(solution)/shard_map/psum | solution.py:75
  547.2 4.4 convolution_bitcast_fusion
  551.6 5.8 copy.34
  557.4 6.4 %fusion.3 = f32[16,128,128]{2,0,1:T(8,128)S(1)} fusion(s32[192]{0:T(256)S(1)} %eq.72, bf16[24,8,128,128]{3,2,1,0:T(8,128)(2,1)} %bitcast.51), kind=kOutput, calls=%fused_computation.11 | convolution fusion | flops 100666368 | bytes 7340800 | tf_op jit(solution)/shard_map/dot_general | solution.py:9
  563.8 3.9 fusion.32
  (75 shorter events, 17.1 us)
Async XLA Ops:
  8.0 211.1 %copy-start = (bf16[128,256]{1,0:T(8,128)(2,1)S(1)}, bf16[128,256]{1,0:T(8,128)(2,1)}, u32[]{:S(2)}) copy-start(bf16[128,256]{1,0:T(8,128)(2,1)} %param.13) | copy-start | bytes 196612
  18.1 13.5 %copy-start.16 = (s32[1,64]{1,0:T(1,128)S(1)}, s32[1,64]{1,0:T(1,128)}, u32[]{:S(2)}) copy-start(s32[1,64]{1,0:T(1,128)} %param.21) | copy-start | bytes 772
  18.1 13.7 %copy-start.3 = (bf16[1,64,128,128]{3,2,1,0:T(8,128)(2,1)S(1)}, bf16[1,64,128,128]{3,2,1,0:T(8,128)(2,1)}, u32[]{:S(2)}) copy-start(bf16[1,64,128,128]{3,2,1,0:T(8,128)(2,1)} %param.17) | copy-start | bytes 6291460
  18.1 14.4 %copy-start.18 = (s32[1,64]{1,0:T(1,128)S(1)}, s32[1,64]{1,0:T(1,128)}, u32[]{:S(2)}) copy-start(s32[1,64]{1,0:T(1,128)} %param.15) | copy-start | bytes 772
  18.1 151.8 %all-to-all-start = ((bf16[64,3,128,128]{3,2,1,0:T(8,128)(2,1)}), bf16[64,3,128,128]{3,2,1,0:T(8,128)(2,1)}, u32[]{:S(2)}, u32[]{:S(2)}) async-start(bf16[64,3,128,128]{3,2,1,0:T(8,128)(2,1)} %bitcast.153), calls=%async_computation | async-start | bytes 12582912 | tf_op jit(solution)/shard_map/all_to_all | solution.py:51
  31.3 257.3 %all-reduce.7.cloned.1.call-start = ((), (), s32[]{:S(2)}) async-start(), calls=%async_computation.3 | async-start | bytes 4194304 | tf_op jit(solution)/shard_map/psum | solution.py:83
  31.8 5.3 copy-start.14
  31.8 5.6 copy-start.17
  31.8 5.6 copy-start.2
  44.9 5.7 copy-start.12
  196.2 18.5 %copy-start.8 = (f32[64,128,128]{2,1,0:T(8,128)S(1)}, f32[64,128,128]{2,1,0:T(8,128)}, u32[]{:S(2)}) copy-start(f32[64,128,128]{2,1,0:T(8,128)} %copy.23) | copy-start | bytes 12582916
  214.6 4.5 copy-start.9
  214.6 4.5 copy-start.19
  219.1 2.2 copy-start.10
  221.3 1.0 copy-start.5
  290.3 0.8 copy-start.6
  318.6 15.8 %copy-start.15 = (s32[1,64,3]{1,0,2:T(1,128)S(1)}, s32[1,64,3]{1,0,2:T(1,128)}, u32[]{:S(2)}) copy-start(s32[1,64,3]{1,0,2:T(1,128)} %param.18) | copy-start | bytes 2308
  318.6 238.8 %all-to-all-start.1 = ((bf16[64,3,128,128]{3,2,1,0:T(8,128)(2,1)}), bf16[64,3,128,128]{3,2,1,0:T(8,128)(2,1)}, u32[]{:S(2)}, u32[]{:S(2)}) async-start(bf16[64,3,128,128]{3,2,1,0:T(8,128)(2,1)} %copy.39), calls=%async_computation.1 | async-start | bytes 12582912 | tf_op jit(solution)/shard_map/all_to_all | solution.py:94
  329.6 213.9 %all-reduce.5.cloned.1.call-start = ((), (), s32[]{:S(2)}) async-start(), calls=%async_computation.2 | async-start | bytes 524288 | tf_op jit(solution)/shard_map/psum | solution.py:75
  557.4 6.4 %copy-start.4 = (f32[64,128,128]{2,1,0:T(8,128)S(1)}, f32[64,128,128]{2,1,0:T(8,128)}, u32[]{:S(2)}) copy-start(f32[64,128,128]{2,1,0:T(8,128)} %copy.34) | copy-start | bytes 12582916
  557.4 6.4 %copy-start.7 = (bf16[16,128,128]{2,0,1:T(8,128)(2,1)S(1)}, bf16[16,128,128]{2,0,1:T(8,128)(2,1)}, u32[]{:S(2)}) copy-start(bf16[16,128,128]{2,0,1:T(8,128)(2,1)} %copy-done.6) | copy-start | bytes 1572868
  563.7 4.3 copy-start.11
  563.8 6.1 %copy-start.1 = (bf16[128,256]{1,0:T(8,128)(2,1)S(1)}, bf16[128,256]{1,0:T(8,128)(2,1)}, u32[]{:S(2)}) copy-start(bf16[128,256]{1,0:T(8,128)(2,1)} %param.13) | copy-start | bytes 196612
  567.7 1.5 copy-start.13
Sparse Core Ops, SparseCore 0:
  225.5 63.1 all-reduce.6
Sparse Core Ops, SparseCore 1:
  334.6 208.8 all-reduce.4
where the time goes:
time: 582 us; the launch traced here: 577 us
  waiting for transfers between devices  390 us (67%)
  matrix products  77.4 us (13%)
  local copies, waits for them, and re-layouts  61.3 us (11%)
  starting transfers between devices  24.5 us (4%)
  between operations  16 us (3%)
  other arithmetic  8.63 us (1%)
    psum x1, waiting for transfers between devices, shards(): grad_self, grad_neigh = lax.psum((grad_self, grad_neigh), 'dom')  209 us
    all_to_all x1, waiting for transfers between devices, shards(): lax.all_to_all(outgoing, 'dom', split_axis=0, concat_axis=0, tiled=True)  118 us
    psum x1, waiting for transfers between devices, shards(): self_back, neigh_back = lax.psum((self_part, neigh_part), 'grp')  63.3 us
    dot_general x4, matrix products, block_segment(): jnp.dot(one_hot, products.reshape(count, -1), precision=lax.Precision.HIG...  33 us
    dot_general x1, matrix products, shards(): jnp.einsum('nij,njf->nif', outer_a, incoming, preferred_element_type=jnp....  13.7 us
    all_to_all x1, starting transfers between devices, shards(): lax.all_to_all(outgoing, 'dom', split_axis=0, concat_axis=0, tiled=True)  13.3 us
    dot_general x1, local copies, waits for them, and re-layouts, shards(): jnp.einsum('nij,njf->nif', outer_a, incoming, preferred_element_type=jnp....  12.6 us
  transfers between devices with their start and end apart: 4, of which 3 were waited for; matrix products, arithmetic and copies ran while one was open for 7% of the time, Pallas kernels for 0%

commit v1 on v0

v1 whole, which is shorter than its diff:
```python
import functools

import jax
import jax.numpy as jnp
from jax import lax
from jax.experimental import pallas as pl
from jax.experimental.pallas import tpu as pltpu
from jax.sharding import PartitionSpec as P

MESH = pl.DeviceIdType.MESH
ANY = pl.BlockSpec(memory_space=pl.ANY)
VM = pl.BlockSpec(memory_space=pltpu.VMEM)
SM = pl.BlockSpec(memory_space=pltpu.SMEM)
F32 = jnp.float32
BF16 = jnp.bfloat16
TRANS_A = (((0,), (0,)), ((), ()))
TRANS_B = (((1,), (1,)), ((), ()))


def x_extent(parts):
    return 4 if parts == 64 else 1


def plane_peer(i, q, g, x):
    z = q // (2 * x)
    return (((i // x) * 2 + (z + g // 2) % 2) * x + i % x) * 2 + (q + g) % 2


def plane_slot(q, x):
    return (q // (4 * x)) * x + (q // 2) % x


def enter(peers, count):
    barrier = pltpu.get_barrier_semaphore()
    for peer in peers:
        peer(barrier)
    pl.semaphore_wait(barrier, count)


def signal_plane(q, g, x, n_src):
    slot = plane_slot(q, x)

    def go(barrier):
        @pl.when(g != 0)
        def _():
            pl.semaphore_signal(barrier, inc=1, device_id=(plane_peer(slot, q, g, x), g), device_id_type=MESH)

        @pl.loop(1, n_src)
        def _(i):
            peer = plane_peer((slot + i) % n_src, q, g, x)
            pl.semaphore_signal(barrier, inc=1, device_id=(peer, g), device_id_type=MESH)

    return go


def signal_group(q, g, n_grp):
    def go(barrier):
        for r in range(1, n_grp):
            pl.semaphore_signal(barrier, inc=1, device_id=(q, (g + r) % n_grp), device_id_type=MESH)

    return go


def forward_exchange(x, n_src, n_grp, idx, feat, cot, w_self, w_neigh, inc, cot_all, w_all, stage, send, recv, cot_s, cot_r, w_s, w_r, loc):
    q, g = lax.axis_index("dom"), lax.axis_index("grp")
    slots = stage.shape[1]
    quarter = cot_all.shape[1]
    fw = w_self.shape[0]
    slot = plane_slot(q, x)
    barrier = pltpu.get_barrier_semaphore()
    signal_plane(q, g, x, n_src)(barrier)
    signal_group(q, g, n_grp)(barrier)
    own = [
        pltpu.make_async_copy(cot.at[pl.ds(g * quarter, quarter)], cot_all.at[g], loc.at[0]),
        pltpu.make_async_copy(w_self, w_all.at[g, pl.ds(0, fw)], loc.at[1]),
        pltpu.make_async_copy(w_neigh, w_all.at[g, pl.ds(fw, fw)], loc.at[2]),
    ]
    for c in own:
        c.start()

    def fill(d):
        peer = plane_peer(d, q, g, x)
        for s in range(slots):
            stage[d, s] = feat[idx[peer, s]]
        return peer

    def remote(d, peer):
        return pltpu.make_async_remote_copy(
            src_ref=stage.at[d], dst_ref=inc.at[slot], send_sem=send.at[d], recv_sem=recv.at[slot],
            device_id=(peer, g), device_id_type=MESH)

    home = fill(slot)

    @pl.when(g == 0)
    def _():
        pl.semaphore_wait(barrier, n_src - 1 + n_grp - 1)

    @pl.when(g != 0)
    def _():
        pl.semaphore_wait(barrier, n_src + n_grp - 1)

    far = []
    for r in range(1, n_grp):
        y = (g + r) % n_grp
        to = dict(device_id=(q, y), device_id_type=MESH)
        far.append(pltpu.make_async_remote_copy(
            src_ref=cot.at[pl.ds(y * quarter, quarter)], dst_ref=cot_all.at[g],
            send_sem=cot_s.at[r - 1], recv_sem=cot_r.at[r - 1], **to))
        far.append(pltpu.make_async_remote_copy(
            src_ref=w_self, dst_ref=w_all.at[g, pl.ds(0, fw)],
            send_sem=w_s.at[r - 1, 0], recv_sem=w_r.at[r - 1, 0], **to))
        far.append(pltpu.make_async_remote_copy(
            src_ref=w_neigh, dst_ref=w_all.at[g, pl.ds(fw, fw)],
            send_sem=w_s.at[r - 1, 1], recv_sem=w_r.at[r - 1, 1], **to))

    @pl.when(g == 0)
    def _():
        pltpu.make_async_copy(stage.at[slot], inc.at[slot], recv.at[slot]).start()

    @pl.when(g != 0)
    def _():
        remote(slot, home).start()

    @pl.loop(1, n_src)
    def _(i):
        d = (slot + i) % n_src
        remote(d, fill(d)).start()

    for c in far:
        c.start()
    for c in own:
        c.wait()
    for c in far:
        c.wait()

    @pl.when(g != 0)
    def _():
        remote(slot, home).wait_send()

    @pl.loop(1, n_src)
    def _(i):
        d = (slot + i) % n_src
        remote(d, plane_peer(d, q, g, x)).wait_send()

    @pl.loop(0, n_src)
    def _(j):
        pltpu.make_async_copy(stage.at[j], inc.at[j], recv.at[j]).wait()


def aggregate_kernel(x, n_src, n_grp, in_rows, in_cols, out_rows, live, feat, inc, inner, outer, part, deg, acc, deg_acc, a_in, a_out, x_in, sem_in, sem_out, sem_x):
    q, g = lax.axis_index("dom"), lax.axis_index("grp")
    slots = inc.shape[1]
    n_in = inner.shape[0] // n_grp
    load_in = pltpu.make_async_copy(inner.at[pl.ds(g * n_in, n_in)], a_in, sem_in)
    load_in.start()
    load_x = pltpu.make_async_copy(inc, x_in, sem_x)
    load_x.start()

    def load(i):
        peer = plane_peer(i, q, g, x)
        return pltpu.make_async_copy(outer.at[pl.ds(peer * slots, slots)], a_out.at[i], sem_out)

    @pl.loop(0, n_src)
    def _(i):
        load(i).start()

    acc[...] = jnp.zeros_like(acc)
    deg_acc[...] = jnp.zeros_like(deg_acc)
    ones = jnp.ones((8, acc.shape[1]), BF16)

    def add(row, a, b):
        acc[row] += jnp.dot(a, b, preferred_element_type=F32)
        deg_acc[row] += lax.dot_general(ones, a, TRANS_B, preferred_element_type=F32)

    load_in.wait()

    @pl.loop(0, n_in)
    def _(n):
        add(in_rows[g * n_in + n], a_in[n], feat[in_cols[g * n_in + n]])

    load_x.wait()
    pltpu.make_async_copy(a_out, a_out, sem_out).wait()

    @pl.loop(0, n_src)
    def _(i):
        peer = plane_peer(i, q, g, x)
        for s in range(slots):
            @pl.when(s < live[peer])
            def _():
                add(out_rows[peer * slots + s], a_out[i, s], x_in[i, s])

    part[...] = acc[...].astype(BF16)
    deg[...] = deg_acc[...]


def dense_kernel(n_grp, part, deg, feat, cot_all, w_all, out_all, scaled, base, wgrad, got, got_d, sent, s1, r1, s2, r2, s3, r3):
    q, g = lax.axis_index("dom"), lax.axis_index("grp")
    n_blk, blk, fw = part.shape
    own_blk = n_blk // n_grp
    rows = own_blk * blk
    mine = pl.ds(g * own_blk, own_blk)
    barrier = pltpu.get_barrier_semaphore()
    signal_group(q, g, n_grp)(barrier)
    pl.semaphore_wait(barrier, n_grp - 1)
    copies, last = [], []
    for r in range(1, n_grp):
        y = (g + r) % n_grp
        to = dict(device_id=(q, y), device_id_type=MESH)
        theirs = pl.ds(y * own_blk, own_blk)
        copies.append(pltpu.make_async_remote_copy(
            src_ref=part.at[theirs], dst_ref=got.at[r - 1], send_sem=s1.at[r - 1], recv_sem=r1.at[r - 1], **to))
        copies.append(pltpu.make_async_remote_copy(
            src_ref=deg.at[theirs], dst_ref=got_d.at[r - 1], send_sem=s2.at[r - 1], recv_sem=r2.at[r - 1], **to))
        last.append(pltpu.make_async_remote_copy(
            src_ref=sent, dst_ref=scaled.at[mine], send_sem=s3.at[r - 1], recv_sem=r3.at[r - 1], **to))
    for c in copies:
        c.start()
    for c in copies:
        c.wait()
    total = part[mine].astype(F32)
    degree = 1.0 + deg[mine]
    for r in range(n_grp - 1):
        total = total + got[r].astype(F32)
        degree = degree + got_d[r]
    own_feat = feat[mine]
    divisor = jnp.stack([jnp.broadcast_to(degree[b, 0:1, :], (blk, blk)).T for b in range(own_blk)])
    agg = ((own_feat.astype(F32) + total) / divisor).astype(BF16)
    both = jnp.concatenate([own_feat.reshape(rows, fw), agg.reshape(rows, fw)], axis=1)
    back = jnp.zeros((rows, 2 * fw), F32)
    for j in range(n_grp):
        pre = jnp.dot(both, w_all[j], preferred_element_type=F32)
        sig = jax.nn.sigmoid(pre)
        out_all[j] = (pre * sig).astype(BF16)
        grad = (cot_all[j].astype(F32) * sig * (1.0 + pre * (1.0 - sig))).astype(BF16)
        wgrad[j] = lax.dot_general(both, grad, TRANS_A, preferred_element_type=F32)
        back = back + lax.dot_general(grad, w_all[j], TRANS_B, preferred_element_type=F32)
    down = (back[:, fw:].reshape(own_blk, blk, fw) / divisor).astype(BF16)
    sent[...] = down
    scaled[mine] = down
    base[...] = back[:, :fw].reshape(own_blk, blk, fw) + down.astype(F32)
    for c in last:
        c.start()
    for c in last:
        c.wait()


def backward_exchange(x, n_src, n_grp, out_rows, live, scaled, outer, out_all, inc, out, a_out, stage, send, recv, o_s, o_r, a_sem, loc):
    q, g = lax.axis_index("dom"), lax.axis_index("grp")
    slots = stage.shape[1]
    quarter = out_all.shape[1]
    slot = plane_slot(q, x)
    barrier = pltpu.get_barrier_semaphore()
    signal_plane(q, g, x, n_src)(barrier)
    signal_group(q, g, n_grp)(barrier)

    def load(d):
        peer = plane_peer(d, q, g, x)
        return pltpu.make_async_copy(outer.at[pl.ds(peer * slots, slots)], a_out.at[d], a_sem.at[d])

    @pl.loop(0, n_src)
    def _(i):
        load((slot + i) % n_src).start()

    own = pltpu.make_async_copy(out_all.at[g], out.at[pl.ds(g * quarter, quarter)], loc)
    own.start()

    def fill(d):
        peer = plane_peer(d, q, g, x)
        load(d).wait()
        for s in range(slots):
            value = lax.dot_general(a_out[d, s], scaled[out_rows[peer * slots + s]], TRANS_A, preferred_element_type=F32)
            stage[d, s] = jnp.where(s < live[peer], value, 0.0).astype(BF16)
        return peer

    def remote(d, peer):
        return pltpu.make_async_remote_copy(
            src_ref=stage.at[d], dst_ref=inc.at[slot], send_sem=send.at[d], recv_sem=recv.at[slot],
            device_id=(peer, g), device_id_type=MESH)

    home = fill(slot)

    @pl.when(g == 0)
    def _():
        pl.semaphore_wait(barrier, n_src - 1 + n_grp - 1)

    @pl.when(g != 0)
    def _():
        pl.semaphore_wait(barrier, n_src + n_grp - 1)

    @pl.when(g == 0)
    def _():
        pltpu.make_async_copy(stage.at[slot], inc.at[slot], recv.at[slot]).start()

    @pl.when(g != 0)
    def _():
        remote(slot, home).start()

    @pl.loop(1, n_src)
    def _(i):
        d = (slot + i) % n_src
        remote(d, fill(d)).start()

    far = []
    for r in range(1, n_grp):
        y = (g + r) % n_grp
        far.append(pltpu.make_async_remote_copy(
            src_ref=out_all.at[y], dst_ref=out.at[pl.ds(g * quarter, quarter)],
            send_sem=o_s.at[r - 1], recv_sem=o_r.at[r - 1], device_id=(q, y), device_id_type=MESH))
    for c in far:
        c.start()
    own.wait()
    for c in far:
        c.wait()

    @pl.when(g != 0)
    def _():
        remote(slot, home).wait_send()

    @pl.loop(1, n_src)
    def _(i):
        d = (slot + i) % n_src
        remote(d, plane_peer(d, q, g, x)).wait_send()

    @pl.loop(0, n_src)
    def _(j):
        pltpu.make_async_copy(stage.at[j], inc.at[j], recv.at[j]).wait()


def pull_kernel(x, n_src, n_grp, in_rows, in_cols, idx, scaled, inc, inner, part, acc, a_in, x_in, sem_in, sem_x):
    q, g = lax.axis_index("dom"), lax.axis_index("grp")
    slots = inc.shape[1]
    n_in = inner.shape[0] // n_grp
    load_in = pltpu.make_async_copy(inner.at[pl.ds(g * n_in, n_in)], a_in, sem_in)
    load_in.start()
    load_x = pltpu.make_async_copy(inc, x_in, sem_x)
    load_x.start()
    acc[...] = jnp.zeros_like(acc)
    load_in.wait()

    @pl.loop(0, n_in)
    def _(n):
        acc[in_cols[g * n_in + n]] += lax.dot_general(
            a_in[n], scaled[in_rows[g * n_in + n]], TRANS_A, preferred_element_type=F32)

    load_x.wait()

    @pl.loop(0, n_src)
    def _(i):
        peer = plane_peer(i, q, g, x)
        for s in range(slots):
            acc[idx[peer, s]] += x_in[i, s].astype(F32)

    part[...] = acc[...].astype(BF16)


def finish_kernel(n_grp, part, base, out, got, whole, s1, r1, s2, r2):
    q, g = lax.axis_index("dom"), lax.axis_index("grp")
    own_blk = base.shape[0]
    mine = pl.ds(g * own_blk, own_blk)
    barrier = pltpu.get_barrier_semaphore()
    signal_group(q, g, n_grp)(barrier)
    pl.semaphore_wait(barrier, n_grp - 1)
    first, last = [], []
    for r in range(1, n_grp):
        y = (g + r) % n_grp
        to = dict(device_id=(q, y), device_id_type=MESH)
        first.append(pltpu.make_async_remote_copy(
            src_ref=part.at[pl.ds(y * own_blk, own_blk)], dst_ref=got.at[r - 1],
            send_sem=s1.at[r - 1], recv_sem=r1.at[r - 1], **to))
        last.append(pltpu.make_async_remote_copy(
            src_ref=whole.at[mine], dst_ref=whole.at[mine], send_sem=s2.at[r - 1], recv_sem=r2.at[r - 1], **to))
    for c in first:
        c.start()
    for c in first:
        c.wait()
    total = base[...] + part[mine].astype(F32)
    for r in range(n_grp - 1):
        total = total + got[r].astype(F32)
    whole[mine] = total.astype(BF16)
    for c in last:
        c.start()
    for c in last:
        c.wait()
    out[...] = whole[...].astype(F32)


def params(collective=None, vmem=48):
    if collective is None:
        return pltpu.CompilerParams(vmem_limit_bytes=vmem << 20)
    return pltpu.CompilerParams(vmem_limit_bytes=vmem << 20, collective_id=collective, has_side_effects=True)


def shards(features, w_self, w_neigh, cotangent, inner_rows, inner_cols, inner_values, send_blocks, outer_rows, outer_values, live_count):
    blk = inner_values.shape[-1]
    nodes, fw = features.shape
    n_blk = nodes // blk
    parts, n_grp = lax.axis_size("dom"), lax.axis_size("grp")
    x = x_extent(parts)
    n_src = parts // n_grp
    slots = send_blocks.shape[-1]
    hid = w_self.shape[1]
    own_blk = n_blk // n_grp
    rows = own_blk * blk
    n_in = inner_values.shape[1] // n_grp
    inner, outer = inner_values[0], outer_values[0]
    rows_in, cols_in, rows_out, live, idx = inner_rows[0], inner_cols[0], outer_rows[0], live_count[0], send_blocks[0]
    feat = features.reshape(n_blk, blk, fw)
    dma, sds = pltpu.SemaphoreType.DMA, jax.ShapeDtypeStruct
    block = (n_src, slots, blk, fw)

    inc, cot_all, w_all = pl.pallas_call(
        functools.partial(forward_exchange, x, n_src, n_grp),
        out_shape=(sds(block, BF16), sds((n_grp, rows, hid), BF16), sds((n_grp, 2 * fw, hid), BF16)),
        in_specs=[SM, VM, ANY, ANY, ANY],
        out_specs=(ANY, ANY, ANY),
        scratch_shapes=[pltpu.VMEM(block, BF16), dma((n_src,)), dma((n_src,)), dma((n_grp - 1,)), dma((n_grp - 1,)),
                        dma((n_grp - 1, 2)), dma((n_grp - 1, 2)), dma((3,))],
        compiler_params=params(0), name="forward_exchange",
    )(idx, feat, cotangent, w_self, w_neigh)

    part, deg = pl.pallas_call(
        functools.partial(aggregate_kernel, x, n_src, n_grp),
        out_shape=(sds((n_blk, blk, fw), BF16), sds((n_blk, 8, blk), F32)),
        in_specs=[SM, SM, SM, SM, VM, ANY, ANY, ANY],
        out_specs=(VM, VM),
        scratch_shapes=[pltpu.VMEM((n_blk, blk, fw), F32), pltpu.VMEM((n_blk, 8, blk), F32),
                        pltpu.VMEM((n_in, blk, blk), BF16), pltpu.VMEM((n_src, slots, blk, blk), BF16),
                        pltpu.VMEM(block, BF16), dma, dma, dma],
        compiler_params=params(), name="aggregate",
    )(rows_in, cols_in, rows_out, live, feat, inc, inner, outer)

    y_sems = [dma((n_grp - 1,))] * 6
    out_all, scaled, base, wgrad = pl.pallas_call(
        functools.partial(dense_kernel, n_grp),
        out_shape=(sds((n_grp, rows, hid), BF16), sds((n_blk, blk, fw), BF16), sds((own_blk, blk, fw), F32), sds((n_grp, 2 * fw, hid), F32)),
        in_specs=[VM] * 5,
        out_specs=(VM,) * 4,
        scratch_shapes=[pltpu.VMEM((n_grp - 1, own_blk, blk, fw), BF16), pltpu.VMEM((n_grp - 1, own_blk, 8, blk), F32),
                        pltpu.VMEM((own_blk, blk, fw), BF16)] + y_sems,
        compiler_params=params(1), name="dense",
    )(part, deg, feat, cot_all, w_all)

    grads = lax.psum(lax.psum_scatter(wgrad, "grp", scatter_dimension=0, tiled=False), "dom")

    inc_back, layer_out = pl.pallas_call(
        functools.partial(backward_exchange, x, n_src, n_grp),
        out_shape=(sds(block, BF16), sds((nodes, hid), BF16)),
        in_specs=[SM, SM, VM, ANY, ANY],
        out_specs=(ANY, ANY),
        scratch_shapes=[pltpu.VMEM((n_src, slots, blk, blk), BF16), pltpu.VMEM(block, BF16), dma((n_src,)), dma((n_src,)),
                        dma((n_grp - 1,)), dma((n_grp - 1,)), dma((n_src,)), dma],
        compiler_params=params(2), name="backward_exchange",
    )(rows_out, live, scaled, outer, out_all)

    pulled = pl.pallas_call(
        functools.partial(pull_kernel, x, n_src, n_grp),
        out_shape=sds((n_blk, blk, fw), BF16),
        in_specs=[SM, SM, SM, VM, ANY, ANY],
        out_specs=VM,
        scratch_shapes=[pltpu.VMEM((n_blk, blk, fw), F32), pltpu.VMEM((n_in, blk, blk), BF16), pltpu.VMEM(block, BF16), dma, dma],
        compiler_params=params(), name="pull",
    )(rows_in, cols_in, idx, scaled, inc_back, inner)

    feature_grad = pl.pallas_call(
        functools.partial(finish_kernel, n_grp),
        out_shape=sds((n_blk, blk, fw), F32),
        in_specs=[VM, VM],
        out_specs=VM,
        scratch_shapes=[pltpu.VMEM((n_grp - 1, own_blk, blk, fw), BF16), pltpu.VMEM((n_blk, blk, fw), BF16)] + [dma((n_grp - 1,))] * 4,
        compiler_params=params(3), name="finish",
    )(pulled, base)

    return layer_out, feature_grad.reshape(nodes, fw), grads[:fw], grads[fw:]


def solution(mesh):
    placed = (
        P("dom", None),
        P(None, "grp"),
        P(None, "grp"),
        P("dom", "grp"),
        P("dom", None),
        P("dom", None),
        P("dom", None, None, None),
        P("dom", None, None),
        P("dom", None),
        P("dom", None, None, None),
        P("dom", None),
    )
    return jax.shard_map(
        shards,
        mesh=mesh,
        in_specs=placed,
        out_specs=(P("dom", "grp"), P("dom", None), P(None, "grp"), P(None, "grp")),
        check_vma=False,
    )
```

time: 582 us -> 322 us (0.55)
  waiting for transfers between devices: 390 us -> 150 us
  Pallas kernels: 0 us -> 145 us
  matrix products: 77.4 us -> 0 us
  local copies, waits for them, and re-layouts: 61.3 us -> 12.6 us
  starting transfers between devices: 24.5 us -> 0.08 us
  other arithmetic: 8.63 us -> 0 us
    psum x2 -> x1, waiting for transfers between devices: 272 us -> 122 us  [shards(): lax.psum(lax.psum_scatter(wgrad, 'grp', scatter_dimension=0, tiled=False)...]
    pallas_call x0 -> x6, Pallas kernels: none -> 145 us  [the longest x1 46.9 us: shards(): pl.pallas_call(functools.partial(backward_exchange, x, n_src, n_grp), out...]
    all_to_all x2 -> x0, waiting for transfers between devices: 118 us -> none  [the longest x1 118 us: shards(): lax.all_to_all(outgoing, 'dom', split_axis=0, concat_axis=0, tiled=True)]
    dot_general x16 -> x0, matrix products: 77.4 us -> none  [the longest x4 33 us: block_segment(): jnp.dot(one_hot, products.reshape(count, -1), precision=lax.Precision.HIG...]
    reduce_scatter x0 -> x1, waiting for transfers between devices: none -> 27.2 us  [shards(): lax.psum_scatter(wgrad, 'grp', scatter_dimension=0, tiled=False)]
    all_to_all x2 -> x0, starting transfers between devices: 24.2 us -> none  [the longest x1 13.3 us: shards(): lax.all_to_all(outgoing, 'dom', split_axis=0, concat_axis=0, tiled=True)]
    dot_general x3 -> x0, local copies, waits for them, and re-layouts: 24.1 us -> none  [the longest x1 12.6 us: shards(): jnp.einsum('nij,njf->nif', outer_a, incoming, preferred_element_type=jnp....]
    gather x4 -> x0, local copies, waits for them, and re-layouts: 21.8 us -> none  [the longest x1 9.07 us: shards(): outgoing = feat_blocks[targets]]
  transfers between devices with their start and end apart: 4 -> 2, of which waited for: 3 -> 2; matrix products, arithmetic and copies ran while one was open for 7% -> 0% of each run, Pallas kernels for 0% -> 21%
where the time goes in v1:
time: 322 us
  waiting for transfers between devices  150 us (47%)
  Pallas kernels  145 us (45%)
  between operations  14.2 us (4%)
  local copies, waits for them, and re-layouts  12.6 us (4%)
    psum x1, waiting for transfers between devices, shards(): lax.psum(lax.psum_scatter(wgrad, 'grp', scatter_dimension=0, tiled=False)...  122 us
    pallas_call x1, Pallas kernels, shards(): pl.pallas_call(functools.partial(backward_exchange, x, n_src, n_grp), out...  46.9 us
    pallas_call x1, Pallas kernels, shards(): pl.pallas_call(functools.partial(forward_exchange, x, n_src, n_grp), out_...  43.8 us
    pallas_call x1, Pallas kernels, shards(): pl.pallas_call(functools.partial(dense_kernel, n_grp), out_shape=(sds((n_...  27.3 us
    reduce_scatter x1, waiting for transfers between devices, shards(): lax.psum_scatter(wgrad, 'grp', scatter_dimension=0, tiled=False)  27.2 us
    pallas_call x1, Pallas kernels, shards(): pl.pallas_call(functools.partial(finish_kernel, n_grp), out_shape=sds((n_...  15.1 us
    unnamed x33, local copies, waits for them, and re-layouts  10.9 us
    pallas_call x1, Pallas kernels, shards(): pl.pallas_call(functools.partial(aggregate_kernel, x, n_src, n_grp), out_...  6.86 us
  transfers between devices with their start and end apart: 2, of which 2 were waited for; matrix products, arithmetic and copies ran while one was open for 0% of the time, Pallas kernels for 21%

profile of v1, /device:TPU:1, one launch (start us, length us, event | category | flops | bytes accessed | tf_op | source)
XLA Modules:
  0.0 321.6 jit_solution(4445217043426596119)
XLA Ops:
  7.2 0.0 reduce-scatter.2.cloned.1.call-start
  7.2 0.8 copy.15
  8.0 1.0 copy-done.2
  9.0 1.2 copy-done.4
  10.3 0.8 copy-done.5
  11.1 0.8 copy-done.6
  11.9 43.8 %forward_exchange.1 = (bf16[16,3,128,128]{3,2,1,0:T(8,128)(2,1)S(1)}, bf16[4,512,256]{2,1,0:T(8,128)(2,1)S(1)}, bf16[4,256,256]{2,1,0:T(8,128)(2,1)S(1)}) custom-call(s32[64,3]{1,0:T(8,128)S(1)} %bitcast.16, bf16[16,128,128]{2,1,0:T(8,128)(2,1)S(1)} %bitcast.12, bf16[2048,256]{1,0:T(8,128)(2,1)S(1)} %copy-done.4, bf16[128,256]{1,0:T(8,128)(2,1)S(1)} %copy-done.5, ...), custom_call_target="tpu_custom_call" | custom-call | tf_op jit(solution)/shard_map/forward_exchange/pallas_call | solution.py:411
  55.7 1.6 copy-done
  57.3 0.7 copy-done.7
  58.0 0.7 copy-done.9
  58.7 0.7 copy-done.11
  59.3 0.7 copy-done.13
  60.0 6.9 %aggregate.1 = (bf16[16,128,128]{2,1,0:T(8,128)(2,1)S(1)}, f32[16,8,128]{2,1,0:T(8,128)S(1)}) custom-call(s32[64]{0:T(128)S(1)} %bitcast.22, s32[64]{0:T(128)S(1)} %bitcast.24, s32[192]{0:T(256)S(1)} %bitcast.18, s32[64]{0:T(128)S(1)} %bitcast.20, bf16[16,128,128]{2,1,0:T(8,128)(2,1)S(1)} %bitcast.13, bf16[16,3,128,128]{3,2,1,0:T(8,128)(2,1)S(1)} %get-tuple-element.15.inc, ...), custom_call_target="tpu_custom_call" | custom-call | tf_op jit(solution)/shard_map/aggregate/pallas_call | solution.py:421
  66.9 27.3 %dense.1 = (bf16[4,512,256]{2,1,0:T(8,128)(2,1)S(1)}, bf16[16,128,128]{2,1,0:T(8,128)(2,1)S(1)}, f32[4,128,128]{2,1,0:T(8,128)S(1)}, f32[4,256,256]{2,1,0:T(8,128)}) custom-call(bf16[16,128,128]{2,1,0:T(8,128)(2,1)S(1)} %get-tuple-element.16.part, f32[16,8,128]{2,1,0:T(8,128)S(1)} %get-tuple-element.17.deg, bf16[16,128,128]{2,1,0:T(8,128)(2,1)S(1)} %bitcast.14, ...), custom_call_target="tpu_custom_call" | custom-call | tf_op jit(solution)/shard_map/dense/pallas_call | solution.py:433
  94.1 0.0 reduce-scatter.2.cloned.1.call-update
  94.2 0.0 all-reduce.2.cloned.1.call-start
  94.2 27.2 %reduce-scatter.2.cloned.1.call-done = f32[1,256,256]{2,1,0:T(8,128)} async-done(((f32[4,256,256]{2,1,0:T(8,128)}), f32[1,256,256]{2,1,0:T(8,128)}) %reduce-scatter.2.cloned.1.call-update) | async-done | bytes 262160 | tf_op jit(solution)/shard_map/reduce_scatter | solution.py:443
  121.5 46.9 %backward_exchange.1 = (bf16[16,3,128,128]{3,2,1,0:T(8,128)(2,1)S(1)}, bf16[2048,256]{1,0:T(8,128)(2,1)S(1)}) custom-call(s32[192]{0:T(256)S(1)} %bitcast.19, s32[64]{0:T(128)S(1)} %bitcast.21, bf16[16,128,128]{2,1,0:T(8,128)(2,1)S(1)} %get-tuple-element.20.scaled, bf16[192,128,128]{2,1,0:T(8,128)(2,1)} %bitcast.27, ...), custom_call_target="tpu_custom_call" | custom-call | tf_op jit(solution)/shard_map/backward_exchange/pallas_call | solution.py:445
  168.5 5.1 %pull.1.part = bf16[16,128,128]{2,1,0:T(8,128)(2,1)S(1)} custom-call(s32[64]{0:T(128)S(1)} %bitcast.23, s32[64]{0:T(128)S(1)} %bitcast.25, s32[64,3]{1,0:T(8,128)S(1)} %bitcast.17, bf16[16,128,128]{2,1,0:T(8,128)(2,1)S(1)} %get-tuple-element.20.scaled, bf16[16,3,128,128]{3,2,1,0:T(8,128)(2,1)S(1)} %get-tuple-element.23.inc, bf16[64,128,128]{2,1,0:T(8,128)(2,1)S(1)} %bitcast.11), custom_call_target="tpu_custom_call" | custom-call | tf_op jit(solution)/shard_map/pull/pallas_call | solution.py:455
  173.5 15.1 %finish.1 = f32[16,128,128]{2,1,0:T(8,128)S(1)} custom-call(bf16[16,128,128]{2,1,0:T(8,128)(2,1)S(1)} %pull.1.part, f32[4,128,128]{2,1,0:T(8,128)S(1)} %get-tuple-element.24.base), custom_call_target="tpu_custom_call" | custom-call | tf_op jit(solution)/shard_map/finish/pallas_call | solution.py:464
  188.7 122.5 %all-reduce.2.cloned.1.call-done = f32[256,256]{1,0:T(8,128)} async-done(((f32[256,256]{1,0:T(8,128)}), f32[256,256]{1,0:T(8,128)}) %all-reduce.2.cloned.1.call-update) | async-done | bytes 262160 | tf_op jit(solution)/shard_map/psum | solution.py:443
  311.2 1.7 fusion
  312.8 1.0 copy.19
  313.8 1.0 copy.20
  (22 shorter events, 0.1 us)
Async XLA Ops:
  7.2 114.2 %reduce-scatter.2.cloned.1.call-start = ((), (), s32[]{:S(2)}) async-start(), calls=%async_computation.1 | async-start | bytes 1310720 | tf_op jit(solution)/shard_map/reduce_scatter | solution.py:443
  8.0 1.0 copy-start.2
  9.0 1.2 copy-start.4
  10.2 0.8 copy-start.5
  11.1 0.8 copy-start.6
  11.9 43.8 %copy-start.3 = (bf16[2048,128]{1,0:T(8,128)(2,1)S(1)}, bf16[2048,128]{1,0:T(8,128)(2,1)}, u32[]{:S(2)}) copy-start(bf16[2048,128]{1,0:T(8,128)(2,1)} %param.11) | copy-start | bytes 1572868
  55.7 1.6 copy-start
  57.3 0.7 copy-start.7
  58.0 0.7 copy-start.9
  58.6 0.7 copy-start.11
  59.3 0.7 copy-start.13
  66.8 54.6 %copy-start.8 = (s32[1,192]{1,0:T(1,128)S(1)}, s32[1,192]{1,0:T(1,128)}, u32[]{:S(2)}) copy-start(s32[1,192]{1,0:T(1,128)} %param.19) | copy-start | bytes 2308
  66.8 54.6 %copy-start.10 = (s32[1,64]{1,0:T(1,128)S(1)}, s32[1,64]{1,0:T(1,128)}, u32[]{:S(2)}) copy-start(s32[1,64]{1,0:T(1,128)} %param.21) | copy-start | bytes 772
  94.2 217.0 %all-reduce.2.cloned.1.call-start = ((), (), s32[]{:S(2)}) async-start(), calls=%async_computation.2 | async-start | bytes 524288 | tf_op jit(solution)/shard_map/psum | solution.py:443
  121.5 47.0 %copy-start.1 = (bf16[1,64,128,128]{3,2,1,0:T(8,128)(2,1)S(1)}, bf16[1,64,128,128]{3,2,1,0:T(8,128)(2,1)}, u32[]{:S(2)}) copy-start(bf16[1,64,128,128]{3,2,1,0:T(8,128)(2,1)} %param.17) | copy-start | bytes 6291460
  121.5 47.0 %copy-start.12 = (s32[1,64]{1,0:T(1,128)S(1)}, s32[1,64]{1,0:T(1,128)}, u32[]{:S(2)}) copy-start(s32[1,64]{1,0:T(1,128)} %param.15) | copy-start | bytes 772
  121.5 47.0 %copy-start.14 = (s32[1,64]{1,0:T(1,128)S(1)}, s32[1,64]{1,0:T(1,128)}, u32[]{:S(2)}) copy-start(s32[1,64]{1,0:T(1,128)} %param.16) | copy-start | bytes 772
Sparse Core Ops, SparseCore 0:
  94.3 27.0 reduce-scatter.1
  125.3 185.8 all-reduce.1

commit v2 on v1

--- a/solution.py
+++ b/solution.py
@@ -11,6 +11,7 @@
 ANY = pl.BlockSpec(memory_space=pl.ANY)
 VM = pl.BlockSpec(memory_space=pltpu.VMEM)
 SM = pl.BlockSpec(memory_space=pltpu.SMEM)
+HB = pl.BlockSpec(memory_space=pltpu.HBM)
 F32 = jnp.float32
 BF16 = jnp.bfloat16
 TRANS_A = (((0,), (0,)), ((), ()))
@@ -61,13 +62,15 @@
     return go
 
 
-def forward_exchange(x, n_src, n_grp, idx, feat, cot, w_self, w_neigh, inc, cot_all, w_all, stage, send, recv, cot_s, cot_r, w_s, w_r, loc):
+def forward_exchange(x, n_src, n_grp, table, features, cot, w_self, w_neigh, inc, cot_all, w_all, feat, stage, send, recv, cot_s, cot_r, w_s, w_r, loc):
     q, g = lax.axis_index("dom"), lax.axis_index("grp")
     slots = stage.shape[1]
     quarter = cot_all.shape[1]
     fw = w_self.shape[0]
     slot = plane_slot(q, x)
     barrier = pltpu.get_barrier_semaphore()
+    load_feat = pltpu.make_async_copy(features, feat, loc.at[3])
+    load_feat.start()
     signal_plane(q, g, x, n_src)(barrier)
     signal_group(q, g, n_grp)(barrier)
     own = [
@@ -81,7 +84,7 @@
     def fill(d):
         peer = plane_peer(d, q, g, x)
         for s in range(slots):
-            stage[d, s] = feat[idx[peer, s]]
+            stage[d, s] = feat[table[peer * slots + s]]
         return peer
 
     def remote(d, peer):
@@ -89,6 +92,7 @@
             src_ref=stage.at[d], dst_ref=inc.at[slot], send_sem=send.at[d], recv_sem=recv.at[slot],
             device_id=(peer, g), device_id_type=MESH)
 
+    load_feat.wait()
     home = fill(slot)
 
     @pl.when(g == 0)
@@ -147,10 +151,19 @@
         pltpu.make_async_copy(stage.at[j], inc.at[j], recv.at[j]).wait()
 
 
-def aggregate_kernel(x, n_src, n_grp, in_rows, in_cols, out_rows, live, feat, inc, inner, outer, part, deg, acc, deg_acc, a_in, a_out, x_in, sem_in, sem_out, sem_x):
+def tables(parts, slots, n_inner):
+    out_rows = parts * slots
+    live = 2 * parts * slots
+    return out_rows, live, live + parts, live + parts + n_inner
+
+
+def aggregate_kernel(x, n_src, n_grp, table, features, inc, inner, outer, part, deg, feat, acc, deg_acc, a_in, a_out, x_in, sem_f, sem_in, sem_out, sem_x):
     q, g = lax.axis_index("dom"), lax.axis_index("grp")
     slots = inc.shape[1]
     n_in = inner.shape[0] // n_grp
+    out_rows, live, in_rows, in_cols = tables(n_grp * n_src, slots, inner.shape[0])
+    load_f = pltpu.make_async_copy(features, feat, sem_f)
+    load_f.start()
     load_in = pltpu.make_async_copy(inner.at[pl.ds(g * n_in, n_in)], a_in, sem_in)
     load_in.start()
     load_x = pltpu.make_async_copy(inc, x_in, sem_x)
@@ -172,11 +185,12 @@
         acc[row] += jnp.dot(a, b, preferred_element_type=F32)
         deg_acc[row] += lax.dot_general(ones, a, TRANS_B, preferred_element_type=F32)
 
+    load_f.wait()
     load_in.wait()
 
     @pl.loop(0, n_in)
     def _(n):
-        add(in_rows[g * n_in + n], a_in[n], feat[in_cols[g * n_in + n]])
+        add(table[in_rows + g * n_in + n], a_in[n], feat[table[in_cols + g * n_in + n]])
 
     load_x.wait()
     pltpu.make_async_copy(a_out, a_out, sem_out).wait()
@@ -185,22 +199,29 @@
     def _(i):
         peer = plane_peer(i, q, g, x)
         for s in range(slots):
-            @pl.when(s < live[peer])
+            @pl.when(s < table[live + peer])
             def _():
-                add(out_rows[peer * slots + s], a_out[i, s], x_in[i, s])
+                add(table[out_rows + peer * slots + s], a_out[i, s], x_in[i, s])
 
     part[...] = acc[...].astype(BF16)
     deg[...] = deg_acc[...]
 
 
-def dense_kernel(n_grp, part, deg, feat, cot_all, w_all, out_all, scaled, base, wgrad, got, got_d, sent, s1, r1, s2, r2, s3, r3):
+def dense_kernel(n_grp, part, deg, features, cots, ws, out_all, scaled, base, wgrad, feat, cot_all, w_all, got, got_d, sent, s1, r1, s2, r2, s3, r3, loc):
     q, g = lax.axis_index("dom"), lax.axis_index("grp")
     n_blk, blk, fw = part.shape
     own_blk = n_blk // n_grp
-    rows = own_blk * blk
+    rows, hid = own_blk * blk, ws.shape[2]
     mine = pl.ds(g * own_blk, own_blk)
     barrier = pltpu.get_barrier_semaphore()
     signal_group(q, g, n_grp)(barrier)
+    loads = [
+        pltpu.make_async_copy(features.at[mine], feat, loc.at[0]),
+        pltpu.make_async_copy(ws, w_all, loc.at[1]),
+        pltpu.make_async_copy(cots, cot_all, loc.at[2]),
+    ]
+    for c in loads:
+        c.start()
     pl.semaphore_wait(barrier, n_grp - 1)
     copies, last = [], []
     for r in range(1, n_grp):
@@ -215,6 +236,8 @@
             src_ref=sent, dst_ref=scaled.at[mine], send_sem=s3.at[r - 1], recv_sem=r3.at[r - 1], **to))
     for c in copies:
         c.start()
+    for c in loads:
+        c.wait()
     for c in copies:
         c.wait()
     total = part[mine].astype(F32)
@@ -222,7 +245,7 @@
     for r in range(n_grp - 1):
         total = total + got[r].astype(F32)
         degree = degree + got_d[r]
-    own_feat = feat[mine]
+    own_feat = feat[...]
     divisor = jnp.stack([jnp.broadcast_to(degree[b, 0:1, :], (blk, blk)).T for b in range(own_blk)])
     agg = ((own_feat.astype(F32) + total) / divisor).astype(BF16)
     both = jnp.concatenate([own_feat.reshape(rows, fw), agg.reshape(rows, fw)], axis=1)
@@ -232,7 +255,9 @@
         sig = jax.nn.sigmoid(pre)
         out_all[j] = (pre * sig).astype(BF16)
         grad = (cot_all[j].astype(F32) * sig * (1.0 + pre * (1.0 - sig))).astype(BF16)
-        wgrad[j] = lax.dot_general(both, grad, TRANS_A, preferred_element_type=F32)
+        gw = lax.dot_general(both, grad, TRANS_A, preferred_element_type=F32).astype(BF16)
+        for h in range(hid // 128):
+            wgrad[j, h] = gw[:, 128 * h:128 * (h + 1)]
         back = back + lax.dot_general(grad, w_all[j], TRANS_B, preferred_element_type=F32)
     down = (back[:, fw:].reshape(own_blk, blk, fw) / divisor).astype(BF16)
     sent[...] = down
@@ -244,11 +269,12 @@
         c.wait()
 
 
-def backward_exchange(x, n_src, n_grp, out_rows, live, scaled, outer, out_all, inc, out, a_out, stage, send, recv, o_s, o_r, a_sem, loc):
+def backward_exchange(x, n_src, n_grp, table, scaled, outer, out_all, wgrad, inc, out, wsum, a_out, stage, w_got, send, recv, o_s, o_r, w_s, w_r, a_sem, loc):
     q, g = lax.axis_index("dom"), lax.axis_index("grp")
     slots = stage.shape[1]
     quarter = out_all.shape[1]
     slot = plane_slot(q, x)
+    out_rows, live, _, _ = tables(n_grp * n_src, slots, 0)
     barrier = pltpu.get_barrier_semaphore()
     signal_plane(q, g, x, n_src)(barrier)
     signal_group(q, g, n_grp)(barrier)
@@ -261,15 +287,15 @@
     def _(i):
         load((slot + i) % n_src).start()
 
-    own = pltpu.make_async_copy(out_all.at[g], out.at[pl.ds(g * quarter, quarter)], loc)
+    own = pltpu.make_async_copy(out_all.at[g], out.at[g], loc)
     own.start()
 
     def fill(d):
         peer = plane_peer(d, q, g, x)
         load(d).wait()
         for s in range(slots):
-            value = lax.dot_general(a_out[d, s], scaled[out_rows[peer * slots + s]], TRANS_A, preferred_element_type=F32)
-            stage[d, s] = jnp.where(s < live[peer], value, 0.0).astype(BF16)
+            value = lax.dot_general(a_out[d, s], scaled[table[out_rows + peer * slots + s]], TRANS_A, preferred_element_type=F32)
+            stage[d, s] = jnp.where(s < table[live + peer], value, 0.0).astype(BF16)
         return peer
 
     def remote(d, peer):
@@ -287,28 +313,41 @@
     def _():
         pl.semaphore_wait(barrier, n_src + n_grp - 1)
 
-    @pl.when(g == 0)
-    def _():
-        pltpu.make_async_copy(stage.at[slot], inc.at[slot], recv.at[slot]).start()
-
-    @pl.when(g != 0)
-    def _():
-        remote(slot, home).start()
-
-    @pl.loop(1, n_src)
-    def _(i):
-        d = (slot + i) % n_src
-        remote(d, fill(d)).start()
-
-    far = []
+    far, grad_far = [], []
     for r in range(1, n_grp):
         y = (g + r) % n_grp
         far.append(pltpu.make_async_remote_copy(
-            src_ref=out_all.at[y], dst_ref=out.at[pl.ds(g * quarter, quarter)],
+            src_ref=out_all.at[y], dst_ref=out.at[g],
             send_sem=o_s.at[r - 1], recv_sem=o_r.at[r - 1], device_id=(q, y), device_id_type=MESH))
+        grad_far.append(pltpu.make_async_remote_copy(
+            src_ref=wgrad.at[y], dst_ref=w_got.at[r - 1],
+            send_sem=w_s.at[r - 1], recv_sem=w_r.at[r - 1], device_id=(q, y), device_id_type=MESH))
+    for c in grad_far:
+        c.start()
+
+    @pl.when(g == 0)
+    def _():
+        pltpu.make_async_copy(stage.at[slot], inc.at[slot], recv.at[slot]).start()
+
+    @pl.when(g != 0)
+    def _():
+        remote(slot, home).start()
+
+    @pl.loop(1, n_src)
+    def _(i):
+        d = (slot + i) % n_src
+        remote(d, fill(d)).start()
+
     for c in far:
         c.start()
     own.wait()
+    for c in grad_far:
+        c.wait()
+    for h in range(wsum.shape[0]):
+        total = wgrad[g, h].astype(F32)
+        for r in range(n_grp - 1):
+            total = total + w_got[r, h].astype(F32)
+        wsum[h] = total
     for c in far:
         c.wait()
 
@@ -326,7 +365,7 @@
         pltpu.make_async_copy(stage.at[j], inc.at[j], recv.at[j]).wait()
 
 
-def pull_kernel(x, n_src, n_grp, in_rows, in_cols, idx, scaled, inc, inner, part, acc, a_in, x_in, sem_in, sem_x):
+def pull_kernel(x, n_src, n_grp, table, scaled, inc, inner, out_parts, part, out, acc, a_in, x_in, sem_in, sem_x, sem_o):
     q, g = lax.axis_index("dom"), lax.axis_index("grp")
     slots = inc.shape[1]
     n_in = inner.shape[0] // n_grp
@@ -334,13 +373,16 @@
     load_in.start()
     load_x = pltpu.make_async_copy(inc, x_in, sem_x)
     load_x.start()
+    keep = pltpu.make_async_copy(out_parts, out, sem_o)
+    keep.start()
+    _, _, in_rows, in_cols = tables(n_grp * n_src, slots, inner.shape[0])
     acc[...] = jnp.zeros_like(acc)
     load_in.wait()
 
     @pl.loop(0, n_in)
     def _(n):
-        acc[in_cols[g * n_in + n]] += lax.dot_general(
-            a_in[n], scaled[in_rows[g * n_in + n]], TRANS_A, preferred_element_type=F32)
+        acc[table[in_cols + g * n_in + n]] += lax.dot_general(
+            a_in[n], scaled[table[in_rows + g * n_in + n]], TRANS_A, preferred_element_type=F32)
 
     load_x.wait()
 
@@ -348,18 +390,29 @@
     def _(i):
         peer = plane_peer(i, q, g, x)
         for s in range(slots):
-            acc[idx[peer, s]] += x_in[i, s].astype(F32)
+            acc[table[peer * slots + s]] += x_in[i, s].astype(F32)
 
     part[...] = acc[...].astype(BF16)
-
-
-def finish_kernel(n_grp, part, base, out, got, whole, s1, r1, s2, r2):
+    keep.wait()
+
+
+def finish_kernel(x, n_grp, part, base, pieces, whole, grads, got, near_got, far_sent, far_got, s1, r1, s2, r2, a_s, a_r, b_s, b_r, c_s, c_r, d_s, d_r):
     q, g = lax.axis_index("dom"), lax.axis_index("grp")
     own_blk = base.shape[0]
+    near, layers = near_got.shape[0], near_got.shape[1]
     mine = pl.ds(g * own_blk, own_blk)
+    z, k = q // near, q % near
     barrier = pltpu.get_barrier_semaphore()
     signal_group(q, g, n_grp)(barrier)
-    pl.semaphore_wait(barrier, n_grp - 1)
+
+    @pl.loop(1, near)
+    def _(r):
+        pl.semaphore_signal(barrier, inc=1, device_id=(z * near + (k + r) % near, g), device_id_type=MESH)
+
+    @pl.loop(1, layers)
+    def _(r):
+        pl.semaphore_signal(barrier, inc=1, device_id=((z + r) % layers * near + k, g), device_id_type=MESH)
+
     first, last = [], []
     for r in range(1, n_grp):
         y = (g + r) % n_grp
@@ -369,8 +422,48 @@
             send_sem=s1.at[r - 1], recv_sem=r1.at[r - 1], **to))
         last.append(pltpu.make_async_remote_copy(
             src_ref=whole.at[mine], dst_ref=whole.at[mine], send_sem=s2.at[r - 1], recv_sem=r2.at[r - 1], **to))
+
+    def near_peer(r):
+        return (k + r) % near
+
+    def far_peer(r):
+        return (z + r) % layers
+
+    def near_reduce(r):
+        return pltpu.make_async_remote_copy(
+            src_ref=pieces.at[pl.ds(near_peer(r) * layers, layers)], dst_ref=near_got.at[r],
+            send_sem=a_s.at[r], recv_sem=a_r.at[r], device_id=(z * near + near_peer(r), g), device_id_type=MESH)
+
+    def far_reduce(r):
+        return pltpu.make_async_remote_copy(
+            src_ref=far_sent.at[far_peer(r)], dst_ref=far_got.at[r],
+            send_sem=b_s.at[r], recv_sem=b_r.at[r], device_id=(far_peer(r) * near + k, g), device_id_type=MESH)
+
+    def far_gather(r):
+        return pltpu.make_async_remote_copy(
+            src_ref=grads.at[k * layers + z], dst_ref=grads.at[k * layers + z],
+            send_sem=c_s.at[r], recv_sem=c_r.at[r], device_id=(far_peer(r) * near + k, g), device_id_type=MESH)
+
+    def near_gather(r):
+        return pltpu.make_async_remote_copy(
+            src_ref=grads.at[pl.ds(k * layers, layers)], dst_ref=grads.at[pl.ds(k * layers, layers)],
+            send_sem=d_s.at[r], recv_sem=d_r.at[r], device_id=(z * near + near_peer(r), g), device_id_type=MESH)
+
+    def each(count, make, act):
+        @pl.loop(1, count)
+        def _(r):
+            act(make(r))
+
+    pl.semaphore_wait(barrier, n_grp - 1 + near - 1 + layers - 1)
     for c in first:
         c.start()
+    each(near, near_reduce, lambda c: c.start())
+    each(near, near_reduce, lambda c: c.wait())
+    total = pieces[pl.ds(k * layers, layers)]
+    for r in range(1, near):
+        total = total + near_got[r]
+    far_sent[...] = total
+    each(layers, far_reduce, lambda c: c.start())
     for c in first:
         c.wait()
     total = base[...] + part[mine].astype(F32)
@@ -379,9 +472,17 @@
     whole[mine] = total.astype(BF16)
     for c in last:
         c.start()
+    each(layers, far_reduce, lambda c: c.wait())
+    total = far_sent[z]
+    for r in range(1, layers):
+        total = total + far_got[r]
+    grads[k * layers + z] = total
+    each(layers, far_gather, lambda c: c.start())
+    each(layers, far_gather, lambda c: c.wait())
+    each(near, near_gather, lambda c: c.start())
+    each(near, near_gather, lambda c: c.wait())
     for c in last:
         c.wait()
-    out[...] = whole[...].astype(F32)
 
 
 def params(collective=None, vmem=48):
@@ -403,7 +504,7 @@
     rows = own_blk * blk
     n_in = inner_values.shape[1] // n_grp
     inner, outer = inner_values[0], outer_values[0]
-    rows_in, cols_in, rows_out, live, idx = inner_rows[0], inner_cols[0], outer_rows[0], live_count[0], send_blocks[0]
+    table = jnp.concatenate([send_blocks.reshape(-1), outer_rows[0], live_count[0], inner_rows[0], inner_cols[0]])
     feat = features.reshape(n_blk, blk, fw)
     dma, sds = pltpu.SemaphoreType.DMA, jax.ShapeDtypeStruct
     block = (n_src, slots, blk, fw)
@@ -411,64 +512,74 @@
     inc, cot_all, w_all = pl.pallas_call(
         functools.partial(forward_exchange, x, n_src, n_grp),
         out_shape=(sds(block, BF16), sds((n_grp, rows, hid), BF16), sds((n_grp, 2 * fw, hid), BF16)),
-        in_specs=[SM, VM, ANY, ANY, ANY],
+        in_specs=[SM, HB, HB, HB, HB],
         out_specs=(ANY, ANY, ANY),
-        scratch_shapes=[pltpu.VMEM(block, BF16), dma((n_src,)), dma((n_src,)), dma((n_grp - 1,)), dma((n_grp - 1,)),
-                        dma((n_grp - 1, 2)), dma((n_grp - 1, 2)), dma((3,))],
+        scratch_shapes=[pltpu.VMEM((n_blk, blk, fw), BF16), pltpu.VMEM(block, BF16), dma((n_src,)), dma((n_src,)), dma((n_grp - 1,)), dma((n_grp - 1,)),
+                        dma((n_grp - 1, 2)), dma((n_grp - 1, 2)), dma((4,))],
         compiler_params=params(0), name="forward_exchange",
-    )(idx, feat, cotangent, w_self, w_neigh)
+    )(table, feat, cotangent, w_self, w_neigh)
 
     part, deg = pl.pallas_call(
         functools.partial(aggregate_kernel, x, n_src, n_grp),
         out_shape=(sds((n_blk, blk, fw), BF16), sds((n_blk, 8, blk), F32)),
-        in_specs=[SM, SM, SM, SM, VM, ANY, ANY, ANY],
+        in_specs=[SM, HB, ANY, HB, HB],
         out_specs=(VM, VM),
-        scratch_shapes=[pltpu.VMEM((n_blk, blk, fw), F32), pltpu.VMEM((n_blk, 8, blk), F32),
+        scratch_shapes=[pltpu.VMEM((n_blk, blk, fw), BF16), pltpu.VMEM((n_blk, blk, fw), F32), pltpu.VMEM((n_blk, 8, blk), F32),
                         pltpu.VMEM((n_in, blk, blk), BF16), pltpu.VMEM((n_src, slots, blk, blk), BF16),
-                        pltpu.VMEM(block, BF16), dma, dma, dma],
+                        pltpu.VMEM(block, BF16), dma, dma, dma, dma],
         compiler_params=params(), name="aggregate",
-    )(rows_in, cols_in, rows_out, live, feat, inc, inner, outer)
+    )(table, feat, inc, inner, outer)
 
     y_sems = [dma((n_grp - 1,))] * 6
     out_all, scaled, base, wgrad = pl.pallas_call(
         functools.partial(dense_kernel, n_grp),
-        out_shape=(sds((n_grp, rows, hid), BF16), sds((n_blk, blk, fw), BF16), sds((own_blk, blk, fw), F32), sds((n_grp, 2 * fw, hid), F32)),
-        in_specs=[VM] * 5,
+        out_shape=(sds((n_grp, rows, hid), BF16), sds((n_blk, blk, fw), BF16), sds((own_blk, blk, fw), F32), sds((n_grp, hid // 128, 2 * fw, 128), BF16)),
+        in_specs=[VM, VM, HB, ANY, ANY],
         out_specs=(VM,) * 4,
-        scratch_shapes=[pltpu.VMEM((n_grp - 1, own_blk, blk, fw), BF16), pltpu.VMEM((n_grp - 1, own_blk, 8, blk), F32),
-                        pltpu.VMEM((own_blk, blk, fw), BF16)] + y_sems,
+        scratch_shapes=[pltpu.VMEM((own_blk, blk, fw), BF16), pltpu.VMEM((n_grp, rows, hid), BF16), pltpu.VMEM((n_grp, 2 * fw, hid), BF16),
+                        pltpu.VMEM((n_grp - 1, own_blk, blk, fw), BF16), pltpu.VMEM((n_grp - 1, own_blk, 8, blk), F32),
+                        pltpu.VMEM((own_blk, blk, fw), BF16)] + y_sems + [dma((3,))],
         compiler_params=params(1), name="dense",
     )(part, deg, feat, cot_all, w_all)
 
-    grads = lax.psum(lax.psum_scatter(wgrad, "grp", scatter_dimension=0, tiled=False), "dom")
-
-    inc_back, layer_out = pl.pallas_call(
+    halves = hid // 128
+    inc_back, out_parts, wsum = pl.pallas_call(
         functools.partial(backward_exchange, x, n_src, n_grp),
-        out_shape=(sds(block, BF16), sds((nodes, hid), BF16)),
-        in_specs=[SM, SM, VM, ANY, ANY],
-        out_specs=(ANY, ANY),
-        scratch_shapes=[pltpu.VMEM((n_src, slots, blk, blk), BF16), pltpu.VMEM(block, BF16), dma((n_src,)), dma((n_src,)),
-                        dma((n_grp - 1,)), dma((n_grp - 1,)), dma((n_src,)), dma],
+        out_shape=(sds(block, BF16), sds((n_grp, rows, hid), BF16), sds((halves, 2 * fw, 128), F32)),
+        in_specs=[SM, VM, HB, ANY, VM],
+        out_specs=(ANY, ANY, VM),
+        scratch_shapes=[pltpu.VMEM((n_src, slots, blk, blk), BF16), pltpu.VMEM(block, BF16), pltpu.VMEM((n_grp - 1, halves, 2 * fw, 128), BF16),
+                        dma((n_src,)), dma((n_src,)), dma((n_grp - 1,)), dma((n_grp - 1,)), dma((n_grp - 1,)), dma((n_grp - 1,)),
+                        dma((n_src,)), dma],
         compiler_params=params(2), name="backward_exchange",
-    )(rows_out, live, scaled, outer, out_all)
-
-    pulled = pl.pallas_call(
+    )(table, scaled, outer, out_all, wgrad)
+
+    pulled, layer_out = pl.pallas_call(
         functools.partial(pull_kernel, x, n_src, n_grp),
-        out_shape=sds((n_blk, blk, fw), BF16),
-        in_specs=[SM, SM, SM, VM, ANY, ANY],
-        out_specs=VM,
-        scratch_shapes=[pltpu.VMEM((n_blk, blk, fw), F32), pltpu.VMEM((n_in, blk, blk), BF16), pltpu.VMEM(block, BF16), dma, dma],
+        out_shape=(sds((n_blk, blk, fw), BF16), sds((n_grp, rows, hid), BF16)),
+        in_specs=[SM, VM, ANY, HB, ANY],
+        out_specs=(VM, ANY),
+        scratch_shapes=[pltpu.VMEM((n_blk, blk, fw), F32), pltpu.VMEM((n_in, blk, blk), BF16), pltpu.VMEM(block, BF16), dma, dma, dma],
         compiler_params=params(), name="pull",
-    )(rows_in, cols_in, idx, scaled, inc_back, inner)
-
-    feature_grad = pl.pallas_call(
-        functools.partial(finish_kernel, n_grp),
-        out_shape=sds((n_blk, blk, fw), F32),
-        in_specs=[VM, VM],
-        out_specs=VM,
-        scratch_shapes=[pltpu.VMEM((n_grp - 1, own_blk, blk, fw), BF16), pltpu.VMEM((n_blk, blk, fw), BF16)] + [dma((n_grp - 1,))] * 4,
+    )(table, scaled, inc_back, inner, out_parts)
+
+    near = 2 * x
+    layers = parts // near
+    pieces = wsum.reshape(parts, -1, 128)
+    depth = pieces.shape[1]
+    whole, grads = pl.pallas_call(
+        functools.partial(finish_kernel, x, n_grp),
+        out_shape=(sds((n_blk, blk, fw), BF16), sds(pieces.shape, F32)),
+        in_specs=[VM, VM, VM],
+        out_specs=(VM, VM),
+        scratch_shapes=[pltpu.VMEM((n_grp - 1, own_blk, blk, fw), BF16), pltpu.VMEM((near, layers, depth, 128), F32), pltpu.VMEM((layers, depth, 128), F32),
+                        pltpu.VMEM((layers, depth, 128), F32)]
+        + [dma((n_grp - 1,))] * 4 + [dma((near,))] * 2 + [dma((layers,))] * 2 + [dma((layers,))] * 2 + [dma((near,))] * 2,
         compiler_params=params(3), name="finish",
-    )(pulled, base)
+    )(pulled, base, pieces)
+    grads = jnp.concatenate([grads.reshape(halves, 2 * fw, 128)[h] for h in range(halves)], axis=1)
+    feature_grad = whole.astype(F32)
+    layer_out = layer_out.reshape(nodes, hid)
 
     return layer_out, feature_grad.reshape(nodes, fw), grads[:fw], grads[fw:]
 

time: 322 us -> 166 us (0.52)
  waiting for transfers between devices: 150 us -> 0 us
  between operations: 14.2 us -> 0.73 us
  Pallas kernels: 145 us -> 156 us
  local copies, waits for them, and re-layouts: 12.6 us -> 7.25 us
    psum x1 -> x0, waiting for transfers between devices: 122 us -> none  [shards(): lax.psum(lax.psum_scatter(wgrad, 'grp', scatter_dimension=0, tiled=False)...]
    reduce_scatter x1 -> x0, waiting for transfers between devices: 27.2 us -> none  [shards(): lax.psum_scatter(wgrad, 'grp', scatter_dimension=0, tiled=False)]
    pallas_call x1, Pallas kernels: 15.1 us -> 30.1 us  [shards(): pl.pallas_call(functools.partial(finish_kernel, x, n_grp), out_shape=(sds...]
    unnamed x33 -> x15, local copies, waits for them, and re-layouts: 10.9 us -> 6.31 us
  transfers between devices with their start and end apart: 2 -> 0, of which waited for: 2 -> 0; matrix products, arithmetic and copies ran while one was open for 0% -> 0% of each run, Pallas kernels for 21% -> 0%
where the time goes in v2:
time: 166 us
  Pallas kernels  156 us (94%)
  local copies, waits for them, and re-layouts  7.25 us (4%)
  other arithmetic  1.79 us (1%)
    pallas_call x1, Pallas kernels, shards(): pl.pallas_call(functools.partial(backward_exchange, x, n_src, n_grp), out...  43.9 us
    pallas_call x1, Pallas kernels, shards(): pl.pallas_call(functools.partial(forward_exchange, x, n_src, n_grp), out_...  43.3 us
    pallas_call x1, Pallas kernels, shards(): pl.pallas_call(functools.partial(finish_kernel, x, n_grp), out_shape=(sds...  30.1 us
    pallas_call x1, Pallas kernels, shards(): pl.pallas_call(functools.partial(dense_kernel, n_grp), out_shape=(sds((n_...  25.3 us
    pallas_call x1, Pallas kernels, shards(): pl.pallas_call(functools.partial(aggregate_kernel, x, n_src, n_grp), out_...  8.91 us
    unnamed x15, local copies, waits for them, and re-layouts  6.31 us
    pallas_call x1, Pallas kernels, shards(): pl.pallas_call(functools.partial(pull_kernel, x, n_src, n_grp), out_shape...  4.59 us

profile of v2, /device:TPU:1, one launch (start us, length us, event | category | flops | bytes accessed | tf_op | source)
XLA Modules:
  0.0 166.0 jit_solution(1940839133573829558)
XLA Ops:
  0.6 0.8 copy.15
  1.4 0.1 reshape.32
  1.5 0.8 concatenate.6.table
  2.3 0.0 copy-start.2
  2.3 1.0 copy-done.2
  3.4 0.0 copy-start.4
  3.4 1.2 copy-done.4
  4.6 0.0 copy-start.5
  4.6 0.8 copy-done.5
  5.4 0.0 copy-start.6
  5.4 0.8 copy-done.6
  6.3 43.3 %forward_exchange.1 = (bf16[16,3,128,128]{3,2,1,0:T(8,128)(2,1)S(1)}, bf16[4,512,256]{2,1,0:T(8,128)(2,1)S(1)}, bf16[4,256,256]{2,1,0:T(8,128)(2,1)S(1)}) custom-call(s32[576]{0:T(1024)S(1)} %concatenate.6.table, bf16[16,128,128]{2,1,0:T(8,128)(2,1)S(1)} %bitcast.18, bf16[2048,256]{1,0:T(8,128)(2,1)S(1)} %copy-done.4, bf16[128,256]{1,0:T(8,128)(2,1)S(1)} %copy-done.5, ...), custom_call_target="tpu_custom_call" | custom-call | tf_op jit(solution)/shard_map/forward_exchange/pallas_call | solution.py:512
  49.6 0.0 copy-start
  49.6 1.6 copy-done
  51.2 8.9 %aggregate.1 = (bf16[16,128,128]{2,1,0:T(8,128)(2,1)S(1)}, f32[16,8,128]{2,1,0:T(8,128)S(1)}) custom-call(s32[576]{0:T(1024)S(1)} %concatenate.6.table, bf16[16,128,128]{2,1,0:T(8,128)(2,1)S(1)} %bitcast.19, bf16[16,3,128,128]{3,2,1,0:T(8,128)(2,1)S(1)} %get-tuple-element.20.inc, bf16[64,128,128]{2,1,0:T(8,128)(2,1)S(1)} %bitcast.16, ...), custom_call_target="tpu_custom_call" | custom-call | tf_op jit(solution)/shard_map/aggregate/pallas_call | solution.py:522
  60.1 0.0 copy-done.3
  60.1 25.3 %dense.1 = (bf16[4,512,256]{2,1,0:T(8,128)(2,1)S(1)}, bf16[16,128,128]{2,1,0:T(8,128)(2,1)S(1)}, f32[4,128,128]{2,1,0:T(8,128)S(1)}, bf16[4,2,256,128]{3,2,1,0:T(8,128)(2,1)S(1)}) custom-call(bf16[16,128,128]{2,1,0:T(8,128)(2,1)S(1)} %get-tuple-element.21.part, f32[16,8,128]{2,1,0:T(8,128)S(1)} %get-tuple-element.22.deg, bf16[16,128,128]{2,1,0:T(8,128)(2,1)S(1)} %bitcast.20, ...), custom_call_target="tpu_custom_call" | custom-call | tf_op jit(solution)/shard_map/dense/pallas_call | solution.py:534
  85.5 0.0 copy-start.1
  85.5 43.9 %backward_exchange.1 = (bf16[16,3,128,128]{3,2,1,0:T(8,128)(2,1)S(1)}, bf16[4,512,256]{2,1,0:T(8,128)(2,1)S(1)}, f32[2,256,128]{2,1,0:T(8,128)S(1)}) custom-call(s32[576]{0:T(1024)S(1)} %concatenate.6.table, bf16[16,128,128]{2,1,0:T(8,128)(2,1)S(1)} %get-tuple-element.25.scaled, bf16[192,128,128]{2,1,0:T(8,128)(2,1)} %bitcast.23, ...), custom_call_target="tpu_custom_call" | custom-call | tf_op jit(solution)/shard_map/backward_exchange/pallas_call | solution.py:546
  129.4 0.0 copy-done.1
  129.4 4.6 %pull.1 = (bf16[16,128,128]{2,1,0:T(8,128)(2,1)S(1)}, bf16[4,512,256]{2,1,0:T(8,128)(2,1)}) custom-call(s32[576]{0:T(1024)S(1)} %concatenate.6.table, bf16[16,128,128]{2,1,0:T(8,128)(2,1)S(1)} %get-tuple-element.25.scaled, bf16[16,3,128,128]{3,2,1,0:T(8,128)(2,1)S(1)} %get-tuple-element.28.inc, bf16[64,128,128]{2,1,0:T(8,128)(2,1)S(1)} %bitcast.17, ...), custom_call_target="tpu_custom_call" | custom-call | tf_op jit(solution)/shard_map/pull/pallas_call | solution.py:557
  134.0 30.1 %finish.1 = (bf16[16,128,128]{2,1,0:T(8,128)(2,1)S(1)}, f32[64,8,128]{2,1,0:T(8,128)S(1)}) custom-call(bf16[16,128,128]{2,1,0:T(8,128)(2,1)S(1)} %get-tuple-element.31.part, f32[4,128,128]{2,1,0:T(8,128)S(1)} %get-tuple-element.32.base, f32[64,8,128]{2,1,0:T(8,128)S(1)} %bitcast.21), custom_call_target="tpu_custom_call" | custom-call | tf_op jit(solution)/shard_map/finish/pallas_call | solution.py:570
  164.2 0.7 pad_maximum_fusion
  164.9 1.1 bitcast_convert_fusion
  (2 shorter events, 0.0 us)
Async XLA Ops:
  2.3 1.0 copy-start.2
  3.4 1.2 copy-start.4
  4.6 0.8 copy-start.5
  5.4 0.8 copy-start.6
  49.6 1.6 copy-start
  51.2 8.9 %copy-start.3 = (bf16[2048,128]{1,0:T(8,128)(2,1)S(1)}, bf16[2048,128]{1,0:T(8,128)(2,1)}, u32[]{:S(2)}) copy-start(bf16[2048,128]{1,0:T(8,128)(2,1)} %param.11) | copy-start | bytes 1572868
  85.5 44.0 %copy-start.1 = (bf16[1,64,128,128]{3,2,1,0:T(8,128)(2,1)S(1)}, bf16[1,64,128,128]{3,2,1,0:T(8,128)(2,1)}, u32[]{:S(2)}) copy-start(bf16[1,64,128,128]{3,2,1,0:T(8,128)(2,1)} %param.17) | copy-start | bytes 6291460

commit v3 on v1

v3 whole, which is shorter than its diff:
```python
import functools

import jax
import jax.numpy as jnp
from jax import lax
from jax.experimental import pallas as pl
from jax.experimental.pallas import tpu as pltpu
from jax.sharding import PartitionSpec as P

MESH = pl.DeviceIdType.MESH
ANY = pl.BlockSpec(memory_space=pl.ANY)
VM = pl.BlockSpec(memory_space=pltpu.VMEM)
SM = pl.BlockSpec(memory_space=pltpu.SMEM)
HB = pl.BlockSpec(memory_space=pltpu.HBM)
F32 = jnp.float32
BF16 = jnp.bfloat16
TRANS_A = (((0,), (0,)), ((), ()))
TRANS_B = (((1,), (1,)), ((), ()))


def x_extent(parts):
    return 4 if parts == 64 else 1


def plane_peer(i, q, g, x):
    z = q // (2 * x)
    return (((i // x) * 2 + (z + g // 2) % 2) * x + i % x) * 2 + (q + g) % 2


def plane_slot(q, x):
    return (q // (4 * x)) * x + (q // 2) % x


def enter(peers, count):
    barrier = pltpu.get_barrier_semaphore()
    for peer in peers:
        peer(barrier)
    pl.semaphore_wait(barrier, count)


def signal_plane(q, g, x, n_src):
    slot = plane_slot(q, x)

    def go(barrier):
        @pl.when(g != 0)
        def _():
            pl.semaphore_signal(barrier, inc=1, device_id=(plane_peer(slot, q, g, x), g), device_id_type=MESH)

        @pl.loop(1, n_src)
        def _(i):
            peer = plane_peer((slot + i) % n_src, q, g, x)
            pl.semaphore_signal(barrier, inc=1, device_id=(peer, g), device_id_type=MESH)

    return go


def signal_group(q, g, n_grp):
    def go(barrier):
        for r in range(1, n_grp):
            pl.semaphore_signal(barrier, inc=1, device_id=(q, (g + r) % n_grp), device_id_type=MESH)

    return go


def tables(parts, slots, n_inner):
    out_rows = parts * slots
    live = 2 * parts * slots
    return out_rows, live, live + parts, live + parts + n_inner


def signal_ring(q, g, near, layers):
    z, k = q // near, q % near

    def go(barrier):
        @pl.loop(1, near)
        def _(r):
            pl.semaphore_signal(barrier, inc=1, device_id=(z * near + (k + r) % near, g), device_id_type=MESH)

        @pl.loop(1, layers)
        def _(r):
            pl.semaphore_signal(barrier, inc=1, device_id=((z + r) % layers * near + k, g), device_id_type=MESH)

    return go


def each(first, count, make, act):
    @pl.loop(first, count)
    def _(r):
        act(make(r))


def start(c):
    c.start()


def wait(c):
    c.wait()


def forward_exchange(x, n_src, n_grp, table, keys, places, features, cot, w_self, w_neigh, inner, outer,
                     inc, cot_all, w_all, place_all, cols, divisor,
                     feat, stage, blocks, row_sums, send, recv, cot_s, cot_r, w_s, w_r, p_s, p_r, loc):
    q, g = lax.axis_index("dom"), lax.axis_index("grp")
    slots = stage.shape[1]
    own = cot_all.shape[2]
    fw = w_self.shape[0]
    n_blk, blk, _ = feat.shape
    near = 2 * x
    layers = places.shape[0]
    z, k = q // near, q % near
    slot = plane_slot(q, x)
    n_out, n_in = outer.shape[0], inner.shape[0]
    barrier = pltpu.get_barrier_semaphore()
    load_feat = pltpu.make_async_copy(features, feat, loc.at[3])
    load_feat.start()
    signal_plane(q, g, x, n_src)(barrier)
    signal_group(q, g, n_grp)(barrier)

    @pl.loop(1, layers)
    def _(r):
        pl.semaphore_signal(barrier, inc=1, device_id=((z + r) % layers * near + k, g), device_id_type=MESH)

    mine = pl.ds(pl.multiple_of(g * own, own), own)
    local = [
        pltpu.make_async_copy(cot.at[:, mine], cot_all.at[g], loc.at[0]),
        pltpu.make_async_copy(w_self, w_all.at[g, pl.ds(0, fw)], loc.at[1]),
        pltpu.make_async_copy(w_neigh, w_all.at[g, pl.ds(fw, fw)], loc.at[2]),
        pltpu.make_async_copy(places.at[z], place_all.at[z], loc.at[6]),
    ]
    loads = [
        pltpu.make_async_copy(outer, blocks.at[pl.ds(0, n_out)], loc.at[4]),
        pltpu.make_async_copy(inner, blocks.at[pl.ds(n_out, n_in)], loc.at[5]),
    ]

    def fill(d):
        peer = plane_peer(d, q, g, x)
        for s in range(slots):
            stage[d, s] = feat[table[peer * slots + s]]
        return peer

    def remote(d, peer):
        return pltpu.make_async_remote_copy(
            src_ref=stage.at[d], dst_ref=inc.at[slot], send_sem=send.at[d], recv_sem=recv.at[slot],
            device_id=(peer, g), device_id_type=MESH)

    def place(r):
        to = (z + r) % layers
        return pltpu.make_async_remote_copy(
            src_ref=places.at[to], dst_ref=place_all.at[z], send_sem=p_s.at[r], recv_sem=p_r.at[r],
            device_id=(to * near + k, g), device_id_type=MESH)

    load_feat.wait()
    home = fill(slot)
    others = n_grp - 1 + layers - 1

    @pl.when(g == 0)
    def _():
        pl.semaphore_wait(barrier, n_src - 1 + others)

    @pl.when(g != 0)
    def _():
        pl.semaphore_wait(barrier, n_src + others)

    far = []
    for r in range(1, n_grp):
        y = (g + r) % n_grp
        to = dict(device_id=(q, y), device_id_type=MESH)
        theirs = pl.ds(pl.multiple_of(y * own, own), own)
        far.append(pltpu.make_async_remote_copy(
            src_ref=cot.at[:, theirs], dst_ref=cot_all.at[g],
            send_sem=cot_s.at[r - 1], recv_sem=cot_r.at[r - 1], **to))
        far.append(pltpu.make_async_remote_copy(
            src_ref=w_self, dst_ref=w_all.at[g, pl.ds(0, fw)],
            send_sem=w_s.at[r - 1, 0], recv_sem=w_r.at[r - 1, 0], **to))
        far.append(pltpu.make_async_remote_copy(
            src_ref=w_neigh, dst_ref=w_all.at[g, pl.ds(fw, fw)],
            send_sem=w_s.at[r - 1, 1], recv_sem=w_r.at[r - 1, 1], **to))

    @pl.when(g == 0)
    def _():
        pltpu.make_async_copy(stage.at[slot], inc.at[slot], recv.at[slot]).start()

    @pl.when(g != 0)
    def _():
        remote(slot, home).start()

    @pl.loop(1, n_src)
    def _(i):
        d = (slot + i) % n_src
        remote(d, fill(d)).start()

    for c in far + local + loads:
        c.start()
    each(1, layers, place, start)

    row = lax.broadcasted_iota(jnp.int32, (own + 16, blk), 0)
    lane = lax.broadcasted_iota(jnp.int32, (own + 16, blk), 1)
    pick = jnp.where((row == own) | (lane == row + g * own) & (row < own), 1.0, 0.0).astype(BF16)
    for c in loads:
        c.wait()

    @pl.loop(0, (n_out + n_in) // 4)
    def _(m):
        for u in range(4):
            n = m * 4 + u
            got = lax.dot_general(pick, blocks[n], TRANS_B, preferred_element_type=F32)
            cols[n] = got[:own].astype(BF16)
            row_sums[pl.ds(n, 1), :] = got[own:own + 1]

    hits = jnp.where(lax.broadcasted_iota(jnp.int32, (n_blk, n_out + n_in), 0) == keys[...], 1.0, 0.0)
    degree = 1.0 + jnp.dot(hits, row_sums[...], precision=lax.Precision.HIGHEST, preferred_element_type=F32)
    sel = (lax.broadcasted_iota(jnp.int32, (own, blk), 1) == lax.broadcasted_iota(jnp.int32, (own, blk), 0) + g * own)
    for b in range(n_blk):
        column = jnp.sum(jnp.where(sel, degree[b:b + 1], 0.0), axis=1, keepdims=True)
        divisor[b] = jnp.broadcast_to(column, (own, fw))

    for c in local:
        c.wait()
    for c in far:
        c.wait()
    each(1, layers, place, wait)

    @pl.when(g != 0)
    def _():
        remote(slot, home).wait_send()

    @pl.loop(1, n_src)
    def _(i):
        d = (slot + i) % n_src
        remote(d, plane_peer(d, q, g, x)).wait_send()

    @pl.loop(0, n_src)
    def _(j):
        pltpu.make_async_copy(stage.at[j], inc.at[j], recv.at[j]).wait()


def aggregate_kernel(x, n_src, n_grp, table, features, inc, inner, outer, part, feat, acc, a_in, a_out, x_in, sem_f, sem_in, sem_out, sem_x):
    q, g = lax.axis_index("dom"), lax.axis_index("grp")
    slots = inc.shape[1]
    n_in = inner.shape[0] // n_grp
    out_rows, live, in_rows, in_cols = tables(n_grp * n_src, slots, inner.shape[0])
    load_f = pltpu.make_async_copy(features, feat, sem_f)
    load_f.start()
    load_in = pltpu.make_async_copy(inner.at[pl.ds(g * n_in, n_in)], a_in, sem_in)
    load_in.start()
    load_x = pltpu.make_async_copy(inc, x_in, sem_x)
    load_x.start()

    def load(i):
        peer = plane_peer(i, q, g, x)
        return pltpu.make_async_copy(outer.at[pl.ds(peer * slots, slots)], a_out.at[i], sem_out)

    @pl.loop(0, n_src)
    def _(i):
        load(i).start()

    acc[...] = jnp.zeros_like(acc)
    load_f.wait()
    load_in.wait()

    @pl.loop(0, n_in)
    def _(n):
        acc[table[in_rows + g * n_in + n]] += jnp.dot(
            a_in[n], feat[table[in_cols + g * n_in + n]], preferred_element_type=F32)

    load_x.wait()
    pltpu.make_async_copy(a_out, a_out, sem_out).wait()

    @pl.loop(0, n_src)
    def _(i):
        peer = plane_peer(i, q, g, x)
        for s in range(slots):
            @pl.when(s < table[live + peer])
            def _():
                acc[table[out_rows + peer * slots + s]] += jnp.dot(a_out[i, s], x_in[i, s], preferred_element_type=F32)

    part[...] = acc[...].astype(BF16)


def dense_kernel(n_grp, part, features, divisor, cots, ws, out_all, scaled, base, wgrad, feat, cot_all, w_all, got, sent, s1, r1, s3, r3, loc):
    q, g = lax.axis_index("dom"), lax.axis_index("grp")
    n_blk, blk, fw = part.shape
    own = base.shape[1]
    rows, hid = n_blk * own, ws.shape[2]
    mine = pl.ds(pl.multiple_of(g * own, own), own)
    barrier = pltpu.get_barrier_semaphore()
    signal_group(q, g, n_grp)(barrier)
    loads = [
        pltpu.make_async_copy(features.at[:, mine], feat, loc.at[0]),
        pltpu.make_async_copy(ws, w_all, loc.at[1]),
        pltpu.make_async_copy(cots, cot_all, loc.at[2]),
    ]
    for c in loads:
        c.start()
    pl.semaphore_wait(barrier, n_grp - 1)
    copies, last = [], []
    for r in range(1, n_grp):
        y = (g + r) % n_grp
        to = dict(device_id=(q, y), device_id_type=MESH)
        theirs = pl.ds(pl.multiple_of(y * own, own), own)
        copies.append(pltpu.make_async_remote_copy(
            src_ref=part.at[:, theirs], dst_ref=got.at[r - 1], send_sem=s1.at[r - 1], recv_sem=r1.at[r - 1], **to))
        last.append(pltpu.make_async_remote_copy(
            src_ref=sent, dst_ref=scaled.at[:, mine], send_sem=s3.at[r - 1], recv_sem=r3.at[r - 1], **to))
    for c in copies:
        c.start()
    for c in loads:
        c.wait()
    for c in copies:
        c.wait()
    own_feat = feat[...]
    total = own_feat.astype(F32) + part[:, mine].astype(F32)
    for r in range(n_grp - 1):
        total = total + got[r].astype(F32)
    agg = (total / divisor[...]).astype(BF16)
    both = jnp.concatenate([own_feat.reshape(rows, fw), agg.reshape(rows, fw)], axis=1)
    back = jnp.zeros((rows, 2 * fw), F32)
    grads = []
    for j in range(n_grp):
        pre = jnp.dot(both, w_all[j], preferred_element_type=F32)
        sig = jax.nn.sigmoid(pre)
        out_all[j] = (pre * sig).astype(BF16).reshape(n_blk, own, hid)
        cot = cot_all[j].reshape(rows, hid).astype(F32)
        grad = (cot * sig * (1.0 + pre * (1.0 - sig))).astype(BF16)
        grads.append(grad)
        back = back + lax.dot_general(grad, w_all[j], TRANS_B, preferred_element_type=F32)
    down = (back[:, fw:].reshape(n_blk, own, fw) / divisor[...]).astype(BF16)
    sent[...] = down
    for c in last:
        c.start()
    scaled[:, mine] = down
    base[...] = back[:, :fw].reshape(n_blk, own, fw) + down.astype(F32)
    for j in range(n_grp):
        gw = lax.dot_general(both, grads[j], TRANS_A, preferred_element_type=F32).astype(BF16)
        for h in range(hid // 128):
            wgrad[j, h] = gw[:, 128 * h:128 * (h + 1)]
    for c in last:
        c.wait()


def backward_exchange(x, n_grp, table, scaled, cols, out_all, wgrad, places, pulled, out, grads,
                      stage, inbox, right_out, right_in, left_out, left_in, w_got, pieces, near_got, far_sent, far_got,
                      send, recv, rs, rr, ls, lr, o_s, o_r, w_s, w_r, a_s, a_r, b_s, b_r, c_s, c_r, d_s, d_r, loc):
    q, g = lax.axis_index("dom"), lax.axis_index("grp")
    layers, near, slots, own, fw = stage.shape
    n_blk = pulled.shape[0]
    cut = n_blk // 2
    half = layers // 2
    z, k = q // near, q % near
    out_rows, live, _, _ = tables(layers * near, slots, 0)
    barrier = pltpu.get_barrier_semaphore()
    signal_group(q, g, n_grp)(barrier)
    signal_ring(q, g, near, layers)(barrier)
    mine = pl.ds(pl.multiple_of(g * own, own), own)
    keep = pltpu.make_async_copy(out_all.at[g], out.at[:, mine], loc)
    keep.start()
    far, grad_far = [], []
    for r in range(1, n_grp):
        y = (g + r) % n_grp
        to = dict(device_id=(q, y), device_id_type=MESH)
        far.append(pltpu.make_async_remote_copy(
            src_ref=out_all.at[y], dst_ref=out.at[:, mine], send_sem=o_s.at[r - 1], recv_sem=o_r.at[r - 1], **to))
        grad_far.append(pltpu.make_async_remote_copy(
            src_ref=wgrad.at[y], dst_ref=w_got.at[r - 1], send_sem=w_s.at[r - 1], recv_sem=w_r.at[r - 1], **to))

    def to_near(d, r):
        to = (k + r) % near
        return pltpu.make_async_remote_copy(
            src_ref=stage.at[d, to], dst_ref=inbox.at[d, k], send_sem=send.at[d, r], recv_sem=recv.at[d, r],
            device_id=(z * near + to, g), device_id_type=MESH)

    def own_term(d):
        return pltpu.make_async_copy(stage.at[d, k], inbox.at[d, k], recv.at[d, 0])

    def products(d):
        base = (z + d) % layers * near

        @pl.loop(0, near)
        def _(r):
            to = (k + r) % near
            for s in range(slots):
                n = (base + to) * slots + s
                value = jnp.dot(cols[n], scaled[table[out_rows + n]], preferred_element_type=F32)
                stage[d, to, s] = jnp.where(s < table[live + base + to], value, 0.0).astype(BF16)

    def ship(d):
        own_term(d).start()
        each(1, near, functools.partial(to_near, d), start)

    def reduce(d):
        own_term(d).wait()
        each(1, near, functools.partial(to_near, d), wait)
        n = near * slots * own
        spot = places[(z + d) % layers]
        row = lax.broadcasted_iota(jnp.int32, (n_blk * own, 128), 0)
        hot = [jnp.where(row == spot[c:c + 1], 1.0, 0.0).astype(BF16) for c in range(pl.cdiv(n, 128))]
        hot = jnp.concatenate(hot, axis=1)[:, :n] if len(hot) > 1 else hot[0][:, :n]
        terms = inbox[d].reshape(n, fw)
        return jnp.dot(hot, terms, preferred_element_type=F32).reshape(n_blk, own, fw)

    def ring(i, to_right):
        count = cut if i == 0 else n_blk
        held, lands, s_sem, r_sem, step = (right_out, right_in, rs, rr, 1) if to_right else (left_out, left_in, ls, lr, layers - 1)
        return pltpu.make_async_remote_copy(
            src_ref=held.at[i, pl.ds(0, count)], dst_ref=lands.at[i, pl.ds(0, count)], send_sem=s_sem.at[i], recv_sem=r_sem.at[i],
            device_id=((z + step) % layers * near + k, g), device_id_type=MESH)

    def with_right(i, value):
        ring(i, True).wait()
        if i == 0:
            return jnp.concatenate([value[:cut] + right_in[0, :cut].astype(F32), value[cut:]], axis=0)
        return value + right_in[i].astype(F32)

    def with_left(i, value):
        ring(i, False).wait()
        if i == 0:
            return jnp.concatenate([value[:cut], value[cut:] + left_in[0, :cut].astype(F32)], axis=0)
        return value + left_in[i].astype(F32)

    def near_reduce(r):
        to = (k + r) % near
        return pltpu.make_async_remote_copy(
            src_ref=pieces.at[pl.ds(to * layers, layers)], dst_ref=near_got.at[r],
            send_sem=a_s.at[r], recv_sem=a_r.at[r], device_id=(z * near + to, g), device_id_type=MESH)

    def far_reduce(r):
        to = (z + r) % layers
        return pltpu.make_async_remote_copy(
            src_ref=far_sent.at[to], dst_ref=far_got.at[r],
            send_sem=b_s.at[r], recv_sem=b_r.at[r], device_id=(to * near + k, g), device_id_type=MESH)

    def far_gather(r):
        to = (z + r) % layers
        return pltpu.make_async_remote_copy(
            src_ref=grads.at[k * layers + z], dst_ref=grads.at[k * layers + z],
            send_sem=c_s.at[r], recv_sem=c_r.at[r], device_id=(to * near + k, g), device_id_type=MESH)

    def near_gather(r):
        to = (k + r) % near
        return pltpu.make_async_remote_copy(
            src_ref=grads.at[pl.ds(k * layers, layers)], dst_ref=grads.at[pl.ds(k * layers, layers)],
            send_sem=d_s.at[r], recv_sem=d_r.at[r], device_id=(z * near + to, g), device_id_type=MESH)

    def sum_grp():
        for c in grad_far:
            c.wait()
        halves = wgrad.shape[1]
        per = pieces.shape[0] // halves
        for h in range(halves):
            total = wgrad[g, h].astype(F32)
            for r in range(n_grp - 1):
                total = total + w_got[r, h].astype(F32)
            pieces[h * per:(h + 1) * per] = total.reshape(per, pieces.shape[1], 128)
        each(1, near, near_reduce, start)

    def sum_near():
        each(1, near, near_reduce, wait)
        total = pieces[pl.ds(k * layers, layers)]
        for r in range(1, near):
            total = total + near_got[r]
        far_sent[...] = total
        each(1, layers, far_reduce, start)

    def sum_far():
        each(1, layers, far_reduce, wait)
        total = far_sent[z]
        for r in range(1, layers):
            total = total + far_got[r]
        grads[k * layers + z] = total
        each(1, layers, far_gather, start)

    def spread():
        each(1, layers, far_gather, wait)
        each(1, near, near_gather, start)

    chain = [sum_grp, sum_near, sum_far, spread]
    products(half)
    pl.semaphore_wait(barrier, n_grp - 1 + near - 1 + layers - 1)
    for c in grad_far:
        c.start()
    ship(half)
    for c in far:
        c.start()
    for i in range(half):
        d = half - i
        if d > 1:
            for e in (d - 1, layers - d + 1):
                products(e)
                ship(e)
        else:
            products(0)
            ship(0)
        if i == 0:
            value = reduce(half)
            right_out[0, :cut] = value[:cut].astype(BF16)
            left_out[0, :cut] = value[cut:].astype(BF16)
        else:
            right_out[i] = with_right(i - 1, reduce(d)).astype(BF16)
            left_out[i] = with_left(i - 1, reduce(layers - d)).astype(BF16)
        ring(i, True).start()
        ring(i, False).start()
        if chain:
            chain.pop(0)()
    value = reduce(0)
    value = with_right(half - 1, value)
    pulled[...] = with_left(half - 1, value)
    while chain:
        chain.pop(0)()
    each(1, near, near_gather, wait)
    keep.wait()
    for c in far:
        c.wait()


def pull_kernel(table, scaled, cols, outer_sum, base, out_parts, part, out, acc, sem_o, *, n_out, where):
    keep = pltpu.make_async_copy(out_parts, out, sem_o)
    keep.start()
    in_rows, in_cols = where
    acc[...] = outer_sum[...] + base[...]

    @pl.loop(0, cols.shape[0] - n_out)
    def _(n):
        acc[table[in_cols + n]] += jnp.dot(cols[n_out + n], scaled[table[in_rows + n]], preferred_element_type=F32)

    part[...] = acc[...].astype(BF16)
    keep.wait()


def finish_kernel(n_grp, part, whole, s2, r2):
    q, g = lax.axis_index("dom"), lax.axis_index("grp")
    own = part.shape[1]
    mine = pl.ds(pl.multiple_of(g * own, own), own)
    barrier = pltpu.get_barrier_semaphore()
    signal_group(q, g, n_grp)(barrier)
    pl.semaphore_wait(barrier, n_grp - 1)
    last = []
    for r in range(1, n_grp):
        last.append(pltpu.make_async_remote_copy(
            src_ref=part, dst_ref=whole.at[:, mine], send_sem=s2.at[r - 1], recv_sem=r2.at[r - 1],
            device_id=(q, (g + r) % n_grp), device_id_type=MESH))
    for c in last:
        c.start()
    whole[:, mine] = part[...]
    for c in last:
        c.wait()


def params(collective=None, vmem=48):
    if collective is None:
        return pltpu.CompilerParams(vmem_limit_bytes=vmem << 20)
    return pltpu.CompilerParams(vmem_limit_bytes=vmem << 20, collective_id=collective, has_side_effects=True)


def shards(features, w_self, w_neigh, cotangent, inner_rows, inner_cols, inner_values, send_blocks, outer_rows, outer_values, live_count):
    blk = inner_values.shape[-1]
    nodes, fw = features.shape
    n_blk = nodes // blk
    parts, n_grp = lax.axis_size("dom"), lax.axis_size("grp")
    x = x_extent(parts)
    near = 2 * x
    layers = parts // near
    n_src = parts // n_grp
    slots = send_blocks.shape[-1]
    hid = w_self.shape[1]
    own = blk // n_grp
    n_in, n_out = inner_values.shape[1], outer_values.shape[1]
    n_all = n_in + n_out
    inner, outer = inner_values[0], outer_values[0]
    table = jnp.concatenate([send_blocks.reshape(-1), outer_rows[0], live_count[0], inner_rows[0], inner_cols[0]])
    dead = jnp.tile(jnp.arange(slots, dtype=jnp.int32), parts) >= jnp.repeat(live_count[0], slots)
    keys = jnp.concatenate([jnp.where(dead, n_blk, outer_rows[0]), inner_rows[0]])[None]
    places = (send_blocks.reshape(layers, near * slots, 1) * own + jnp.arange(own, dtype=jnp.int32)).reshape(layers, -1)
    places = jnp.pad(places, ((0, 0), (0, 8 * 128 - places.shape[1]))).reshape(layers, 8, 128)
    feat = features.reshape(n_blk, blk, fw)
    dma, sds = pltpu.SemaphoreType.DMA, jax.ShapeDtypeStruct
    vm = pltpu.VMEM
    block = (n_src, slots, blk, fw)
    mine = (n_blk, own, fw)
    y_sem = dma((n_grp - 1,))

    inc, cot_all, w_all, place_all, cols, divisor = pl.pallas_call(
        functools.partial(forward_exchange, x, n_src, n_grp),
        out_shape=(sds(block, BF16), sds((n_grp, n_blk, own, hid), BF16), sds((n_grp, 2 * fw, hid), BF16), sds((layers, 8, 128), jnp.int32),
                   sds((n_all, own, blk), BF16), sds(mine, F32)),
        in_specs=[SM, VM, HB, HB, HB, HB, HB, HB, HB],
        out_specs=(ANY, ANY, ANY, ANY, VM, VM),
        scratch_shapes=[vm((n_blk, blk, fw), BF16), vm(block, BF16), vm((n_all, blk, blk), BF16), vm((n_all, blk), F32),
                        dma((n_src,)), dma((n_src,)), y_sem, y_sem, dma((n_grp - 1, 2)), dma((n_grp - 1, 2)),
                        dma((layers,)), dma((layers,)), dma((7,))],
        compiler_params=params(0), name="forward_exchange",
    )(table, keys, places, feat, cotangent.reshape(n_blk, blk, hid), w_self, w_neigh, inner, outer)

    part = pl.pallas_call(
        functools.partial(aggregate_kernel, x, n_src, n_grp),
        out_shape=sds((n_blk, blk, fw), BF16),
        in_specs=[SM, HB, ANY, HB, HB],
        out_specs=VM,
        scratch_shapes=[vm((n_blk, blk, fw), BF16), vm((n_blk, blk, fw), F32), vm((n_in // n_grp, blk, blk), BF16),
                        vm((n_src, slots, blk, blk), BF16), vm(block, BF16), dma, dma, dma, dma],
        compiler_params=params(), name="aggregate",
    )(table, feat, inc, inner, outer)

    halves = hid // 128
    out_all, scaled, base, wgrad = pl.pallas_call(
        functools.partial(dense_kernel, n_grp),
        out_shape=(sds((n_grp, n_blk, own, hid), BF16), sds((n_blk, blk, fw), BF16), sds(mine, F32), sds((n_grp, halves, 2 * fw, 128), BF16)),
        in_specs=[VM, HB, VM, ANY, ANY],
        out_specs=(VM,) * 4,
        scratch_shapes=[vm(mine, BF16), vm((n_grp, n_blk, own, hid), BF16), vm((n_grp, 2 * fw, hid), BF16),
                        vm((n_grp - 1,) + mine, BF16), vm(mine, BF16), y_sem, y_sem, y_sem, y_sem, dma((3,))],
        compiler_params=params(1), name="dense",
    )(part, feat, divisor, cot_all, w_all)

    depth = halves * 2 * fw // parts
    half = layers // 2
    near_sem, far_sem = dma((near,)), dma((layers,))
    outer_sum, out_parts, grads = pl.pallas_call(
        functools.partial(backward_exchange, x, n_grp),
        out_shape=(sds(mine, F32), sds((n_blk, blk, hid), BF16), sds((parts, depth, 128), F32)),
        in_specs=[SM, VM, VM, ANY, VM, VM],
        out_specs=(VM, ANY, VM),
        scratch_shapes=[vm((layers, near, slots, own, fw), BF16), vm((layers, near, slots, own, fw), BF16)]
        + [vm((half,) + mine, BF16)] * 4
        + [vm((n_grp - 1, halves, 2 * fw, 128), BF16), vm((parts, depth, 128), F32), vm((near, layers, depth, 128), F32),
           vm((layers, depth, 128), F32), vm((layers, depth, 128), F32)]
        + [dma((layers, near))] * 2 + [dma((half,))] * 4 + [y_sem] * 4
        + [near_sem] * 2 + [far_sem] * 4 + [near_sem] * 2 + [dma],
        compiler_params=params(2), name="backward_exchange",
    )(table, scaled, cols, out_all, wgrad, place_all)

    _, _, in_rows, in_cols = tables(parts, slots, n_in)
    pulled, layer_out = pl.pallas_call(
        functools.partial(pull_kernel, n_out=n_out, where=(in_rows, in_cols)),
        out_shape=(sds(mine, BF16), sds((n_blk, blk, hid), BF16)),
        in_specs=[SM, VM, VM, VM, VM, ANY],
        out_specs=(VM, ANY),
        scratch_shapes=[vm(mine, F32), dma],
        compiler_params=params(), name="pull",
    )(table, scaled, cols, outer_sum, base, out_parts)

    whole = pl.pallas_call(
        functools.partial(finish_kernel, n_grp),
        out_shape=sds((n_blk, blk, fw), BF16),
        in_specs=[VM],
        out_specs=VM,
        scratch_shapes=[y_sem, y_sem],
        compiler_params=params(3), name="finish",
    )(pulled)
    grads = grads.reshape(halves, 2 * fw, 128)
    grads = jnp.concatenate([grads[h] for h in range(halves)], axis=1)
    return layer_out.reshape(nodes, hid), whole.astype(F32).reshape(nodes, fw), grads[:fw], grads[fw:]


def solution(mesh):
    placed = (
        P("dom", None),
        P(None, "grp"),
        P(None, "grp"),
        P("dom", "grp"),
        P("dom", None),
        P("dom", None),
        P("dom", None, None, None),
        P("dom", None, None),
        P("dom", None),
        P("dom", None, None, None),
        P("dom", None),
    )
    return jax.shard_map(
        shards,
        mesh=mesh,
        in_specs=placed,
        out_specs=(P("dom", "grp"), P("dom", None), P(None, "grp"), P(None, "grp")),
        check_vma=False,
    )
```

time: 322 us -> 151 us (0.47)
  waiting for transfers between devices: 150 us -> 0 us
  between operations: 14.2 us -> 0.78 us
  local copies, waits for them, and re-layouts: 12.6 us -> 6.24 us
  Pallas kernels: 145 us -> 139 us
  other arithmetic: 0 us -> 4.63 us
    psum x1 -> x0, waiting for transfers between devices: 122 us -> none  [shards(): lax.psum(lax.psum_scatter(wgrad, 'grp', scatter_dimension=0, tiled=False)...]
    reduce_scatter x1 -> x0, waiting for transfers between devices: 27.2 us -> none  [shards(): lax.psum_scatter(wgrad, 'grp', scatter_dimension=0, tiled=False)]
    pallas_call x1, Pallas kernels: 43.8 us -> 50.3 us  [shards(): pl.pallas_call(functools.partial(forward_exchange, x, n_src, n_grp), out_...]
    unnamed x33 -> x17, local copies, waits for them, and re-layouts: 10.9 us -> 4.74 us
    pallas_call x1, Pallas kernels: 27.3 us -> 22.3 us  [shards(): pl.pallas_call(functools.partial(dense_kernel, n_grp), out_shape=(sds((n_...]
    pallas_call x1, Pallas kernels: 15.1 us -> 10.2 us  [shards(): pl.pallas_call(functools.partial(finish_kernel, n_grp), out_shape=sds((n_...]
    pallas_call x2, Pallas kernels: 52 us -> 48.1 us  [the longest x1 38.9 us: shards(): pl.pallas_call(functools.partial(backward_exchange, x, n_grp), out_shape=...]
  transfers between devices with their start and end apart: 2 -> 0, of which waited for: 2 -> 0; matrix products, arithmetic and copies ran while one was open for 0% -> 0% of each run, Pallas kernels for 21% -> 0%
where the time goes in v3:
time: 151 us; the launch traced here: 150 us
  Pallas kernels  139 us (92%)
  local copies, waits for them, and re-layouts  6.24 us (4%)
  other arithmetic  4.63 us (3%)
    pallas_call x1, Pallas kernels, shards(): pl.pallas_call(functools.partial(forward_exchange, x, n_src, n_grp), out_...  50.3 us
    pallas_call x1, Pallas kernels, shards(): pl.pallas_call(functools.partial(backward_exchange, x, n_grp), out_shape=...  38.9 us
    pallas_call x1, Pallas kernels, shards(): pl.pallas_call(functools.partial(dense_kernel, n_grp), out_shape=(sds((n_...  22.3 us
    pallas_call x1, Pallas kernels, shards(): pl.pallas_call(functools.partial(finish_kernel, n_grp), out_shape=sds((n_...  10.2 us
    pallas_call x1, Pallas kernels, shards(): pl.pallas_call(functools.partial(pull_kernel, n_out=n_out, where=(in_rows...  9.27 us
    pallas_call x1, Pallas kernels, shards(): pl.pallas_call(functools.partial(aggregate_kernel, x, n_src, n_grp), out_...  7.7 us
    unnamed x17, local copies, waits for them, and re-layouts  4.74 us

profile of v3, /device:TPU:1, one launch (start us, length us, event | category | flops | bytes accessed | tf_op | source)
XLA Modules:
  0.0 150.2 jit_solution(4642688214840132047)
XLA Ops:
  0.6 0.7 broadcast_multiply_fusion
  1.3 0.7 iota_compare_fusion
  2.1 0.1 ge.7
  2.2 0.7 broadcast_select_fusion
  2.9 0.7 pad_add_fusion
  3.7 0.1 copy.16
  3.8 0.1 mul.16
  3.9 0.8 copy.15
  4.6 0.1 reshape.49
  4.8 0.8 concatenate.9.table
  5.6 0.1 add.22
  5.6 0.1 add.23
  5.8 1.0 copy-done.2
  6.8 1.2 copy-done.4
  8.0 0.8 copy-done.5
  8.9 0.8 copy-done.6
  9.7 50.3 %forward_exchange.1 = (bf16[16,3,128,128]{3,2,1,0:T(8,128)(2,1)S(1)}, bf16[4,16,32,256]{3,2,1,0:T(8,128)(2,1)S(1)}, bf16[4,256,256]{2,1,0:T(8,128)(2,1)S(1)}, s3...) custom-call(s32[576]{0:T(1024)S(1)} %concatenate.9.table, ...), custom_call_target="tpu_custom_call" | custom-call | tf_op jit(solution)/shard_map/forward_exchange/pallas_call | solution.py:581
  60.0 7.7 %aggregate.1.part = bf16[16,128,128]{2,1,0:T(8,128)(2,1)S(1)} custom-call(s32[576]{0:T(1024)S(1)} %concatenate.9.table, bf16[16,128,128]{2,1,0:T(8,128)(2,1)S(1)} %bitcast.25, bf16[16,3,128,128]{3,2,1,0:T(8,128)(2,1)S(1)} %get-tuple-element.19.inc, bf16[64,128,128]{2,1,0:T(8,128)(2,1)S(1)} %bitcast.23, bf16[192,128,128]{2,1,0:T(8,128)(2,1)} %bitcast.31), custom_call_target="tpu_custom_call" | custom-call | tf_op jit(solution)/shard_map/aggregate/pallas_call | solution.py:593
  67.8 22.3 %dense.1 = (bf16[4,16,32,256]{3,2,1,0:T(8,128)(2,1)S(1)}, bf16[16,128,128]{2,1,0:T(8,128)(2,1)S(1)}, f32[16,32,128]{2,1,0:T(8,128)S(1)}, bf16[4,2,256,128]{3,2,1,0:T(8,128)(2,1)S(1)}) custom-call(bf16[16,128,128]{2,1,0:T(8,128)(2,1)S(1)} %aggregate.1.part, bf16[16,128,128]{2,1,0:T(8,128)(2,1)S(1)} %bitcast.26, f32[16,32,128]{2,1,0:T(8,128)S(1)} %get-tuple-element.20.divisor, ...), custom_call_target="tpu_custom_call" | custom-call | tf_op jit(solution)/shard_map/dense/pallas_call | solution.py:604
  90.1 38.9 %backward_exchange.1 = (f32[16,32,128]{2,1,0:T(8,128)S(1)}, bf16[16,128,256]{2,1,0:T(8,128)(2,1)S(1)}, f32[64,8,128]{2,1,0:T(8,128)S(1)}) custom-call(s32[576]{0:T(1024)S(1)} %concatenate.9.table, bf16[16,128,128]{2,1,0:T(8,128)(2,1)S(1)} %get-tuple-element.23.scaled, bf16[256,32,128]{2,1,0:T(8,128)(2,1)S(1)} %copy-done.1, ...), custom_call_target="tpu_custom_call" | custom-call | tf_op jit(solution)/shard_map/backward_exchange/pallas_call | solution.py:617
  129.0 9.3 %pull.1 = (bf16[16,32,128]{2,1,0:T(8,128)(2,1)S(1)}, bf16[16,128,256]{2,1,0:T(8,128)(2,1)}) custom-call(s32[576]{0:T(1024)S(1)} %concatenate.9.table, bf16[16,128,128]{2,1,0:T(8,128)(2,1)S(1)} %get-tuple-element.23.scaled, bf16[256,32,128]{2,1,0:T(8,128)(2,1)S(1)} %copy-done.1, f32[16,32,128]{2,1,0:T(8,128)S(1)} %get-tuple-element.28.outer_sum, ...), custom_call_target="tpu_custom_call" | custom-call | tf_op jit(solution)/shard_map/pull/pallas_call | solution.py:632
  138.3 0.7 pad_maximum_fusion
  139.0 10.2 %finish.1 = bf16[16,128,128]{2,1,0:T(8,128)(2,1)S(1)} custom-call(bf16[16,32,128]{2,1,0:T(8,128)(2,1)S(1)} %get-tuple-element.32.part), custom_call_target="tpu_custom_call" | custom-call | tf_op jit(solution)/shard_map/finish/pallas_call | solution.py:641
  149.1 1.1 bitcast_convert_fusion
  (16 shorter events, 0.1 us)
Async XLA Ops:
  5.8 1.0 copy-start.2
  6.8 1.2 copy-start.4
  8.0 0.8 copy-start.5
  8.9 0.8 copy-start.6
  9.7 50.3 %copy-start = (bf16[1,64,128,128]{3,2,1,0:T(8,128)(2,1)S(1)}, bf16[1,64,128,128]{3,2,1,0:T(8,128)(2,1)}, u32[]{:S(2)}) copy-start(bf16[1,64,128,128]{3,2,1,0:T(8,128)(2,1)} %param.17) | copy-start | bytes 6291460
  60.0 7.7 %copy-start.3 = (bf16[2048,128]{1,0:T(8,128)(2,1)S(1)}, bf16[2048,128]{1,0:T(8,128)(2,1)}, u32[]{:S(2)}) copy-start(bf16[2048,128]{1,0:T(8,128)(2,1)} %param.11) | copy-start | bytes 1572868
  67.8 22.3 %copy-start.1 = (bf16[256,32,128]{2,1,0:T(8,128)(2,1)S(1)}, bf16[256,32,128]{2,1,0:T(8,128)(2,1)}, u32[]{:S(2)}) copy-start(bf16[256,32,128]{2,1,0:T(8,128)(2,1)} %get-tuple-element.24.cols) | copy-start | bytes 6291460

commit v4 on v3

--- a/solution.py
+++ b/solution.py
@@ -97,16 +97,16 @@
     c.wait()
 
 
-def forward_exchange(x, n_src, n_grp, table, keys, places, features, cot, w_self, w_neigh, inner, outer,
-                     inc, cot_all, w_all, place_all, cols, divisor,
-                     feat, stage, blocks, row_sums, send, recv, cot_s, cot_r, w_s, w_r, p_s, p_r, loc):
+def forward_exchange(x, n_src, n_grp, table, rows_out, rows_in, live, features, cot, w_self, w_neigh, inner, outer,
+                     inc, cot_all, w_all, place_all, cols_out, divisor_out,
+                     feat, stage, blocks, row_sums, places, key_out, key_in, key_live, cols, divisor, send, recv, cot_s, cot_r, w_s, w_r, p_s, p_r, loc):
     q, g = lax.axis_index("dom"), lax.axis_index("grp")
     slots = stage.shape[1]
     own = cot_all.shape[2]
     fw = w_self.shape[0]
     n_blk, blk, _ = feat.shape
     near = 2 * x
-    layers = places.shape[0]
+    layers = place_all.shape[0]
     z, k = q // near, q % near
     slot = plane_slot(q, x)
     n_out, n_in = outer.shape[0], inner.shape[0]
@@ -126,6 +126,11 @@
         pltpu.make_async_copy(w_self, w_all.at[g, pl.ds(0, fw)], loc.at[1]),
         pltpu.make_async_copy(w_neigh, w_all.at[g, pl.ds(fw, fw)], loc.at[2]),
         pltpu.make_async_copy(places.at[z], place_all.at[z], loc.at[6]),
+    ]
+    small = [
+        pltpu.make_async_copy(rows_out, key_out, loc.at[7]),
+        pltpu.make_async_copy(rows_in, key_in, loc.at[8]),
+        pltpu.make_async_copy(live, key_live, loc.at[9]),
     ]
     loads = [
         pltpu.make_async_copy(outer, blocks.at[pl.ds(0, n_out)], loc.at[4]),
@@ -189,8 +194,23 @@
         d = (slot + i) % n_src
         remote(d, fill(d)).start()
 
-    for c in far + local + loads:
+    for c in far + local[:3] + loads + small:
         c.start()
+
+    per = 128 // own
+    lane = lax.broadcasted_iota(jnp.int32, (1, 128), 1)
+
+    @pl.loop(0, layers)
+    def _(t):
+        for c in range(pl.cdiv(near * slots, per)):
+            spot = lane
+            for u in range(per):
+                if c * per + u < near * slots:
+                    target = table[t * (near * slots) + c * per + u]
+                    spot = jnp.where(lane // own == u, lane + (target - u) * own, spot)
+            places[t, c:c + 1, :] = spot
+
+    local[3].start()
     each(1, layers, place, start)
 
     row = lax.broadcasted_iota(jnp.int32, (own + 16, blk), 0)
@@ -199,21 +219,35 @@
     for c in loads:
         c.wait()
 
-    @pl.loop(0, (n_out + n_in) // 4)
+    @pl.loop(0, (n_out + n_in) // 8)
     def _(m):
-        for u in range(4):
-            n = m * 4 + u
-            got = lax.dot_general(pick, blocks[n], TRANS_B, preferred_element_type=F32)
-            cols[n] = got[:own].astype(BF16)
-            row_sums[pl.ds(n, 1), :] = got[own:own + 1]
-
-    hits = jnp.where(lax.broadcasted_iota(jnp.int32, (n_blk, n_out + n_in), 0) == keys[...], 1.0, 0.0)
+        got = [lax.dot_general(pick, blocks[m * 8 + u], TRANS_B, preferred_element_type=F32) for u in range(8)]
+        for u in range(8):
+            cols[m * 8 + u] = got[u][:own].astype(BF16)
+        row_sums[pl.ds(pl.multiple_of(m * 8, 8), 8), :] = jnp.concatenate([v[own:own + 1] for v in got], axis=0)
+
+    keep = pltpu.make_async_copy(cols, cols_out, loc.at[10])
+    keep.start()
+    for c in small:
+        c.wait()
+    n_part = key_live.shape[1]
+    first = slots * lax.broadcasted_iota(jnp.int32, (n_part, n_out), 0)
+    at = lax.broadcasted_iota(jnp.int32, (n_part, n_out), 1) - first
+    spread = jnp.where((at >= 0) & (at < slots), 1.0, 0.0)
+    limit = jnp.dot(key_live[...].astype(F32), spread, precision=lax.Precision.HIGHEST, preferred_element_type=F32)
+    index = jnp.sum(jnp.where((at >= 0) & (at < slots), at, 0), axis=0, keepdims=True)
+    key = jnp.concatenate([jnp.where(index.astype(F32) < limit, key_out[...], n_blk), key_in[...]], axis=1)
+    hits = jnp.where(lax.broadcasted_iota(jnp.int32, (n_blk, n_out + n_in), 0) == key, 1.0, 0.0)
     degree = 1.0 + jnp.dot(hits, row_sums[...], precision=lax.Precision.HIGHEST, preferred_element_type=F32)
     sel = (lax.broadcasted_iota(jnp.int32, (own, blk), 1) == lax.broadcasted_iota(jnp.int32, (own, blk), 0) + g * own)
     for b in range(n_blk):
         column = jnp.sum(jnp.where(sel, degree[b:b + 1], 0.0), axis=1, keepdims=True)
         divisor[b] = jnp.broadcast_to(column, (own, fw))
 
+    keep_too = pltpu.make_async_copy(divisor, divisor_out, loc.at[11])
+    keep_too.start()
+    keep.wait()
+    keep_too.wait()
     for c in local:
         c.wait()
     for c in far:
@@ -258,10 +292,11 @@
     load_f.wait()
     load_in.wait()
 
-    @pl.loop(0, n_in)
-    def _(n):
-        acc[table[in_rows + g * n_in + n]] += jnp.dot(
-            a_in[n], feat[table[in_cols + g * n_in + n]], preferred_element_type=F32)
+    @pl.loop(0, n_in // 2)
+    def _(m):
+        value = [jnp.dot(a_in[m * 2 + u], feat[table[in_cols + g * n_in + m * 2 + u]], preferred_element_type=F32) for u in range(2)]
+        for u in range(2):
+            acc[table[in_rows + g * n_in + m * 2 + u]] += value[u]
 
     load_x.wait()
     pltpu.make_async_copy(a_out, a_out, sem_out).wait()
@@ -269,10 +304,11 @@
     @pl.loop(0, n_src)
     def _(i):
         peer = plane_peer(i, q, g, x)
+        value = [jnp.dot(a_out[i, s], x_in[i, s], preferred_element_type=F32) for s in range(slots)]
         for s in range(slots):
             @pl.when(s < table[live + peer])
-            def _():
-                acc[table[out_rows + peer * slots + s]] += jnp.dot(a_out[i, s], x_in[i, s], preferred_element_type=F32)
+            def _(s=s):
+                acc[table[out_rows + peer * slots + s]] += value[s]
 
     part[...] = acc[...].astype(BF16)
 
@@ -375,13 +411,19 @@
     def products(d):
         base = (z + d) % layers * near
 
-        @pl.loop(0, near)
+        group = max(1, near // 2)
+
+        @pl.loop(0, near // group)
         def _(r):
-            to = (k + r) % near
-            for s in range(slots):
-                n = (base + to) * slots + s
-                value = jnp.dot(cols[n], scaled[table[out_rows + n]], preferred_element_type=F32)
-                stage[d, to, s] = jnp.where(s < table[live + base + to], value, 0.0).astype(BF16)
+            value = []
+            for u in range(group):
+                for s in range(slots):
+                    n = (base + r * group + u) * slots + s
+                    value.append(jnp.dot(cols[n], scaled[table[out_rows + n]], preferred_element_type=F32))
+            for u in range(group):
+                to = r * group + u
+                for s in range(slots):
+                    stage[d, to, s] = jnp.where(s < table[live + base + to], value[u * slots + s], 0.0).astype(BF16)
 
     def ship(d):
         own_term(d).start()
@@ -518,9 +560,11 @@
     in_rows, in_cols = where
     acc[...] = outer_sum[...] + base[...]
 
-    @pl.loop(0, cols.shape[0] - n_out)
-    def _(n):
-        acc[table[in_cols + n]] += jnp.dot(cols[n_out + n], scaled[table[in_rows + n]], preferred_element_type=F32)
+    @pl.loop(0, (cols.shape[0] - n_out) // 8)
+    def _(m):
+        value = [jnp.dot(cols[n_out + m * 8 + u], scaled[table[in_rows + m * 8 + u]], preferred_element_type=F32) for u in range(8)]
+        for u in range(8):
+            acc[table[in_cols + m * 8 + u]] += value[u]
 
     part[...] = acc[...].astype(BF16)
     keep.wait()
@@ -567,10 +611,6 @@
     n_all = n_in + n_out
     inner, outer = inner_values[0], outer_values[0]
     table = jnp.concatenate([send_blocks.reshape(-1), outer_rows[0], live_count[0], inner_rows[0], inner_cols[0]])
-    dead = jnp.tile(jnp.arange(slots, dtype=jnp.int32), parts) >= jnp.repeat(live_count[0], slots)
-    keys = jnp.concatenate([jnp.where(dead, n_blk, outer_rows[0]), inner_rows[0]])[None]
-    places = (send_blocks.reshape(layers, near * slots, 1) * own + jnp.arange(own, dtype=jnp.int32)).reshape(layers, -1)
-    places = jnp.pad(places, ((0, 0), (0, 8 * 128 - places.shape[1]))).reshape(layers, 8, 128)
     feat = features.reshape(n_blk, blk, fw)
     dma, sds = pltpu.SemaphoreType.DMA, jax.ShapeDtypeStruct
     vm = pltpu.VMEM
@@ -582,13 +622,14 @@
         functools.partial(forward_exchange, x, n_src, n_grp),
         out_shape=(sds(block, BF16), sds((n_grp, n_blk, own, hid), BF16), sds((n_grp, 2 * fw, hid), BF16), sds((layers, 8, 128), jnp.int32),
                    sds((n_all, own, blk), BF16), sds(mine, F32)),
-        in_specs=[SM, VM, HB, HB, HB, HB, HB, HB, HB],
-        out_specs=(ANY, ANY, ANY, ANY, VM, VM),
+        in_specs=[SM] + [HB] * 9,
+        out_specs=(ANY,) * 6,
         scratch_shapes=[vm((n_blk, blk, fw), BF16), vm(block, BF16), vm((n_all, blk, blk), BF16), vm((n_all, blk), F32),
+                        vm((layers, 8, 128), jnp.int32), vm((1, n_out), jnp.int32), vm((1, n_in), jnp.int32), vm((1, parts), jnp.int32), vm((n_all, own, blk), BF16), vm(mine, F32),
                         dma((n_src,)), dma((n_src,)), y_sem, y_sem, dma((n_grp - 1, 2)), dma((n_grp - 1, 2)),
-                        dma((layers,)), dma((layers,)), dma((7,))],
-        compiler_params=params(0), name="forward_exchange",
-    )(table, keys, places, feat, cotangent.reshape(n_blk, blk, hid), w_self, w_neigh, inner, outer)
+                        dma((layers,)), dma((layers,)), dma((12,))],
+        compiler_params=params(0, 62), name="forward_exchange",
+    )(table, outer_rows, inner_rows, live_count, feat, cotangent.reshape(n_blk, blk, hid), w_self, w_neigh, inner, outer)
 
     part = pl.pallas_call(
         functools.partial(aggregate_kernel, x, n_src, n_grp),
@@ -597,7 +638,7 @@
         out_specs=VM,
         scratch_shapes=[vm((n_blk, blk, fw), BF16), vm((n_blk, blk, fw), F32), vm((n_in // n_grp, blk, blk), BF16),
                         vm((n_src, slots, blk, blk), BF16), vm(block, BF16), dma, dma, dma, dma],
-        compiler_params=params(), name="aggregate",
+        compiler_params=params(None, 62), name="aggregate",
     )(table, feat, inc, inner, outer)
 
     halves = hid // 128

time: 151 us -> 137 us (0.907)
  Pallas kernels: 139 us -> 130 us
  other arithmetic: 4.63 us -> 1.79 us
  local copies, waits for them, and re-layouts: 6.24 us -> 4.4 us
    pallas_call x1, Pallas kernels: 9.27 us -> 2.15 us  [shards(): pl.pallas_call(functools.partial(pull_kernel, n_out=n_out, where=(in_rows...]
    unnamed x17, local copies, waits for them, and re-layouts: 4.74 us -> 2.87 us
where the time goes in v4:
time: 137 us
  Pallas kernels  130 us (95%)
  local copies, waits for them, and re-layouts  4.4 us (3%)
  other arithmetic  1.79 us (1%)
    pallas_call x1, Pallas kernels, shards(): pl.pallas_call(functools.partial(forward_exchange, x, n_src, n_grp), out_...  48.9 us
    pallas_call x1, Pallas kernels, shards(): pl.pallas_call(functools.partial(backward_exchange, x, n_grp), out_shape=...  39.1 us
    pallas_call x1, Pallas kernels, shards(): pl.pallas_call(functools.partial(dense_kernel, n_grp), out_shape=(sds((n_...  21.5 us
    pallas_call x1, Pallas kernels, shards(): pl.pallas_call(functools.partial(finish_kernel, n_grp), out_shape=sds((n_...  10.3 us
    pallas_call x1, Pallas kernels, shards(): pl.pallas_call(functools.partial(aggregate_kernel, x, n_src, n_grp), out_...  7.61 us
    unnamed x17, local copies, waits for them, and re-layouts  2.87 us

profile of v4, /device:TPU:1, one launch (start us, length us, event | category | flops | bytes accessed | tf_op | source)
XLA Modules:
  0.0 136.5 jit_solution(2519589918287819987)
XLA Ops:
  0.6 0.8 copy.15
  1.4 0.1 reshape.31
  1.5 1.4 %concatenate.6.table = s32[576]{0:T(1024)} concatenate(s32[192]{0:T(256)S(1)} %reshape.31, s32[192]{0:T(256)} %bitcast.24, s32[64]{0:T(128)} %bitcast.25, s32[64]{0:T(128)} %bitcast.26, s32[64]{0:T(128)} %bitcast.27), dimensions={0} | concatenate | bytes 4608 | tf_op jit(solution)/shard_map/concatenate | solution.py:613
  2.9 48.9 %forward_exchange.1 = (bf16[16,3,128,128]{3,2,1,0:T(8,128)(2,1)}, bf16[4,16,32,256]{3,2,1,0:T(8,128)(2,1)}, bf16[4,256,256]{2,1,0:T(8,128)(2,1)}, s32[8,8,128]{2...) custom-call(s32[576]{0:T(1024)} %concatenate.6.table, s32[1,192]{1,0:T(1,128)} %rows_out.1, ...), custom_call_target="tpu_custom_call" | custom-call | tf_op jit(solution)/shard_map/forward_exchange/pallas_call | solution.py:621
  51.8 0.0 copy-start.1
  51.8 0.0 copy-start.3
  51.8 0.0 copy-start.5
  51.8 7.6 %aggregate.1.part = bf16[16,128,128]{2,1,0:T(8,128)(2,1)} custom-call(s32[576]{0:T(1024)} %concatenate.6.table, bf16[16,128,128]{2,1,0:T(8,128)(2,1)} %bitcast.17, bf16[16,3,128,128]{3,2,1,0:T(8,128)(2,1)} %get-tuple-element.19.inc, bf16[64,128,128]{2,1,0:T(8,128)(2,1)} %bitcast.22, bf16[192,128,128]{2,1,0:T(8,128)(2,1)} %bitcast.20), custom_call_target="tpu_custom_call" | custom-call | tf_op jit(solution)/shard_map/aggregate/pallas_call | solution.py:634
  59.4 0.0 copy-done.1
  59.5 0.0 copy-done.3
  59.5 0.0 copy-done.5
  59.5 0.0 copy-start.2
  59.5 1.0 copy-done.2
  60.5 0.0 copy-start.4
  60.5 1.0 copy-done.4
  61.6 21.5 %dense.1 = (bf16[4,16,32,256]{3,2,1,0:T(8,128)(2,1)S(1)}, bf16[16,128,128]{2,1,0:T(8,128)(2,1)S(1)}, f32[16,32,128]{2,1,0:T(8,128)S(1)}, bf16[4,2,256,128]{3,2,1,0:T(8,128)(2,1)S(1)}) custom-call(bf16[16,128,128]{2,1,0:T(8,128)(2,1)S(1)} %copy-done.2, bf16[16,128,128]{2,1,0:T(8,128)(2,1)S(1)} %bitcast.18, f32[16,32,128]{2,1,0:T(8,128)S(1)} %copy-done.5, ...), custom_call_target="tpu_custom_call" | custom-call | tf_op jit(solution)/shard_map/dense/pallas_call | solution.py:645
  83.0 0.0 copy-done
  83.1 0.0 copy-done.6
  83.1 0.0 copy-done.7
  83.1 39.1 %backward_exchange.1 = (f32[16,32,128]{2,1,0:T(8,128)S(1)}, bf16[16,128,256]{2,1,0:T(8,128)(2,1)S(1)}, f32[64,8,128]{2,1,0:T(8,128)S(1)}) custom-call(s32[576]{0:T(1024)S(1)} %copy-done.6, bf16[16,128,128]{2,1,0:T(8,128)(2,1)S(1)} %get-tuple-element.23.scaled, bf16[256,32,128]{2,1,0:T(8,128)(2,1)S(1)} %copy-done, ...), custom_call_target="tpu_custom_call" | custom-call | tf_op jit(solution)/shard_map/backward_exchange/pallas_call | solution.py:658
  122.2 2.2 %pull.1 = (bf16[16,32,128]{2,1,0:T(8,128)(2,1)S(1)}, bf16[16,128,256]{2,1,0:T(8,128)(2,1)}) custom-call(s32[576]{0:T(1024)S(1)} %copy-done.6, bf16[16,128,128]{2,1,0:T(8,128)(2,1)S(1)} %get-tuple-element.23.scaled, bf16[256,32,128]{2,1,0:T(8,128)(2,1)S(1)} %copy-done, f32[16,32,128]{2,1,0:T(8,128)S(1)} %get-tuple-element.28.outer_sum, ...), custom_call_target="tpu_custom_call" | custom-call | tf_op jit(solution)/shard_map/pull/pallas_call | solution.py:673
  124.4 0.7 pad_maximum_fusion
  125.1 10.3 %finish.1 = bf16[16,128,128]{2,1,0:T(8,128)(2,1)S(1)} custom-call(bf16[16,32,128]{2,1,0:T(8,128)(2,1)S(1)} %get-tuple-element.32.part), custom_call_target="tpu_custom_call" | custom-call | tf_op jit(solution)/shard_map/finish/pallas_call | solution.py:682
  135.4 1.1 bitcast_convert_fusion
  (4 shorter events, 0.0 us)
Async XLA Ops:
  51.8 7.7 %copy-start.1 = (bf16[2048,128]{1,0:T(8,128)(2,1)S(1)}, bf16[2048,128]{1,0:T(8,128)(2,1)}, u32[]{:S(2)}) copy-start(bf16[2048,128]{1,0:T(8,128)(2,1)} %param.11) | copy-start | bytes 1572868
  51.8 7.7 %copy-start.3 = (bf16[4,16,32,256]{3,2,1,0:T(8,128)(2,1)S(1)}, bf16[4,16,32,256]{3,2,1,0:T(8,128)(2,1)}, u32[]{:S(2)}) copy-start(bf16[4,16,32,256]{3,2,1,0:T(8,128)(2,1)} %get-tuple-element.21.cots) | copy-start | bytes 3145732
  51.8 7.7 %copy-start.5 = (f32[16,32,128]{2,1,0:T(8,128)S(1)}, f32[16,32,128]{2,1,0:T(8,128)}, u32[]{:S(2)}) copy-start(f32[16,32,128]{2,1,0:T(8,128)} %get-tuple-element.20.divisor) | copy-start | bytes 786436
  59.5 1.0 copy-start.2
  60.5 1.0 copy-start.4
  61.6 21.5 %copy-start = (bf16[256,32,128]{2,1,0:T(8,128)(2,1)S(1)}, bf16[256,32,128]{2,1,0:T(8,128)(2,1)}, u32[]{:S(2)}) copy-start(bf16[256,32,128]{2,1,0:T(8,128)(2,1)} %get-tuple-element.24.cols) | copy-start | bytes 6291460
  61.6 21.5 %copy-start.6 = (s32[576]{0:T(1024)S(1)}, s32[576]{0:T(1024)}, u32[]{:S(2)}) copy-start(s32[576]{0:T(1024)} %concatenate.6.table) | copy-start | bytes 6916
  61.6 21.5 %copy-start.7 = (s32[8,8,128]{2,1,0:T(8,128)S(1)}, s32[8,8,128]{2,1,0:T(8,128)}, u32[]{:S(2)}) copy-start(s32[8,8,128]{2,1,0:T(8,128)} %get-tuple-element.27.places) | copy-start | bytes 98308

commit v5 on v4

--- a/solution.py
+++ b/solution.py
@@ -374,26 +374,29 @@
         c.wait()
 
 
-def backward_exchange(x, n_grp, table, scaled, cols, out_all, wgrad, places, pulled, out, grads,
-                      stage, inbox, right_out, right_in, left_out, left_in, w_got, pieces, near_got, far_sent, far_got,
-                      send, recv, rs, rr, ls, lr, o_s, o_r, w_s, w_r, a_s, a_r, b_s, b_r, c_s, c_r, d_s, d_r, loc):
+def backward_exchange(x, n_grp, n_in, table, scaled, cols, out_all, wgrad, places, base_sum, whole, out, grads,
+                      inner_terms, inner_sum, sent, stage, inbox, right_out, right_in, left_out, left_in, w_got, pieces, near_got, far_sent, far_got,
+                      send, recv, rs, rr, ls, lr, o_s, o_r, w_s, w_r, a_s, a_r, b_s, b_r, c_s, c_r, d_s, d_r, e_s, e_r, loc):
     q, g = lax.axis_index("dom"), lax.axis_index("grp")
     layers, near, slots, own, fw = stage.shape
-    n_blk = pulled.shape[0]
+    n_blk = whole.shape[0]
     cut = n_blk // 2
     half = layers // 2
     z, k = q // near, q % near
-    out_rows, live, _, _ = tables(layers * near, slots, 0)
+    out_rows, live, in_rows, in_cols = tables(layers * near, slots, n_in)
+    n_out = layers * near * slots
     barrier = pltpu.get_barrier_semaphore()
     signal_group(q, g, n_grp)(barrier)
     signal_ring(q, g, near, layers)(barrier)
     mine = pl.ds(pl.multiple_of(g * own, own), own)
     keep = pltpu.make_async_copy(out_all.at[g], out.at[:, mine], loc)
     keep.start()
-    far, grad_far = [], []
+    far, grad_far, last = [], [], []
     for r in range(1, n_grp):
         y = (g + r) % n_grp
         to = dict(device_id=(q, y), device_id_type=MESH)
+        last.append(pltpu.make_async_remote_copy(
+            src_ref=sent, dst_ref=whole.at[:, mine], send_sem=e_s.at[r - 1], recv_sem=e_r.at[r - 1], **to))
         far.append(pltpu.make_async_remote_copy(
             src_ref=out_all.at[y], dst_ref=out.at[:, mine], send_sem=o_s.at[r - 1], recv_sem=o_r.at[r - 1], **to))
         grad_far.append(pltpu.make_async_remote_copy(
@@ -515,7 +518,41 @@
         each(1, layers, far_gather, wait)
         each(1, near, near_gather, start)
 
-    chain = [sum_grp, sum_near, sum_far, spread]
+    def inner():
+        per = 128 // own
+        step = 4 * per
+
+        @pl.loop(0, n_in // 8)
+        def _(m):
+            value = [jnp.dot(cols[n_out + m * 8 + u], scaled[table[in_rows + m * 8 + u]], preferred_element_type=F32) for u in range(8)]
+            for u in range(8):
+                inner_terms[m * 8 + u] = value[u].astype(BF16)
+
+        lane = lax.broadcasted_iota(jnp.int32, (1, 128), 1)
+        row = lax.broadcasted_iota(jnp.int32, (n_blk * own, 128), 0)
+        inner_sum[...] = base_sum[...]
+
+        def add(m, count):
+            hot = []
+            for c in range(count):
+                spot = lane
+                for u in range(per):
+                    target = table[in_cols + m * step + c * per + u]
+                    spot = jnp.where(lane // own == u, lane + (target - u) * own, spot)
+                hot.append(jnp.where(row == spot, 1.0, 0.0).astype(BF16))
+            hot = jnp.concatenate(hot, axis=1) if count > 1 else hot[0]
+            terms = inner_terms[pl.ds(m * step, count * per)].reshape(count * per * own, fw)
+            inner_sum[...] += jnp.dot(hot, terms, preferred_element_type=F32).reshape(n_blk, own, fw)
+
+        if n_in % step:
+            for m in range(n_in // step):
+                add(m, 4)
+            add(n_in // step, n_in % step // per)
+        else:
+            @pl.loop(0, n_in // step)
+            def _(m):
+                add(m, 4)
+
     products(half)
     pl.semaphore_wait(barrier, n_grp - 1 + near - 1 + layers - 1)
     for c in grad_far:
@@ -541,50 +578,23 @@
             left_out[i] = with_left(i - 1, reduce(layers - d)).astype(BF16)
         ring(i, True).start()
         ring(i, False).start()
-        if chain:
-            chain.pop(0)()
-    value = reduce(0)
-    value = with_right(half - 1, value)
-    pulled[...] = with_left(half - 1, value)
-    while chain:
-        chain.pop(0)()
-    each(1, near, near_gather, wait)
+        if i == 0:
+            sum_grp()
+            inner()
+        if i == min(2, half - 1):
+            sum_near()
+    value = reduce(0) + inner_sum[...]
+    sum_far()
+    value = with_left(half - 1, with_right(half - 1, value)).astype(BF16)
+    sent[...] = value
+    for c in last:
+        c.start()
+    whole[:, mine] = value
+    spread()
     keep.wait()
     for c in far:
         c.wait()
-
-
-def pull_kernel(table, scaled, cols, outer_sum, base, out_parts, part, out, acc, sem_o, *, n_out, where):
-    keep = pltpu.make_async_copy(out_parts, out, sem_o)
-    keep.start()
-    in_rows, in_cols = where
-    acc[...] = outer_sum[...] + base[...]
-
-    @pl.loop(0, (cols.shape[0] - n_out) // 8)
-    def _(m):
-        value = [jnp.dot(cols[n_out + m * 8 + u], scaled[table[in_rows + m * 8 + u]], preferred_element_type=F32) for u in range(8)]
-        for u in range(8):
-            acc[table[in_cols + m * 8 + u]] += value[u]
-
-    part[...] = acc[...].astype(BF16)
-    keep.wait()
-
-
-def finish_kernel(n_grp, part, whole, s2, r2):
-    q, g = lax.axis_index("dom"), lax.axis_index("grp")
-    own = part.shape[1]
-    mine = pl.ds(pl.multiple_of(g * own, own), own)
-    barrier = pltpu.get_barrier_semaphore()
-    signal_group(q, g, n_grp)(barrier)
-    pl.semaphore_wait(barrier, n_grp - 1)
-    last = []
-    for r in range(1, n_grp):
-        last.append(pltpu.make_async_remote_copy(
-            src_ref=part, dst_ref=whole.at[:, mine], send_sem=s2.at[r - 1], recv_sem=r2.at[r - 1],
-            device_id=(q, (g + r) % n_grp), device_id_type=MESH))
-    for c in last:
-        c.start()
-    whole[:, mine] = part[...]
+    each(1, near, near_gather, wait)
     for c in last:
         c.wait()
 
@@ -655,38 +665,20 @@
     depth = halves * 2 * fw // parts
     half = layers // 2
     near_sem, far_sem = dma((near,)), dma((layers,))
-    outer_sum, out_parts, grads = pl.pallas_call(
-        functools.partial(backward_exchange, x, n_grp),
-        out_shape=(sds(mine, F32), sds((n_blk, blk, hid), BF16), sds((parts, depth, 128), F32)),
-        in_specs=[SM, VM, VM, ANY, VM, VM],
+    whole, layer_out, grads = pl.pallas_call(
+        functools.partial(backward_exchange, x, n_grp, n_in),
+        out_shape=(sds((n_blk, blk, fw), BF16), sds((n_blk, blk, hid), BF16), sds((parts, depth, 128), F32)),
+        in_specs=[SM, VM, VM, ANY, VM, VM, VM],
         out_specs=(VM, ANY, VM),
-        scratch_shapes=[vm((layers, near, slots, own, fw), BF16), vm((layers, near, slots, own, fw), BF16)]
+        scratch_shapes=[vm((n_in, own, fw), BF16), vm(mine, F32), vm(mine, BF16), vm((layers, near, slots, own, fw), BF16), vm((layers, near, slots, own, fw), BF16)]
         + [vm((half,) + mine, BF16)] * 4
         + [vm((n_grp - 1, halves, 2 * fw, 128), BF16), vm((parts, depth, 128), F32), vm((near, layers, depth, 128), F32),
            vm((layers, depth, 128), F32), vm((layers, depth, 128), F32)]
         + [dma((layers, near))] * 2 + [dma((half,))] * 4 + [y_sem] * 4
-        + [near_sem] * 2 + [far_sem] * 4 + [near_sem] * 2 + [dma],
+        + [near_sem] * 2 + [far_sem] * 4 + [near_sem] * 2 + [y_sem] * 2 + [dma],
         compiler_params=params(2), name="backward_exchange",
-    )(table, scaled, cols, out_all, wgrad, place_all)
-
-    _, _, in_rows, in_cols = tables(parts, slots, n_in)
-    pulled, layer_out = pl.pallas_call(
-        functools.partial(pull_kernel, n_out=n_out, where=(in_rows, in_cols)),
-        out_shape=(sds(mine, BF16), sds((n_blk, blk, hid), BF16)),
-        in_specs=[SM, VM, VM, VM, VM, ANY],
-        out_specs=(VM, ANY),
-        scratch_shapes=[vm(mine, F32), dma],
-        compiler_params=params(), name="pull",
-    )(table, scaled, cols, outer_sum, base, out_parts)
-
-    whole = pl.pallas_call(
-        functools.partial(finish_kernel, n_grp),
-        out_shape=sds((n_blk, blk, fw), BF16),
-        in_specs=[VM],
-        out_specs=VM,
-        scratch_shapes=[y_sem, y_sem],
-        compiler_params=params(3), name="finish",
-    )(pulled)
+    )(table, scaled, cols, out_all, wgrad, place_all, base)
+
     grads = grads.reshape(halves, 2 * fw, 128)
     grads = jnp.concatenate([grads[h] for h in range(halves)], axis=1)
     return layer_out.reshape(nodes, hid), whole.astype(F32).reshape(nodes, fw), grads[:fw], grads[fw:]

time: 137 us -> 135 us (0.985)
  Pallas kernels: 130 us -> 127 us
    pallas_call x3 -> x1, Pallas kernels: 51.6 us -> 48.9 us  [shards(): pl.pallas_call(functools.partial(backward_exchange, x, n_grp, n_in), out_...]
    unnamed x17 -> x16, local copies, waits for them, and re-layouts: 2.87 us -> 3.84 us
where the time goes in v5:
time: 135 us
  Pallas kernels  127 us (94%)
  local copies, waits for them, and re-layouts  5.36 us (4%)
  other arithmetic  1.79 us (1%)
    pallas_call x1, Pallas kernels, shards(): pl.pallas_call(functools.partial(backward_exchange, x, n_grp, n_in), out_...  48.9 us
    pallas_call x1, Pallas kernels, shards(): pl.pallas_call(functools.partial(forward_exchange, x, n_src, n_grp), out_...  48.9 us
    pallas_call x1, Pallas kernels, shards(): pl.pallas_call(functools.partial(dense_kernel, n_grp), out_shape=(sds((n_...  21.4 us
    pallas_call x1, Pallas kernels, shards(): pl.pallas_call(functools.partial(aggregate_kernel, x, n_src, n_grp), out_...  7.6 us
    unnamed x16, local copies, waits for them, and re-layouts  3.84 us

profile of v5, /device:TPU:1, one launch (start us, length us, event | category | flops | bytes accessed | tf_op | source)
XLA Modules:
  0.0 134.7 jit_solution(9488649941092503713)
XLA Ops:
  0.6 0.8 copy.15
  1.4 0.1 reshape.31
  1.5 1.4 %concatenate.6.table = s32[576]{0:T(1024)} concatenate(s32[192]{0:T(256)S(1)} %reshape.31, s32[192]{0:T(256)} %bitcast.25, s32[64]{0:T(128)} %bitcast.26, s32[64]{0:T(128)} %bitcast.27, s32[64]{0:T(128)} %bitcast.28), dimensions={0} | concatenate | bytes 4608 | tf_op jit(solution)/shard_map/concatenate | solution.py:623
  2.9 48.9 %forward_exchange.1 = (bf16[16,3,128,128]{3,2,1,0:T(8,128)(2,1)}, bf16[4,16,32,256]{3,2,1,0:T(8,128)(2,1)}, bf16[4,256,256]{2,1,0:T(8,128)(2,1)}, s32[8,8,128]{2...) custom-call(s32[576]{0:T(1024)} %concatenate.6.table, s32[1,192]{1,0:T(1,128)} %rows_out.1, ...), custom_call_target="tpu_custom_call" | custom-call | tf_op jit(solution)/shard_map/forward_exchange/pallas_call | solution.py:631
  51.8 0.0 copy-start
  51.8 0.0 copy-start.2
  51.8 0.0 copy-start.4
  51.8 7.6 %aggregate.1.part = bf16[16,128,128]{2,1,0:T(8,128)(2,1)} custom-call(s32[576]{0:T(1024)} %concatenate.6.table, bf16[16,128,128]{2,1,0:T(8,128)(2,1)} %bitcast.17, bf16[16,3,128,128]{3,2,1,0:T(8,128)(2,1)} %get-tuple-element.17.inc, bf16[64,128,128]{2,1,0:T(8,128)(2,1)} %bitcast.23, bf16[192,128,128]{2,1,0:T(8,128)(2,1)} %bitcast.21), custom_call_target="tpu_custom_call" | custom-call | tf_op jit(solution)/shard_map/aggregate/pallas_call | solution.py:644
  59.4 0.0 copy-done
  59.4 0.0 copy-done.2
  59.5 0.0 copy-done.4
  59.5 0.0 copy-start.1
  59.5 1.0 copy-done.1
  60.5 0.0 copy-start.3
  60.5 1.0 copy-done.3
  61.6 0.0 copy-start.5
  61.6 0.0 copy-start.6
  61.6 21.4 %dense.1 = (bf16[4,16,32,256]{3,2,1,0:T(8,128)(2,1)S(1)}, bf16[16,128,128]{2,1,0:T(8,128)(2,1)S(1)}, f32[16,32,128]{2,1,0:T(8,128)S(1)}, bf16[4,2,256,128]{3,2,1,0:T(8,128)(2,1)S(1)}) custom-call(bf16[16,128,128]{2,1,0:T(8,128)(2,1)S(1)} %copy-done.1, bf16[16,128,128]{2,1,0:T(8,128)(2,1)S(1)} %bitcast.18, f32[16,32,128]{2,1,0:T(8,128)S(1)} %copy-done.4, ...), custom_call_target="tpu_custom_call" | custom-call | tf_op jit(solution)/shard_map/dense/pallas_call | solution.py:655
  83.0 0.0 copy-done.5
  83.0 0.0 copy-done.6
  83.0 48.9 %backward_exchange.1 = (bf16[16,128,128]{2,1,0:T(8,128)(2,1)S(1)}, bf16[16,128,256]{2,1,0:T(8,128)(2,1)S(1)}, f32[64,8,128]{2,1,0:T(8,128)S(1)}) custom-call(s32[576]{0:T(1024)S(1)} %copy-done.5, bf16[16,128,128]{2,1,0:T(8,128)(2,1)S(1)} %get-tuple-element.21.scaled, bf16[256,32,128]{2,1,0:T(8,128)(2,1)} %get-tuple-element.22.cols, ...), custom_call_target="tpu_custom_call" | custom-call | tf_op jit(solution)/shard_map/backward_exchange/pallas_call | solution.py:668
  131.9 0.7 pad_maximum_fusion
  132.6 1.1 bitcast_convert_fusion
  133.7 1.0 copy.17
  (1 shorter events, 0.0 us)
Async XLA Ops:
  51.8 7.6 %copy-start = (bf16[2048,128]{1,0:T(8,128)(2,1)S(1)}, bf16[2048,128]{1,0:T(8,128)(2,1)}, u32[]{:S(2)}) copy-start(bf16[2048,128]{1,0:T(8,128)(2,1)} %param.11) | copy-start | bytes 1572868
  51.8 7.6 %copy-start.2 = (bf16[4,16,32,256]{3,2,1,0:T(8,128)(2,1)S(1)}, bf16[4,16,32,256]{3,2,1,0:T(8,128)(2,1)}, u32[]{:S(2)}) copy-start(bf16[4,16,32,256]{3,2,1,0:T(8,128)(2,1)} %get-tuple-element.19.cots) | copy-start | bytes 3145732
  51.8 7.6 %copy-start.4 = (f32[16,32,128]{2,1,0:T(8,128)S(1)}, f32[16,32,128]{2,1,0:T(8,128)}, u32[]{:S(2)}) copy-start(f32[16,32,128]{2,1,0:T(8,128)} %get-tuple-element.18.divisor) | copy-start | bytes 786436
  59.5 1.0 copy-start.1
  60.5 1.0 copy-start.3
  61.6 21.4 %copy-start.5 = (s32[576]{0:T(1024)S(1)}, s32[576]{0:T(1024)}, u32[]{:S(2)}) copy-start(s32[576]{0:T(1024)} %concatenate.6.table) | copy-start | bytes 6916
  61.6 21.4 %copy-start.6 = (s32[8,8,128]{2,1,0:T(8,128)S(1)}, s32[8,8,128]{2,1,0:T(8,128)}, u32[]{:S(2)}) copy-start(s32[8,8,128]{2,1,0:T(8,128)} %get-tuple-element.25.places) | copy-start | bytes 98308

commit v6 on v5

--- a/solution.py
+++ b/solution.py
@@ -62,10 +62,11 @@
     return go
 
 
-def tables(parts, slots, n_inner):
-    out_rows = parts * slots
-    live = 2 * parts * slots
-    return out_rows, live, live + parts, live + parts + n_inner
+def load_indices(arrays, copies, sem):
+    loads = [pltpu.make_async_copy(a, b, sem.at[n]) for n, (a, b) in enumerate(zip(arrays, copies))]
+    for c in loads:
+        c.start()
+    return loads
 
 
 def signal_ring(q, g, near, layers):
@@ -97,9 +98,9 @@
     c.wait()
 
 
-def forward_exchange(x, n_src, n_grp, table, rows_out, rows_in, live, features, cot, w_self, w_neigh, inner, outer,
-                     inc, cot_all, w_all, place_all, cols_out, divisor_out,
-                     feat, stage, blocks, row_sums, places, key_out, key_in, key_live, cols, divisor, send, recv, cot_s, cot_r, w_s, w_r, p_s, p_r, loc):
+def forward_exchange(x, n_src, n_grp, sends, rows_out, rows_in, live, features, cot, w_self, w_neigh, inner, outer,
+                     inc, cot_all, w_all, place_all, cols_out, divisor_out, own_feat,
+                     feat, stage, blocks, row_sums, places, key_out, key_in, key_live, cols, divisor, table, send, recv, cot_s, cot_r, w_s, w_r, p_s, p_r, loc):
     q, g = lax.axis_index("dom"), lax.axis_index("grp")
     slots = stage.shape[1]
     own = cot_all.shape[2]
@@ -113,6 +114,8 @@
     barrier = pltpu.get_barrier_semaphore()
     load_feat = pltpu.make_async_copy(features, feat, loc.at[3])
     load_feat.start()
+    load_sends = pltpu.make_async_copy(sends, table, loc.at[13])
+    load_sends.start()
     signal_plane(q, g, x, n_src)(barrier)
     signal_group(q, g, n_grp)(barrier)
 
@@ -126,6 +129,7 @@
         pltpu.make_async_copy(w_self, w_all.at[g, pl.ds(0, fw)], loc.at[1]),
         pltpu.make_async_copy(w_neigh, w_all.at[g, pl.ds(fw, fw)], loc.at[2]),
         pltpu.make_async_copy(places.at[z], place_all.at[z], loc.at[6]),
+        pltpu.make_async_copy(feat.at[:, mine], own_feat, loc.at[12]),
     ]
     small = [
         pltpu.make_async_copy(rows_out, key_out, loc.at[7]),
@@ -140,7 +144,7 @@
     def fill(d):
         peer = plane_peer(d, q, g, x)
         for s in range(slots):
-            stage[d, s] = feat[table[peer * slots + s]]
+            stage[d, s] = feat[table[peer, s]]
         return peer
 
     def remote(d, peer):
@@ -154,6 +158,7 @@
             src_ref=places.at[to], dst_ref=place_all.at[z], send_sem=p_s.at[r], recv_sem=p_r.at[r],
             device_id=(to * near + k, g), device_id_type=MESH)
 
+    load_sends.wait()
     load_feat.wait()
     home = fill(slot)
     others = n_grp - 1 + layers - 1
@@ -206,11 +211,13 @@
             spot = lane
             for u in range(per):
                 if c * per + u < near * slots:
-                    target = table[t * (near * slots) + c * per + u]
+                    at = c * per + u
+                    target = table[t * near + at // slots, at % slots]
                     spot = jnp.where(lane // own == u, lane + (target - u) * own, spot)
             places[t, c:c + 1, :] = spot
 
     local[3].start()
+    local[4].start()
     each(1, layers, place, start)
 
     row = lax.broadcasted_iota(jnp.int32, (own + 16, blk), 0)
@@ -268,11 +275,11 @@
         pltpu.make_async_copy(stage.at[j], inc.at[j], recv.at[j]).wait()
 
 
-def aggregate_kernel(x, n_src, n_grp, table, features, inc, inner, outer, part, feat, acc, a_in, a_out, x_in, sem_f, sem_in, sem_out, sem_x):
+def aggregate_kernel(x, n_src, n_grp, i0, i1, i2, i3, features, inc, inner, outer, part, out_rows, live, in_rows, in_cols, i_sem, feat, acc, a_in, a_out, x_in, sem_f, sem_in, sem_out, sem_x):
     q, g = lax.axis_index("dom"), lax.axis_index("grp")
     slots = inc.shape[1]
     n_in = inner.shape[0] // n_grp
-    out_rows, live, in_rows, in_cols = tables(n_grp * n_src, slots, inner.shape[0])
+    indices = load_indices((i0, i1, i2, i3), (out_rows, live, in_rows, in_cols), i_sem)
     load_f = pltpu.make_async_copy(features, feat, sem_f)
     load_f.start()
     load_in = pltpu.make_async_copy(inner.at[pl.ds(g * n_in, n_in)], a_in, sem_in)
@@ -289,14 +296,16 @@
         load(i).start()
 
     acc[...] = jnp.zeros_like(acc)
+    for c in indices:
+        c.wait()
     load_f.wait()
     load_in.wait()
 
     @pl.loop(0, n_in // 2)
     def _(m):
-        value = [jnp.dot(a_in[m * 2 + u], feat[table[in_cols + g * n_in + m * 2 + u]], preferred_element_type=F32) for u in range(2)]
+        value = [jnp.dot(a_in[m * 2 + u], feat[in_cols[0, g * n_in + m * 2 + u]], preferred_element_type=F32) for u in range(2)]
         for u in range(2):
-            acc[table[in_rows + g * n_in + m * 2 + u]] += value[u]
+            acc[in_rows[0, g * n_in + m * 2 + u]] += value[u]
 
     load_x.wait()
     pltpu.make_async_copy(a_out, a_out, sem_out).wait()
@@ -306,14 +315,14 @@
         peer = plane_peer(i, q, g, x)
         value = [jnp.dot(a_out[i, s], x_in[i, s], preferred_element_type=F32) for s in range(slots)]
         for s in range(slots):
-            @pl.when(s < table[live + peer])
+            @pl.when(s < live[0, peer])
             def _(s=s):
-                acc[table[out_rows + peer * slots + s]] += value[s]
+                acc[out_rows[0, peer * slots + s]] += value[s]
 
     part[...] = acc[...].astype(BF16)
 
 
-def dense_kernel(n_grp, part, features, divisor, cots, ws, out_all, scaled, base, wgrad, feat, cot_all, w_all, got, sent, s1, r1, s3, r3, loc):
+def dense_kernel(n_grp, part, feat, divisor, cots, ws, out_all, scaled, base, wgrad, cot_all, w_all, got, sent, s1, r1, s3, r3, loc):
     q, g = lax.axis_index("dom"), lax.axis_index("grp")
     n_blk, blk, fw = part.shape
     own = base.shape[1]
@@ -322,7 +331,6 @@
     barrier = pltpu.get_barrier_semaphore()
     signal_group(q, g, n_grp)(barrier)
     loads = [
-        pltpu.make_async_copy(features.at[:, mine], feat, loc.at[0]),
         pltpu.make_async_copy(ws, w_all, loc.at[1]),
         pltpu.make_async_copy(cots, cot_all, loc.at[2]),
     ]
@@ -374,8 +382,8 @@
         c.wait()
 
 
-def backward_exchange(x, n_grp, n_in, table, scaled, cols, out_all, wgrad, places, base_sum, whole, out, grads,
-                      inner_terms, inner_sum, sent, stage, inbox, right_out, right_in, left_out, left_in, w_got, pieces, near_got, far_sent, far_got,
+def backward_exchange(x, n_grp, n_in, i0, i1, i2, i3, scaled, cols, out_all, wgrad, places, base_sum, whole, out, grads,
+                      out_rows, live, in_rows, in_cols, i_sem, inner_terms, inner_sum, sent, stage, inbox, right_out, right_in, left_out, left_in, w_got, pieces, near_got, far_sent, far_got,
                       send, recv, rs, rr, ls, lr, o_s, o_r, w_s, w_r, a_s, a_r, b_s, b_r, c_s, c_r, d_s, d_r, e_s, e_r, loc):
     q, g = lax.axis_index("dom"), lax.axis_index("grp")
     layers, near, slots, own, fw = stage.shape
@@ -383,7 +391,7 @@
     cut = n_blk // 2
     half = layers // 2
     z, k = q // near, q % near
-    out_rows, live, in_rows, in_cols = tables(layers * near, slots, n_in)
+    indices = load_indices((i0, i1, i2, i3), (out_rows, live, in_rows, in_cols), i_sem)
     n_out = layers * near * slots
     barrier = pltpu.get_barrier_semaphore()
     signal_group(q, g, n_grp)(barrier)
@@ -422,11 +430,11 @@
             for u in range(group):
                 for s in range(slots):
                     n = (base + r * group + u) * slots + s
-                    value.append(jnp.dot(cols[n], scaled[table[out_rows + n]], preferred_element_type=F32))
+                    value.append(jnp.dot(cols[n], scaled[out_rows[0, n]], preferred_element_type=F32))
             for u in range(group):
                 to = r * group + u
                 for s in range(slots):
-                    stage[d, to, s] = jnp.where(s < table[live + base + to], value[u * slots + s], 0.0).astype(BF16)
+                    stage[d, to, s] = jnp.where(s < live[0, base + to], value[u * slots + s], 0.0).astype(BF16)
 
     def ship(d):
         own_term(d).start()
@@ -524,7 +532,7 @@
 
         @pl.loop(0, n_in // 8)
         def _(m):
-            value = [jnp.dot(cols[n_out + m * 8 + u], scaled[table[in_rows + m * 8 + u]], preferred_element_type=F32) for u in range(8)]
+            value = [jnp.dot(cols[n_out + m * 8 + u], scaled[in_rows[0, m * 8 + u]], preferred_element_type=F32) for u in range(8)]
             for u in range(8):
                 inner_terms[m * 8 + u] = value[u].astype(BF16)
 
@@ -537,7 +545,7 @@
             for c in range(count):
                 spot = lane
                 for u in range(per):
-                    target = table[in_cols + m * step + c * per + u]
+                    target = in_cols[0, m * step + c * per + u]
                     spot = jnp.where(lane // own == u, lane + (target - u) * own, spot)
                 hot.append(jnp.where(row == spot, 1.0, 0.0).astype(BF16))
             hot = jnp.concatenate(hot, axis=1) if count > 1 else hot[0]
@@ -553,13 +561,13 @@
             def _(m):
                 add(m, 4)
 
+    for c in indices:
+        c.wait()
     products(half)
     pl.semaphore_wait(barrier, n_grp - 1 + near - 1 + layers - 1)
     for c in grad_far:
         c.start()
     ship(half)
-    for c in far:
-        c.start()
     for i in range(half):
         d = half - i
         if d > 1:
@@ -579,8 +587,10 @@
         ring(i, True).start()
         ring(i, False).start()
         if i == 0:
+            inner()
             sum_grp()
-            inner()
+            for c in far:
+                c.start()
         if i == min(2, half - 1):
             sum_near()
     value = reduce(0) + inner_sum[...]
@@ -597,6 +607,23 @@
     each(1, near, near_gather, wait)
     for c in last:
         c.wait()
+
+
+def results_kernel(whole, pieces, out_parts, feature_grad, self_grad, neigh_grad, out, wide, sem):
+    keep = pltpu.make_async_copy(out_parts, out, sem.at[0])
+    keep.start()
+    wide[...] = whole[...].astype(F32)
+    keep_too = pltpu.make_async_copy(wide, feature_grad, sem.at[1])
+    keep_too.start()
+    fw = self_grad.shape[0]
+    halves = self_grad.shape[1] // 128
+    per, depth = pieces.shape[0] // (2 * halves), pieces.shape[1]
+    for h in range(halves):
+        for m, to in enumerate((self_grad, neigh_grad)):
+            at = (2 * h + m) * per
+            to[:, 128 * h:128 * (h + 1)] = pieces[at:at + per].reshape(fw, 128)
+    keep.wait()
+    keep_too.wait()
 
 
 def params(collective=None, vmem=48):
@@ -620,68 +647,75 @@
     n_in, n_out = inner_values.shape[1], outer_values.shape[1]
     n_all = n_in + n_out
     inner, outer = inner_values[0], outer_values[0]
-    table = jnp.concatenate([send_blocks.reshape(-1), outer_rows[0], live_count[0], inner_rows[0], inner_cols[0]])
     feat = features.reshape(n_blk, blk, fw)
     dma, sds = pltpu.SemaphoreType.DMA, jax.ShapeDtypeStruct
     vm = pltpu.VMEM
     block = (n_src, slots, blk, fw)
+    indices = (outer_rows, live_count, inner_rows, inner_cols)
+    index_room = [pltpu.SMEM(a.shape, jnp.int32) for a in indices] + [dma((4,))]
     mine = (n_blk, own, fw)
     y_sem = dma((n_grp - 1,))
 
-    inc, cot_all, w_all, place_all, cols, divisor = pl.pallas_call(
+    inc, cot_all, w_all, place_all, cols, divisor, own_feat = pl.pallas_call(
         functools.partial(forward_exchange, x, n_src, n_grp),
         out_shape=(sds(block, BF16), sds((n_grp, n_blk, own, hid), BF16), sds((n_grp, 2 * fw, hid), BF16), sds((layers, 8, 128), jnp.int32),
-                   sds((n_all, own, blk), BF16), sds(mine, F32)),
-        in_specs=[SM] + [HB] * 9,
-        out_specs=(ANY,) * 6,
+                   sds((n_all, own, blk), BF16), sds(mine, F32), sds(mine, BF16)),
+        in_specs=[HB] * 10,
+        out_specs=(ANY,) * 7,
         scratch_shapes=[vm((n_blk, blk, fw), BF16), vm(block, BF16), vm((n_all, blk, blk), BF16), vm((n_all, blk), F32),
-                        vm((layers, 8, 128), jnp.int32), vm((1, n_out), jnp.int32), vm((1, n_in), jnp.int32), vm((1, parts), jnp.int32), vm((n_all, own, blk), BF16), vm(mine, F32),
+                        vm((layers, 8, 128), jnp.int32), vm((1, n_out), jnp.int32), vm((1, n_in), jnp.int32), vm((1, parts), jnp.int32), vm((n_all, own, blk), BF16), vm(mine, F32), pltpu.SMEM((parts, slots), jnp.int32),
                         dma((n_src,)), dma((n_src,)), y_sem, y_sem, dma((n_grp - 1, 2)), dma((n_grp - 1, 2)),
-                        dma((layers,)), dma((layers,)), dma((12,))],
+                        dma((layers,)), dma((layers,)), dma((14,))],
         compiler_params=params(0, 62), name="forward_exchange",
-    )(table, outer_rows, inner_rows, live_count, feat, cotangent.reshape(n_blk, blk, hid), w_self, w_neigh, inner, outer)
+    )(send_blocks[0], outer_rows, inner_rows, live_count, feat, cotangent.reshape(n_blk, blk, hid), w_self, w_neigh, inner, outer)
 
     part = pl.pallas_call(
         functools.partial(aggregate_kernel, x, n_src, n_grp),
         out_shape=sds((n_blk, blk, fw), BF16),
-        in_specs=[SM, HB, ANY, HB, HB],
+        in_specs=[HB] * 5 + [ANY, HB, HB],
         out_specs=VM,
-        scratch_shapes=[vm((n_blk, blk, fw), BF16), vm((n_blk, blk, fw), F32), vm((n_in // n_grp, blk, blk), BF16),
+        scratch_shapes=index_room + [vm((n_blk, blk, fw), BF16), vm((n_blk, blk, fw), F32), vm((n_in // n_grp, blk, blk), BF16),
                         vm((n_src, slots, blk, blk), BF16), vm(block, BF16), dma, dma, dma, dma],
         compiler_params=params(None, 62), name="aggregate",
-    )(table, feat, inc, inner, outer)
+    )(*indices, feat, inc, inner, outer)
 
     halves = hid // 128
     out_all, scaled, base, wgrad = pl.pallas_call(
         functools.partial(dense_kernel, n_grp),
         out_shape=(sds((n_grp, n_blk, own, hid), BF16), sds((n_blk, blk, fw), BF16), sds(mine, F32), sds((n_grp, halves, 2 * fw, 128), BF16)),
-        in_specs=[VM, HB, VM, ANY, ANY],
+        in_specs=[VM, VM, VM, ANY, ANY],
         out_specs=(VM,) * 4,
-        scratch_shapes=[vm(mine, BF16), vm((n_grp, n_blk, own, hid), BF16), vm((n_grp, 2 * fw, hid), BF16),
+        scratch_shapes=[vm((n_grp, n_blk, own, hid), BF16), vm((n_grp, 2 * fw, hid), BF16),
                         vm((n_grp - 1,) + mine, BF16), vm(mine, BF16), y_sem, y_sem, y_sem, y_sem, dma((3,))],
         compiler_params=params(1), name="dense",
-    )(part, feat, divisor, cot_all, w_all)
+    )(part, own_feat, divisor, cot_all, w_all)
 
     depth = halves * 2 * fw // parts
     half = layers // 2
     near_sem, far_sem = dma((near,)), dma((layers,))
-    whole, layer_out, grads = pl.pallas_call(
+    whole, out_parts, grads = pl.pallas_call(
         functools.partial(backward_exchange, x, n_grp, n_in),
         out_shape=(sds((n_blk, blk, fw), BF16), sds((n_blk, blk, hid), BF16), sds((parts, depth, 128), F32)),
-        in_specs=[SM, VM, VM, ANY, VM, VM, VM],
+        in_specs=[HB] * 4 + [VM, VM, ANY, VM, VM, VM],
         out_specs=(VM, ANY, VM),
-        scratch_shapes=[vm((n_in, own, fw), BF16), vm(mine, F32), vm(mine, BF16), vm((layers, near, slots, own, fw), BF16), vm((layers, near, slots, own, fw), BF16)]
+        scratch_shapes=index_room + [vm((n_in, own, fw), BF16), vm(mine, F32), vm(mine, BF16), vm((layers, near, slots, own, fw), BF16), vm((layers, near, slots, own, fw), BF16)]
         + [vm((half,) + mine, BF16)] * 4
         + [vm((n_grp - 1, halves, 2 * fw, 128), BF16), vm((parts, depth, 128), F32), vm((near, layers, depth, 128), F32),
            vm((layers, depth, 128), F32), vm((layers, depth, 128), F32)]
         + [dma((layers, near))] * 2 + [dma((half,))] * 4 + [y_sem] * 4
         + [near_sem] * 2 + [far_sem] * 4 + [near_sem] * 2 + [y_sem] * 2 + [dma],
         compiler_params=params(2), name="backward_exchange",
-    )(table, scaled, cols, out_all, wgrad, place_all, base)
-
-    grads = grads.reshape(halves, 2 * fw, 128)
-    grads = jnp.concatenate([grads[h] for h in range(halves)], axis=1)
-    return layer_out.reshape(nodes, hid), whole.astype(F32).reshape(nodes, fw), grads[:fw], grads[fw:]
+    )(*indices, scaled, cols, out_all, wgrad, place_all, base)
+
+    feature_grad, self_grad, neigh_grad, layer_out = pl.pallas_call(
+        results_kernel,
+        out_shape=(sds((n_blk, blk, fw), F32), sds((fw, hid), F32), sds((fw, hid), F32), sds((n_blk, blk, hid), BF16)),
+        in_specs=[VM, VM, ANY],
+        out_specs=(ANY, VM, VM, ANY),
+        scratch_shapes=[vm((n_blk, blk, fw), F32), dma((2,))],
+        compiler_params=params(), name="results",
+    )(whole, grads, out_parts)
+    return layer_out.reshape(nodes, hid), feature_grad.reshape(nodes, fw), self_grad, neigh_grad
 
 
 def solution(mesh):

time: 135 us -> 130 us (0.963)
  local copies, waits for them, and re-layouts: 5.36 us -> 2.46 us
  other arithmetic: 1.79 us -> 0 us
    pallas_call x1, Pallas kernels: 48.9 us -> 46 us  [shards(): pl.pallas_call(functools.partial(backward_exchange, x, n_grp, n_in), out_...]
    pallas_call x1, Pallas kernels: 21.4 us -> 23.9 us  [shards(): pl.pallas_call(functools.partial(dense_kernel, n_grp), out_shape=(sds((n_...]
    pallas_call x0 -> x1, Pallas kernels: none -> 2.03 us  [shards(): pl.pallas_call(results_kernel, out_shape=(sds((n_blk, blk, fw), F32), sds...]
    unnamed x16 -> x21, local copies, waits for them, and re-layouts: 3.84 us -> 2.46 us
    concatenate x1 -> x0, local copies, waits for them, and re-layouts: 1.37 us -> none  [shards(): jnp.concatenate([send_blocks.reshape(-1), outer_rows[0], live_count[0], i...]
where the time goes in v6:
time: 130 us
  Pallas kernels  127 us (98%)
  local copies, waits for them, and re-layouts  2.46 us (2%)
    pallas_call x1, Pallas kernels, shards(): pl.pallas_call(functools.partial(forward_exchange, x, n_src, n_grp), out_...  47.7 us
    pallas_call x1, Pallas kernels, shards(): pl.pallas_call(functools.partial(backward_exchange, x, n_grp, n_in), out_...  46 us
    pallas_call x1, Pallas kernels, shards(): pl.pallas_call(functools.partial(dense_kernel, n_grp), out_shape=(sds((n_...  23.9 us
    pallas_call x1, Pallas kernels, shards(): pl.pallas_call(functools.partial(aggregate_kernel, x, n_src, n_grp), out_...  6.98 us

profile of v6, /device:TPU:1, one launch (start us, length us, event | category | flops | bytes accessed | tf_op | source)
XLA Modules:
  0.0 129.8 jit_solution(3408135177587731257)
XLA Ops:
  0.6 1.4 %copy.15 = s32[1,64,3]{2,1,0:T(8,128)} copy(s32[1,64,3]{1,0,2:T(1,128)} %param.18) | data formatting | bytes 1536 | tf_op args[7]
  2.0 47.7 %forward_exchange.1 = (bf16[16,3,128,128]{3,2,1,0:T(8,128)(2,1)}, bf16[4,16,32,256]{3,2,1,0:T(8,128)(2,1)}, bf16[4,256,256]{2,1,0:T(8,128)(2,1)}, s32[8,8,128]{2...) custom-call(s32[64,3]{1,0:T(8,128)} %bitcast.14, s32[1,192]{1,0:T(1,128)} %i0.3, ...), custom_call_target="tpu_custom_call" | custom-call | tf_op jit(solution)/shard_map/forward_exchange/pallas_call | solution.py:659
  49.7 0.0 copy-start.1
  49.7 0.0 copy-start.2
  49.7 0.0 copy-start.3
  49.8 0.0 copy-start.4
  49.8 7.0 %aggregate.1.part = bf16[16,128,128]{2,1,0:T(8,128)(2,1)} custom-call(s32[1,192]{1,0:T(1,128)} %i0.3, s32[1,64]{1,0:T(1,128)} %i1.3, s32[1,64]{1,0:T(1,128)} %i2.3, s32[1,64]{1,0:T(1,128)} %i3.3, bf16[16,128,128]{2,1,0:T(8,128)(2,1)} %bitcast.12, bf16[16,3,128,128]{3,2,1,0:T(8,128)(2,1)} %get-tuple-element.22.inc, bf16[64,128,128]{2,1,0:T(8,128)(2,1)} %bitcast.10, ...), custom_call_target="tpu_custom_call" | custom-call | tf_op jit(solution)/shard_map/aggregate/pallas_call | solution.py:672
  56.8 0.0 copy-done.1
  56.8 0.0 copy-done.2
  56.8 0.0 copy-done.3
  56.8 0.0 copy-done.4
  56.8 0.0 copy-start
  56.8 1.0 copy-done
  57.8 0.0 copy-start.5
  57.8 0.0 copy-start.6
  57.8 0.0 copy-start.9
  57.9 23.9 %dense.1 = (bf16[4,16,32,256]{3,2,1,0:T(8,128)(2,1)S(1)}, bf16[16,128,128]{2,1,0:T(8,128)(2,1)S(1)}, f32[16,32,128]{2,1,0:T(8,128)S(1)}, bf16[4,2,256,128]{3,2,1,0:T(8,128)(2,1)S(1)}) custom-call(bf16[16,128,128]{2,1,0:T(8,128)(2,1)S(1)} %copy-done, bf16[16,32,128]{2,1,0:T(8,128)(2,1)S(1)} %copy-done.4, f32[16,32,128]{2,1,0:T(8,128)S(1)} %copy-done.3, ...), custom_call_target="tpu_custom_call" | custom-call | tf_op jit(solution)/shard_map/dense/pallas_call | solution.py:683
  81.8 0.0 copy-done.5
  81.8 0.0 copy-done.6
  81.8 0.0 copy-done.7
  81.8 0.0 copy-done.8
  81.8 0.0 copy-done.9
  81.8 46.0 %backward_exchange.1 = (bf16[16,128,128]{2,1,0:T(8,128)(2,1)S(1)}, bf16[16,128,256]{2,1,0:T(8,128)(2,1)S(1)}, f32[64,8,128]{2,1,0:T(8,128)S(1)}) custom-call(s32[1,192]{1,0:T(1,128)S(1)} %copy-done.6, s32[1,64]{1,0:T(1,128)S(1)} %copy-done.7, s32[1,64]{1,0:T(1,128)S(1)} %copy-done.8, s32[1,64]{1,0:T(1,128)S(1)} %copy-done.9, ...), custom_call_target="tpu_custom_call" | custom-call | tf_op jit(solution)/shard_map/backward_exchange/pallas_call | solution.py:696
  127.8 2.0 %results.1 = (f32[16,128,128]{2,1,0:T(8,128)}, f32[128,256]{1,0:T(8,128)}, f32[128,256]{1,0:T(8,128)}, bf16[16,128,256]{2,1,0:T(8,128)(2,1)}) custom-call(bf16[16,128,128]{2,1,0:T(8,128)(2,1)S(1)} %get-tuple-element.33.whole, f32[64,8,128]{2,1,0:T(8,128)S(1)} %get-tuple-element.34.pieces, bf16[16,128,256]{2,1,0:T(8,128)(2,1)S(1)} %get-tuple-element.35.out_parts), custom_call_target="tpu_custom_call" | custom-call | tf_op jit(solution)/shard_map/results/pallas_call | solution.py:710
  (2 shorter events, 0.0 us)
Async XLA Ops:
  49.7 7.0 %copy-start.1 = (bf16[4,16,32,256]{3,2,1,0:T(8,128)(2,1)S(1)}, bf16[4,16,32,256]{3,2,1,0:T(8,128)(2,1)}, u32[]{:S(2)}) copy-start(bf16[4,16,32,256]{3,2,1,0:T(8,128)(2,1)} %get-tuple-element.25.cots) | copy-start | bytes 3145732
  49.7 7.0 %copy-start.2 = (bf16[4,256,256]{2,1,0:T(8,128)(2,1)S(1)}, bf16[4,256,256]{2,1,0:T(8,128)(2,1)}, u32[]{:S(2)}) copy-start(bf16[4,256,256]{2,1,0:T(8,128)(2,1)} %get-tuple-element.26.ws) | copy-start | bytes 1572868
  49.7 7.0 %copy-start.3 = (f32[16,32,128]{2,1,0:T(8,128)S(1)}, f32[16,32,128]{2,1,0:T(8,128)}, u32[]{:S(2)}) copy-start(f32[16,32,128]{2,1,0:T(8,128)} %get-tuple-element.24.divisor) | copy-start | bytes 786436
  49.8 7.0 %copy-start.4 = (bf16[16,32,128]{2,1,0:T(8,128)(2,1)S(1)}, bf16[16,32,128]{2,1,0:T(8,128)(2,1)}, u32[]{:S(2)}) copy-start(bf16[16,32,128]{2,1,0:T(8,128)(2,1)} %get-tuple-element.23.feat) | copy-start | bytes 393220
  56.8 1.0 copy-start
  57.8 23.9 %copy-start.5 = (s32[8,8,128]{2,1,0:T(8,128)S(1)}, s32[8,8,128]{2,1,0:T(8,128)}, u32[]{:S(2)}) copy-start(s32[8,8,128]{2,1,0:T(8,128)} %get-tuple-element.31.places) | copy-start | bytes 98308
  57.8 23.9 %copy-start.6 = (s32[1,192]{1,0:T(1,128)S(1)}, s32[1,192]{1,0:T(1,128)}, u32[]{:S(2)}) copy-start(s32[1,192]{1,0:T(1,128)} %i0.3) | copy-start | bytes 2308
  57.8 24.0 %copy-start.7 = (s32[1,64]{1,0:T(1,128)S(1)}, s32[1,64]{1,0:T(1,128)}, u32[]{:S(2)}) copy-start(s32[1,64]{1,0:T(1,128)} %i1.3) | copy-start | bytes 772
  57.8 24.0 %copy-start.8 = (s32[1,64]{1,0:T(1,128)S(1)}, s32[1,64]{1,0:T(1,128)}, u32[]{:S(2)}) copy-start(s32[1,64]{1,0:T(1,128)} %i2.3) | copy-start | bytes 772
  57.8 24.0 %copy-start.9 = (s32[1,64]{1,0:T(1,128)S(1)}, s32[1,64]{1,0:T(1,128)}, u32[]{:S(2)}) copy-start(s32[1,64]{1,0:T(1,128)} %i3.3) | copy-start | bytes 772

commit v7 on v6

--- a/solution.py
+++ b/solution.py
@@ -326,7 +326,7 @@
     q, g = lax.axis_index("dom"), lax.axis_index("grp")
     n_blk, blk, fw = part.shape
     own = base.shape[1]
-    rows, hid = n_blk * own, ws.shape[2]
+    hid = ws.shape[2]
     mine = pl.ds(pl.multiple_of(g * own, own), own)
     barrier = pltpu.get_barrier_semaphore()
     signal_group(q, g, n_grp)(barrier)
@@ -337,49 +337,58 @@
     for c in loads:
         c.start()
     pl.semaphore_wait(barrier, n_grp - 1)
-    copies, last = [], []
-    for r in range(1, n_grp):
-        y = (g + r) % n_grp
-        to = dict(device_id=(q, y), device_id_type=MESH)
-        theirs = pl.ds(pl.multiple_of(y * own, own), own)
-        copies.append(pltpu.make_async_remote_copy(
-            src_ref=part.at[:, theirs], dst_ref=got.at[r - 1], send_sem=s1.at[r - 1], recv_sem=r1.at[r - 1], **to))
-        last.append(pltpu.make_async_remote_copy(
-            src_ref=sent, dst_ref=scaled.at[:, mine], send_sem=s3.at[r - 1], recv_sem=r3.at[r - 1], **to))
-    for c in copies:
-        c.start()
+    cuts = 2
+    step = n_blk // cuts
+    copies, last = [[] for _ in range(cuts)], [[] for _ in range(cuts)]
+    for h in range(cuts):
+        part_h = pl.ds(h * step, step)
+        for r in range(1, n_grp):
+            y = (g + r) % n_grp
+            to = dict(device_id=(q, y), device_id_type=MESH)
+            theirs = pl.ds(pl.multiple_of(y * own, own), own)
+            copies[h].append(pltpu.make_async_remote_copy(
+                src_ref=part.at[part_h, theirs], dst_ref=got.at[r - 1, part_h], send_sem=s1.at[h, r - 1], recv_sem=r1.at[h, r - 1], **to))
+            last[h].append(pltpu.make_async_remote_copy(
+                src_ref=sent.at[part_h], dst_ref=scaled.at[part_h, mine], send_sem=s3.at[h, r - 1], recv_sem=r3.at[h, r - 1], **to))
+    for h in range(cuts):
+        for c in copies[h]:
+            c.start()
     for c in loads:
         c.wait()
-    for c in copies:
-        c.wait()
-    own_feat = feat[...]
-    total = own_feat.astype(F32) + part[:, mine].astype(F32)
-    for r in range(n_grp - 1):
-        total = total + got[r].astype(F32)
-    agg = (total / divisor[...]).astype(BF16)
-    both = jnp.concatenate([own_feat.reshape(rows, fw), agg.reshape(rows, fw)], axis=1)
-    back = jnp.zeros((rows, 2 * fw), F32)
-    grads = []
+    rows = step * own
+    both, grads = [], []
+    for h in range(cuts):
+        for c in copies[h]:
+            c.wait()
+        at = slice(h * step, (h + 1) * step)
+        own_feat = feat[at]
+        total = own_feat.astype(F32) + part[at, mine].astype(F32)
+        for r in range(n_grp - 1):
+            total = total + got[r, at].astype(F32)
+        agg = (total / divisor[at]).astype(BF16)
+        both.append(jnp.concatenate([own_feat.reshape(rows, fw), agg.reshape(rows, fw)], axis=1))
+        back = jnp.zeros((rows, 2 * fw), F32)
+        for j in range(n_grp):
+            pre = jnp.dot(both[h], w_all[j], preferred_element_type=F32)
+            sig = jax.nn.sigmoid(pre)
+            out_all[j, at] = (pre * sig).astype(BF16).reshape(step, own, hid)
+            cot = cot_all[j, at].reshape(rows, hid).astype(F32)
+            grad = (cot * sig * (1.0 + pre * (1.0 - sig))).astype(BF16)
+            grads.append(grad)
+            back = back + lax.dot_general(grad, w_all[j], TRANS_B, preferred_element_type=F32)
+        down = (back[:, fw:].reshape(step, own, fw) / divisor[at]).astype(BF16)
+        sent[at] = down
+        for c in last[h]:
+            c.start()
+        scaled[at, mine] = down
+        base[at] = back[:, :fw].reshape(step, own, fw) + down.astype(F32)
     for j in range(n_grp):
-        pre = jnp.dot(both, w_all[j], preferred_element_type=F32)
-        sig = jax.nn.sigmoid(pre)
-        out_all[j] = (pre * sig).astype(BF16).reshape(n_blk, own, hid)
-        cot = cot_all[j].reshape(rows, hid).astype(F32)
-        grad = (cot * sig * (1.0 + pre * (1.0 - sig))).astype(BF16)
-        grads.append(grad)
-        back = back + lax.dot_general(grad, w_all[j], TRANS_B, preferred_element_type=F32)
-    down = (back[:, fw:].reshape(n_blk, own, fw) / divisor[...]).astype(BF16)
-    sent[...] = down
-    for c in last:
-        c.start()
-    scaled[:, mine] = down
-    base[...] = back[:, :fw].reshape(n_blk, own, fw) + down.astype(F32)
-    for j in range(n_grp):
-        gw = lax.dot_general(both, grads[j], TRANS_A, preferred_element_type=F32).astype(BF16)
+        gw = sum(lax.dot_general(both[h], grads[h * n_grp + j], TRANS_A, preferred_element_type=F32) for h in range(cuts)).astype(BF16)
         for h in range(hid // 128):
             wgrad[j, h] = gw[:, 128 * h:128 * (h + 1)]
-    for c in last:
-        c.wait()
+    for h in range(cuts):
+        for c in last[h]:
+            c.wait()
 
 
 def backward_exchange(x, n_grp, n_in, i0, i1, i2, i3, scaled, cols, out_all, wgrad, places, base_sum, whole, out, grads,
@@ -686,7 +695,7 @@
         in_specs=[VM, VM, VM, ANY, ANY],
         out_specs=(VM,) * 4,
         scratch_shapes=[vm((n_grp, n_blk, own, hid), BF16), vm((n_grp, 2 * fw, hid), BF16),
-                        vm((n_grp - 1,) + mine, BF16), vm(mine, BF16), y_sem, y_sem, y_sem, y_sem, dma((3,))],
+                        vm((n_grp - 1,) + mine, BF16), vm(mine, BF16)] + [dma((2, n_grp - 1))] * 4 + [dma((3,))],
         compiler_params=params(1), name="dense",
     )(part, own_feat, divisor, cot_all, w_all)
 

time: 130 us -> 128 us (0.985)
  Pallas kernels: 127 us -> 124 us
    pallas_call x1, Pallas kernels: 23.9 us -> 22.1 us  [shards(): pl.pallas_call(functools.partial(dense_kernel, n_grp), out_shape=(sds((n_...]
where the time goes in v7:
time: 128 us
  Pallas kernels  124 us (97%)
  local copies, waits for them, and re-layouts  2.46 us (2%)
    pallas_call x1, Pallas kernels, shards(): pl.pallas_call(functools.partial(forward_exchange, x, n_src, n_grp), out_...  47.7 us
    pallas_call x1, Pallas kernels, shards(): pl.pallas_call(functools.partial(backward_exchange, x, n_grp, n_in), out_...  45.6 us
    pallas_call x1, Pallas kernels, shards(): pl.pallas_call(functools.partial(dense_kernel, n_grp), out_shape=(sds((n_...  22.1 us
    pallas_call x1, Pallas kernels, shards(): pl.pallas_call(functools.partial(aggregate_kernel, x, n_src, n_grp), out_...  6.97 us

profile of v7, /device:TPU:1, one launch (start us, length us, event | category | flops | bytes accessed | tf_op | source)
XLA Modules:
  0.0 127.6 jit_solution(9994550731861137046)
XLA Ops:
  0.6 1.4 %copy.15 = s32[1,64,3]{2,1,0:T(8,128)} copy(s32[1,64,3]{1,0,2:T(1,128)} %param.18) | data formatting | bytes 1536 | tf_op args[7]
  2.0 47.7 %forward_exchange.1 = (bf16[16,3,128,128]{3,2,1,0:T(8,128)(2,1)}, bf16[4,16,32,256]{3,2,1,0:T(8,128)(2,1)}, bf16[4,256,256]{2,1,0:T(8,128)(2,1)}, s32[8,8,128]{2...) custom-call(s32[64,3]{1,0:T(8,128)} %bitcast.14, s32[1,192]{1,0:T(1,128)} %i0.3, ...), custom_call_target="tpu_custom_call" | custom-call | tf_op jit(solution)/shard_map/forward_exchange/pallas_call | solution.py:668
  49.7 0.0 copy-start.1
  49.7 0.0 copy-start.2
  49.7 0.0 copy-start.3
  49.8 0.0 copy-start.4
  49.8 7.0 %aggregate.1.part = bf16[16,128,128]{2,1,0:T(8,128)(2,1)} custom-call(s32[1,192]{1,0:T(1,128)} %i0.3, s32[1,64]{1,0:T(1,128)} %i1.3, s32[1,64]{1,0:T(1,128)} %i2.3, s32[1,64]{1,0:T(1,128)} %i3.3, bf16[16,128,128]{2,1,0:T(8,128)(2,1)} %bitcast.12, bf16[16,3,128,128]{3,2,1,0:T(8,128)(2,1)} %get-tuple-element.22.inc, bf16[64,128,128]{2,1,0:T(8,128)(2,1)} %bitcast.10, ...), custom_call_target="tpu_custom_call" | custom-call | tf_op jit(solution)/shard_map/aggregate/pallas_call | solution.py:681
  56.7 0.0 copy-done.1
  56.8 0.0 copy-done.2
  56.8 0.0 copy-done.3
  56.8 0.0 copy-done.4
  56.8 0.0 copy-start
  56.8 1.0 copy-done
  57.8 0.0 copy-start.5
  57.8 0.0 copy-start.6
  57.8 0.0 copy-start.9
  57.9 22.1 %dense.1 = (bf16[4,16,32,256]{3,2,1,0:T(8,128)(2,1)S(1)}, bf16[16,128,128]{2,1,0:T(8,128)(2,1)S(1)}, f32[16,32,128]{2,1,0:T(8,128)S(1)}, bf16[4,2,256,128]{3,2,1,0:T(8,128)(2,1)S(1)}) custom-call(bf16[16,128,128]{2,1,0:T(8,128)(2,1)S(1)} %copy-done, bf16[16,32,128]{2,1,0:T(8,128)(2,1)S(1)} %copy-done.4, f32[16,32,128]{2,1,0:T(8,128)S(1)} %copy-done.3, ...), custom_call_target="tpu_custom_call" | custom-call | tf_op jit(solution)/shard_map/dense/pallas_call | solution.py:692
  79.9 0.0 copy-done.5
  79.9 0.0 copy-done.6
  80.0 0.0 copy-done.7
  80.0 0.0 copy-done.8
  80.0 0.0 copy-done.9
  80.0 45.6 %backward_exchange.1 = (bf16[16,128,128]{2,1,0:T(8,128)(2,1)S(1)}, bf16[16,128,256]{2,1,0:T(8,128)(2,1)S(1)}, f32[64,8,128]{2,1,0:T(8,128)S(1)}) custom-call(s32[1,192]{1,0:T(1,128)S(1)} %copy-done.6, s32[1,64]{1,0:T(1,128)S(1)} %copy-done.7, s32[1,64]{1,0:T(1,128)S(1)} %copy-done.8, s32[1,64]{1,0:T(1,128)S(1)} %copy-done.9, ...), custom_call_target="tpu_custom_call" | custom-call | tf_op jit(solution)/shard_map/backward_exchange/pallas_call | solution.py:705
  125.6 2.0 %results.1 = (f32[16,128,128]{2,1,0:T(8,128)}, f32[128,256]{1,0:T(8,128)}, f32[128,256]{1,0:T(8,128)}, bf16[16,128,256]{2,1,0:T(8,128)(2,1)}) custom-call(bf16[16,128,128]{2,1,0:T(8,128)(2,1)S(1)} %get-tuple-element.33.whole, f32[64,8,128]{2,1,0:T(8,128)S(1)} %get-tuple-element.34.pieces, bf16[16,128,256]{2,1,0:T(8,128)(2,1)S(1)} %get-tuple-element.35.out_parts), custom_call_target="tpu_custom_call" | custom-call | tf_op jit(solution)/shard_map/results/pallas_call | solution.py:719
  (2 shorter events, 0.0 us)
Async XLA Ops:
  49.7 7.0 %copy-start.1 = (bf16[4,16,32,256]{3,2,1,0:T(8,128)(2,1)S(1)}, bf16[4,16,32,256]{3,2,1,0:T(8,128)(2,1)}, u32[]{:S(2)}) copy-start(bf16[4,16,32,256]{3,2,1,0:T(8,128)(2,1)} %get-tuple-element.25.cots) | copy-start | bytes 3145732
  49.7 7.0 %copy-start.2 = (bf16[4,256,256]{2,1,0:T(8,128)(2,1)S(1)}, bf16[4,256,256]{2,1,0:T(8,128)(2,1)}, u32[]{:S(2)}) copy-start(bf16[4,256,256]{2,1,0:T(8,128)(2,1)} %get-tuple-element.26.ws) | copy-start | bytes 1572868
  49.7 7.0 %copy-start.3 = (f32[16,32,128]{2,1,0:T(8,128)S(1)}, f32[16,32,128]{2,1,0:T(8,128)}, u32[]{:S(2)}) copy-start(f32[16,32,128]{2,1,0:T(8,128)} %get-tuple-element.24.divisor) | copy-start | bytes 786436
  49.8 7.0 %copy-start.4 = (bf16[16,32,128]{2,1,0:T(8,128)(2,1)S(1)}, bf16[16,32,128]{2,1,0:T(8,128)(2,1)}, u32[]{:S(2)}) copy-start(bf16[16,32,128]{2,1,0:T(8,128)(2,1)} %get-tuple-element.23.feat) | copy-start | bytes 393220
  56.8 1.0 copy-start
  57.8 22.1 %copy-start.5 = (s32[8,8,128]{2,1,0:T(8,128)S(1)}, s32[8,8,128]{2,1,0:T(8,128)}, u32[]{:S(2)}) copy-start(s32[8,8,128]{2,1,0:T(8,128)} %get-tuple-element.31.places) | copy-start | bytes 98308
  57.8 22.1 %copy-start.6 = (s32[1,192]{1,0:T(1,128)S(1)}, s32[1,192]{1,0:T(1,128)}, u32[]{:S(2)}) copy-start(s32[1,192]{1,0:T(1,128)} %i0.3) | copy-start | bytes 2308
  57.8 22.1 %copy-start.7 = (s32[1,64]{1,0:T(1,128)S(1)}, s32[1,64]{1,0:T(1,128)}, u32[]{:S(2)}) copy-start(s32[1,64]{1,0:T(1,128)} %i1.3) | copy-start | bytes 772
  57.8 22.1 %copy-start.8 = (s32[1,64]{1,0:T(1,128)S(1)}, s32[1,64]{1,0:T(1,128)}, u32[]{:S(2)}) copy-start(s32[1,64]{1,0:T(1,128)} %i2.3) | copy-start | bytes 772
  57.8 22.1 %copy-start.9 = (s32[1,64]{1,0:T(1,128)S(1)}, s32[1,64]{1,0:T(1,128)}, u32[]{:S(2)}) copy-start(s32[1,64]{1,0:T(1,128)} %i3.3) | copy-start | bytes 772

commit v8 on v7

--- a/solution.py
+++ b/solution.py
@@ -337,7 +337,7 @@
     for c in loads:
         c.start()
     pl.semaphore_wait(barrier, n_grp - 1)
-    cuts = 2
+    cuts = 4
     step = n_blk // cuts
     copies, last = [[] for _ in range(cuts)], [[] for _ in range(cuts)]
     for h in range(cuts):
@@ -695,7 +695,7 @@
         in_specs=[VM, VM, VM, ANY, ANY],
         out_specs=(VM,) * 4,
         scratch_shapes=[vm((n_grp, n_blk, own, hid), BF16), vm((n_grp, 2 * fw, hid), BF16),
-                        vm((n_grp - 1,) + mine, BF16), vm(mine, BF16)] + [dma((2, n_grp - 1))] * 4 + [dma((3,))],
+                        vm((n_grp - 1,) + mine, BF16), vm(mine, BF16)] + [dma((4, n_grp - 1))] * 4 + [dma((3,))],
         compiler_params=params(1), name="dense",
     )(part, own_feat, divisor, cot_all, w_all)
 

time: 128 us -> 127 us (level)
  no operation moved by 1% of the time
where the time goes in v8:
time: 127 us
  Pallas kernels  124 us (98%)
  local copies, waits for them, and re-layouts  2.46 us (2%)
    pallas_call x1, Pallas kernels, shards(): pl.pallas_call(functools.partial(forward_exchange, x, n_src, n_grp), out_...  47.7 us
    pallas_call x1, Pallas kernels, shards(): pl.pallas_call(functools.partial(backward_exchange, x, n_grp, n_in), out_...  45.2 us
    pallas_call x1, Pallas kernels, shards(): pl.pallas_call(functools.partial(dense_kernel, n_grp), out_shape=(sds((n_...  21.8 us
    pallas_call x1, Pallas kernels, shards(): pl.pallas_call(functools.partial(aggregate_kernel, x, n_src, n_grp), out_...  6.97 us

profile of v8, /device:TPU:1, one launch (start us, length us, event | category | flops | bytes accessed | tf_op | source)
XLA Modules:
  0.0 127.0 jit_solution(8952166067082865411)
XLA Ops:
  0.6 1.4 %copy.15 = s32[1,64,3]{2,1,0:T(8,128)} copy(s32[1,64,3]{1,0,2:T(1,128)} %param.18) | data formatting | bytes 1536 | tf_op args[7]
  2.0 47.7 %forward_exchange.1 = (bf16[16,3,128,128]{3,2,1,0:T(8,128)(2,1)}, bf16[4,16,32,256]{3,2,1,0:T(8,128)(2,1)}, bf16[4,256,256]{2,1,0:T(8,128)(2,1)}, s32[8,8,128]{2...) custom-call(s32[64,3]{1,0:T(8,128)} %bitcast.14, s32[1,192]{1,0:T(1,128)} %i0.3, ...), custom_call_target="tpu_custom_call" | custom-call | tf_op jit(solution)/shard_map/forward_exchange/pallas_call | solution.py:668
  49.7 0.0 copy-start.1
  49.7 0.0 copy-start.2
  49.7 0.0 copy-start.3
  49.8 0.0 copy-start.4
  49.8 7.0 %aggregate.1.part = bf16[16,128,128]{2,1,0:T(8,128)(2,1)} custom-call(s32[1,192]{1,0:T(1,128)} %i0.3, s32[1,64]{1,0:T(1,128)} %i1.3, s32[1,64]{1,0:T(1,128)} %i2.3, s32[1,64]{1,0:T(1,128)} %i3.3, bf16[16,128,128]{2,1,0:T(8,128)(2,1)} %bitcast.12, bf16[16,3,128,128]{3,2,1,0:T(8,128)(2,1)} %get-tuple-element.22.inc, bf16[64,128,128]{2,1,0:T(8,128)(2,1)} %bitcast.10, ...), custom_call_target="tpu_custom_call" | custom-call | tf_op jit(solution)/shard_map/aggregate/pallas_call | solution.py:681
  56.7 0.0 copy-done.1
  56.8 0.0 copy-done.2
  56.8 0.0 copy-done.3
  56.8 0.0 copy-done.4
  56.8 0.0 copy-start
  56.8 1.0 copy-done
  57.8 0.0 copy-start.5
  57.8 0.0 copy-start.6
  57.8 0.0 copy-start.9
  57.9 21.8 %dense.1 = (bf16[4,16,32,256]{3,2,1,0:T(8,128)(2,1)S(1)}, bf16[16,128,128]{2,1,0:T(8,128)(2,1)S(1)}, f32[16,32,128]{2,1,0:T(8,128)S(1)}, bf16[4,2,256,128]{3,2,1,0:T(8,128)(2,1)S(1)}) custom-call(bf16[16,128,128]{2,1,0:T(8,128)(2,1)S(1)} %copy-done, bf16[16,32,128]{2,1,0:T(8,128)(2,1)S(1)} %copy-done.4, f32[16,32,128]{2,1,0:T(8,128)S(1)} %copy-done.3, ...), custom_call_target="tpu_custom_call" | custom-call | tf_op jit(solution)/shard_map/dense/pallas_call | solution.py:692
  79.7 0.0 copy-done.5
  79.7 0.0 copy-done.6
  79.7 0.0 copy-done.7
  79.7 0.0 copy-done.8
  79.8 0.0 copy-done.9
  79.8 45.2 %backward_exchange.1 = (bf16[16,128,128]{2,1,0:T(8,128)(2,1)S(1)}, bf16[16,128,256]{2,1,0:T(8,128)(2,1)S(1)}, f32[64,8,128]{2,1,0:T(8,128)S(1)}) custom-call(s32[1,192]{1,0:T(1,128)S(1)} %copy-done.6, s32[1,64]{1,0:T(1,128)S(1)} %copy-done.7, s32[1,64]{1,0:T(1,128)S(1)} %copy-done.8, s32[1,64]{1,0:T(1,128)S(1)} %copy-done.9, ...), custom_call_target="tpu_custom_call" | custom-call | tf_op jit(solution)/shard_map/backward_exchange/pallas_call | solution.py:705
  125.0 2.0 %results.1 = (f32[16,128,128]{2,1,0:T(8,128)}, f32[128,256]{1,0:T(8,128)}, f32[128,256]{1,0:T(8,128)}, bf16[16,128,256]{2,1,0:T(8,128)(2,1)}) custom-call(bf16[16,128,128]{2,1,0:T(8,128)(2,1)S(1)} %get-tuple-element.33.whole, f32[64,8,128]{2,1,0:T(8,128)S(1)} %get-tuple-element.34.pieces, bf16[16,128,256]{2,1,0:T(8,128)(2,1)S(1)} %get-tuple-element.35.out_parts), custom_call_target="tpu_custom_call" | custom-call | tf_op jit(solution)/shard_map/results/pallas_call | solution.py:719
  (2 shorter events, 0.0 us)
Async XLA Ops:
  49.7 7.0 %copy-start.1 = (bf16[4,16,32,256]{3,2,1,0:T(8,128)(2,1)S(1)}, bf16[4,16,32,256]{3,2,1,0:T(8,128)(2,1)}, u32[]{:S(2)}) copy-start(bf16[4,16,32,256]{3,2,1,0:T(8,128)(2,1)} %get-tuple-element.25.cots) | copy-start | bytes 3145732
  49.7 7.0 %copy-start.2 = (bf16[4,256,256]{2,1,0:T(8,128)(2,1)S(1)}, bf16[4,256,256]{2,1,0:T(8,128)(2,1)}, u32[]{:S(2)}) copy-start(bf16[4,256,256]{2,1,0:T(8,128)(2,1)} %get-tuple-element.26.ws) | copy-start | bytes 1572868
  49.7 7.0 %copy-start.3 = (f32[16,32,128]{2,1,0:T(8,128)S(1)}, f32[16,32,128]{2,1,0:T(8,128)}, u32[]{:S(2)}) copy-start(f32[16,32,128]{2,1,0:T(8,128)} %get-tuple-element.24.divisor) | copy-start | bytes 786436
  49.8 7.0 %copy-start.4 = (bf16[16,32,128]{2,1,0:T(8,128)(2,1)S(1)}, bf16[16,32,128]{2,1,0:T(8,128)(2,1)}, u32[]{:S(2)}) copy-start(bf16[16,32,128]{2,1,0:T(8,128)(2,1)} %get-tuple-element.23.feat) | copy-start | bytes 393220
  56.8 1.0 copy-start
  57.8 21.9 %copy-start.5 = (s32[8,8,128]{2,1,0:T(8,128)S(1)}, s32[8,8,128]{2,1,0:T(8,128)}, u32[]{:S(2)}) copy-start(s32[8,8,128]{2,1,0:T(8,128)} %get-tuple-element.31.places) | copy-start | bytes 98308
  57.8 21.9 %copy-start.6 = (s32[1,192]{1,0:T(1,128)S(1)}, s32[1,192]{1,0:T(1,128)}, u32[]{:S(2)}) copy-start(s32[1,192]{1,0:T(1,128)} %i0.3) | copy-start | bytes 2308
  57.8 21.9 %copy-start.7 = (s32[1,64]{1,0:T(1,128)S(1)}, s32[1,64]{1,0:T(1,128)}, u32[]{:S(2)}) copy-start(s32[1,64]{1,0:T(1,128)} %i1.3) | copy-start | bytes 772
  57.8 21.9 %copy-start.8 = (s32[1,64]{1,0:T(1,128)S(1)}, s32[1,64]{1,0:T(1,128)}, u32[]{:S(2)}) copy-start(s32[1,64]{1,0:T(1,128)} %i2.3) | copy-start | bytes 772
  57.8 21.9 %copy-start.9 = (s32[1,64]{1,0:T(1,128)S(1)}, s32[1,64]{1,0:T(1,128)}, u32[]{:S(2)}) copy-start(s32[1,64]{1,0:T(1,128)} %i3.3) | copy-start | bytes 772
